TPU v7x, 32 devices: a whole 2x2x4 slice. The times are simulated.
32 devices in a mesh: users: 16 (over z, x, core), ctx: 2 (over y).
Axes of the slice: x: 2, y: 2, z: 4, core: 2. Of those that a mesh axis runs over, the one named last changes fastest.
Arguments:
- events: bfloat16 [2048, 1024], P(('users', 'ctx')), may hold values from -6 to 6
- owner_id: int32 [2048, 1], P(('users', 'ctx')), may hold values from 0 to 15; in each aligned block of 64 rows (0 to 63, 64 to 127, ...) at most 6 rows name the same one
- event_bucket: int32 [2048], P(('users', 'ctx')), may hold values from 0 to 31
- cross_weight: bfloat16 [1024, 1024], P('users'), may hold values from -0.1875 to 0.1875
- cross_bias: float32 [1024], replicated, may hold values from -3 to 3
- project_weight: bfloat16 [1024, 4096], P('users'), may hold values from -0.1875 to 0.1875
- cache_keys: bfloat16 [16, 2048, 1024], P('users', 'ctx'), may hold values from -6 to 6
- cache_values: bfloat16 [16, 2048, 1024], P('users', 'ctx'), may hold values from -60 to 60
- cache_length: int32 [16], P('users'), may hold values from 256 to 2048
- cache_bucket: int32 [16, 2048], P('users', 'ctx'), may hold values from 0 to 31
- time_bias: float32 [32, 8], replicated, may hold values from -3 to 3
- norm_gain: float32 [1024], replicated, may hold values from 0.1 to 1.9
Outputs:
- gated: bfloat16 [2048, 1024], P(('users', 'ctx'))
Inputs may be any that keep to these rules, and one draw needn't show every extreme that they name: `owner_id`: no user is named by more than 6 of the 64 rows of one ingestion shard, and some user reaches that.
All inputs are finite; a program needn't handle non-finite values.
Results may differ from a plain program's by a relative error of at most 0.035.
Values may be sent and summed in bfloat16 or wider, within the bound.
No kernel may reach another device: no remote copies, remote signals or barrier semaphores. Data moves between devices by JAX's collectives and lax.ppermute only.
A program may use at most 64 MiB of HBM per device.

v0:
```python
import functools

import jax
import jax.numpy as jnp
import numpy as np
from jax import lax
from jax.experimental import pallas as pl
from jax.experimental.pallas import tpu as pltpu
from jax.sharding import PartitionSpec as P

H = 8
AXES = ("users", "ctx")
NORM_EPSILON = 1e-05
DEAD = -1e30
VMEM = pltpu.MemorySpace.VMEM
SMEM = pltpu.MemorySpace.SMEM


def round_up(value, step):
    return -(-value // step) * step


def bias_table(buckets, time_bias):
    levels = jnp.arange(time_bias.shape[0], dtype=jnp.int32)
    picked = (buckets[:, None] == levels[None, :]).astype(jnp.float32)
    return lax.dot_general(
        time_bias, picked, (((0,), (1,)), ((), ())), precision=lax.Precision.HIGHEST
    )


def pick_columns(inner, context_count, head_width, context, matrix_ref, columns_ref):
    owner_count, _, picked = columns_ref.shape
    blocks = picked // head_width
    width = matrix_ref.shape[1] // blocks
    for turn in range(inner):
        for block in range(blocks):
            start = block * width + (turn * context_count + context) * head_width
            piece = matrix_ref[:, pl.ds(pl.multiple_of(start, head_width), head_width)]
            for first in range(0, owner_count, inner):
                lanes = slice(block * head_width, (block + 1) * head_width)
                columns_ref[first + turn, :, lanes] = piece


def prepare_kernel(
    inner,
    context_count,
    context_ref,
    events_ref,
    owner_ref,
    bucket_ref,
    matrix_ref,
    packed_ref,
    columns_ref,
):
    rows, width = events_ref.shape
    head_width = packed_ref.shape[1] - width
    across = owner_ref[...].astype(jnp.float32)
    owners = jnp.broadcast_to(across, (head_width, rows)).T
    lane = lax.broadcasted_iota(jnp.int32, (rows, rows), 1)
    line = lax.broadcasted_iota(jnp.int32, (rows, rows), 0)
    earlier = (across == owners[:, :1]) & (lane < line)
    ranking = jnp.sum(jnp.where(earlier, 1.0, 0.0), axis=1, keepdims=True)
    buckets = jnp.broadcast_to(bucket_ref[...].astype(jnp.float32), (head_width, rows)).T
    lanes = lax.broadcasted_iota(jnp.int32, (rows, head_width), 1)
    meta = jnp.where(lanes == 0, owners, jnp.where(lanes == 1, ranking, buckets))
    packed_ref[:, :width] = events_ref[...]
    packed_ref[:, width:] = jnp.where(lanes < 3, meta, 0.0).astype(jnp.bfloat16)
    pick_columns(inner, context_count, head_width, context_ref[0], matrix_ref, columns_ref)


def spread_columns_kernel(inner, context_count, head_width, context_ref, matrix_ref, columns_ref):
    pick_columns(inner, context_count, head_width, context_ref[0], matrix_ref, columns_ref)


def grant(*arrays):
    held = sum(int(np.prod(a.shape)) * a.dtype.itemsize for a in arrays)
    return pltpu.CompilerParams(vmem_limit_bytes=min(60 << 20, 2 * held + (6 << 20)))


def pick_columns(inner, context_count, head_width, context, matrix_ref, columns_ref):
    owner_count, _, picked = columns_ref.shape
    blocks = picked // head_width
    width = matrix_ref.shape[1] // blocks
    for turn in range(inner):
        for block in range(blocks):
            start = block * width + (turn * context_count + context) * head_width
            piece = matrix_ref[:, pl.ds(pl.multiple_of(start, head_width), head_width)]
            for first in range(0, owner_count, inner):
                lanes = slice(block * head_width, (block + 1) * head_width)
                columns_ref[first + turn, :, lanes] = piece


def prepare_kernel(
    inner,
    context_count,
    context_ref,
    events_ref,
    owner_ref,
    bucket_ref,
    matrix_ref,
    packed_ref,
    columns_ref,
):
    rows, width = events_ref.shape
    head_width = packed_ref.shape[1] - width
    across = owner_ref[...].astype(jnp.float32)
    owners = jnp.broadcast_to(across, (head_width, rows)).T
    lane = lax.broadcasted_iota(jnp.int32, (rows, rows), 1)
    line = lax.broadcasted_iota(jnp.int32, (rows, rows), 0)
    earlier = (across == owners[:, :1]) & (lane < line)
    ranking = jnp.sum(jnp.where(earlier, 1.0, 0.0), axis=1, keepdims=True)
    buckets = jnp.broadcast_to(bucket_ref[...].astype(jnp.float32), (head_width, rows)).T
    lanes = lax.broadcasted_iota(jnp.int32, (rows, head_width), 1)
    meta = jnp.where(lanes == 0, owners, jnp.where(lanes == 1, ranking, buckets))
    packed_ref[:, :width] = events_ref[...]
    packed_ref[:, width:] = jnp.where(lanes < 3, meta, 0.0).astype(jnp.bfloat16)
    pick_columns(inner, context_count, head_width, context_ref[0], matrix_ref, columns_ref)


def spread_columns_kernel(inner, context_count, head_width, context_ref, matrix_ref, columns_ref):
    pick_columns(inner, context_count, head_width, context_ref[0], matrix_ref, columns_ref)


def grant(*arrays):
    held = sum(int(np.prod(a.shape)) * a.dtype.itemsize for a in arrays)
    return pltpu.CompilerParams(vmem_limit_bytes=min(60 << 20, 2 * held + (6 << 20)))


def fetch(copies, sems):
    started = [pltpu.make_async_copy(*pair, sems.at[i]) for i, pair in enumerate(copies)]
    for copy in started:
        copy.start()
    return started


def cross_kernel(me_ref, *refs):
    head_count = H
    pieces = refs[:head_count]
    matrix_ref, bias_ref, crossed_ref, meta_ref = refs[head_count:]
    me = me_ref[0]
    rows = pieces[0].shape[0]
    width = bias_ref.shape[1]
    head_width = width // head_count
    columns = pl.ds(pl.multiple_of(me * head_width, head_width), head_width)
    matrix = matrix_ref[...]
    bias = bias_ref[:, columns]
    for mask in range(head_count):
        piece = pieces[mask]
        target = pl.ds(pl.multiple_of((me ^ mask) * rows, rows), rows)
        crossing = jnp.dot(piece[:, :width], matrix, preferred_element_type=jnp.float32)
        source = piece[:, columns].astype(jnp.float32)
        crossed_ref[target, :] = (source * (crossing + bias) + source).astype(jnp.bfloat16)
        meta_ref[target, :] = piece[:, width:]


def project_kernel(slot_stride, kv_slots, chunk_users, me_ref, *refs):
    head_count = H
    pieces = refs[:head_count]
    matrix_ref, meta_ref, base_ref = refs[head_count : head_count + 3]
    gate_refs = refs[head_count + 3 : 2 * head_count + 3]
    send_ref, rows_ref, gate_ref = refs[2 * head_count + 3 :]
    me = me_ref[0]
    head_width = pieces[0].shape[1]
    for mask in range(head_count):
        columns = pl.ds(pl.multiple_of((me ^ mask) * head_width, head_width), head_width)
        rows_ref[:, columns] = pieces[mask][...]
    meta = meta_ref[...]
    turned = meta.astype(jnp.float32).T
    owner = turned[0:1, :].astype(jnp.int32)
    rank = turned[1:2, :].astype(jnp.int32)
    slot_of_row = owner * slot_stride + rank + base_ref[...]
    labels = jnp.broadcast_to(meta[:, 2:3].astype(jnp.float32), meta.shape).astype(jnp.bfloat16)
    half = 0.5 * jnp.dot(rows_ref[...], matrix_ref[...], preferred_element_type=jnp.float32)
    activated = (half * (1.0 + jnp.tanh(half))).astype(jnp.bfloat16)
    gate_ref[...] = activated[:, :head_width]
    shard_rows = gate_refs[0].shape[0]
    for mask in range(head_count):
        source = pl.ds(pl.multiple_of((me ^ mask) * shard_rows, shard_rows), shard_rows)
        gate_refs[mask][...] = gate_ref[source, :]
    carried = jnp.concatenate([labels, activated[:, head_width:]], axis=1)
    context_count = slot_stride // kv_slots
    user_count = send_ref.shape[0] // context_count
    chunk = chunk_users * slot_stride
    lane = lax.broadcasted_iota(jnp.int32, (8, head_width), 1)
    for first in range(0, user_count, chunk_users):
        slots = lax.broadcasted_iota(jnp.int32, (chunk, slot_of_row.shape[1]), 0)
        picked = (slots + first * slot_stride == slot_of_row).astype(jnp.float32)
        placed = jnp.dot(
            picked.astype(jnp.bfloat16), carried, preferred_element_type=jnp.float32
        )
        for user in range(chunk_users):
            low = user * slot_stride
            queries = placed[low : low + slot_stride, 2 * head_width : 3 * head_width]
            queries = queries.astype(jnp.bfloat16)
            for context in range(context_count):
                target = (first + user) * context_count + context
                start = low + context * kv_slots
                part = placed[start : start + kv_slots]
                send_ref[target, 0:slot_stride, :] = queries
                at = slot_stride
                send_ref[target, at : at + kv_slots, :] = part[:, 3 * head_width :].astype(
                    jnp.bfloat16
                )
                at += kv_slots
                send_ref[target, at : at + kv_slots, :] = part[
                    :, head_width : 2 * head_width
                ].astype(jnp.bfloat16)
                at += kv_slots
                note = part[0:8, :head_width]
                for tile in range(1, kv_slots // 8):
                    note = jnp.where(lane == tile, part[tile * 8 : tile * 8 + 8, :head_width], note)
                send_ref[target, at : at + 8, :] = note.astype(jnp.bfloat16)


def attend_kernel(
    slot_stride,
    kv_slots,
    block_groups,
    half_scale,
    arrived_ref,
    all_keys_ref,
    all_values_ref,
    cache_bias_ref,
    time_bias_ref,
    key_order_ref,
    query_order_ref,
    out_ref,
    summed_ref,
    recv_ref,
    keys_ref,
    values_ref,
    sems,
):
    copies = []
    for head in range(recv_ref.shape[1]):
        part = pl.ds(head * recv_ref.shape[3], recv_ref.shape[3])
        copies.append((arrived_ref.at[:, head], recv_ref.at[:, head]))
        copies.append((all_keys_ref.at[:, part], keys_ref.at[:, part]))
        copies.append((all_values_ref.at[:, part], values_ref.at[:, part]))
    started = fetch(copies, sems)
    group_count, head_count, _, head_width = recv_ref.shape
    context_count = slot_stride // kv_slots
    inner = head_count // context_count
    capacity = out_ref.shape[1] // head_count
    block_rows = block_groups * slot_stride
    key_count = group_count * kv_slots
    nt = (((1,), (1,)), ((), ()))
    tn = (((0,), (0,)), ((), ()))

    def one_block(block, waits):
        first = block * block_groups
        for head in range(head_count):
            if waits:
                for copy in started[3 * head : 3 * head + 3]:
                    copy.wait()
            columns = slice(head * head_width, (head + 1) * head_width)
            queries = recv_ref[pl.ds(first, block_groups), head, 0:slot_stride, :]
            queries = queries.reshape(block_rows, head_width)
            scores = lax.dot_general(
                queries, keys_ref[:, columns], nt, preferred_element_type=jnp.float32
            )
            half = scores * half_scale + cache_bias_ref[head : head + 1, :]
            weights = (half * (1.0 + jnp.tanh(half))).astype(jnp.bfloat16)
            summed = jnp.dot(weights, values_ref[:, columns], preferred_element_type=jnp.float32)
            at = slot_stride
            new_keys = recv_ref[:, head, at : at + kv_slots, :].reshape(key_count, head_width)
            at += kv_slots
            new_values = recv_ref[:, head, at : at + kv_slots, :].reshape(key_count, head_width)
            at += kv_slots
            notes = recv_ref[:, head, at : at + 8, :].astype(jnp.float32)
            buckets = jnp.concatenate(
                [notes[g, :, t : t + 1] for g in range(group_count) for t in range(kv_slots // 8)],
                axis=0,
            ).astype(jnp.int32)
            table = time_bias_ref[head : head + 1, :]
            levels = lax.broadcasted_iota(jnp.int32, (key_count, table.shape[1]), 1)
            new_bias = jnp.sum(jnp.where(levels == buckets, table, 0.0), axis=1, keepdims=True)
            new_scores = lax.dot_general(new_keys, queries, nt, preferred_element_type=jnp.float32)
            new_half = new_scores * half_scale + 0.5 * new_bias
            new_weights = jnp.where(
                key_order_ref[...] <= query_order_ref[pl.ds(block, 1), :],
                new_half * (1.0 + jnp.tanh(new_half)),
                0.0,
            ).astype(jnp.bfloat16)
            summed = summed + lax.dot_general(
                new_weights, new_values, tn, preferred_element_type=jnp.float32
            )
            summed_ref[pl.ds(head, block_rows, stride=head_count), :] = summed
        for group in range(block_groups):
            for context in range(context_count):
                for turn in range(inner):
                    slot = (group * context_count + context) * kv_slots + turn * capacity
                    rows = slice(slot * head_count, (slot + capacity) * head_count)
                    target = (first + group) * head_count + turn * context_count + context
                    out_ref[target] = summed_ref[rows, :].astype(jnp.bfloat16)

    block_count = group_count // block_groups
    if block_count == 1:
        one_block(0, True)
    else:
        for copy in started:
            copy.wait()

        def step(block, carry):
            one_block(block, False)
            return carry

        lax.fori_loop(0, block_count, step, 0)


def finish_kernel(me_ref, place_ref, *refs):
    head_count = H
    gates = refs[:head_count]
    returned_ref, gain_ref, out_ref, tall_ref, gate_ref = refs[head_count:]
    me = me_ref[0]
    rows, width = out_ref.shape
    head_width = width // head_count
    for mask in range(head_count):
        columns = pl.ds(pl.multiple_of((me ^ mask) * head_width, head_width), head_width)
        gate_ref[:, columns] = gates[mask][...]
    for row in range(rows):
        total = returned_ref[place_ref[row, 0]].astype(jnp.float32)
        for context in range(1, place_ref.shape[1]):
            total = total + returned_ref[place_ref[row, context]].astype(jnp.float32)
        tall_ref[row * head_count : (row + 1) * head_count, :] = total
    attended = jnp.concatenate(
        [tall_ref[pl.ds(head, rows, stride=head_count), :] for head in range(head_count)], axis=1
    )
    center = jnp.mean(attended, axis=1, keepdims=True)
    moved = attended - center
    spread = jnp.mean(jnp.square(moved), axis=1, keepdims=True)
    normed = moved * lax.rsqrt(spread + NORM_EPSILON)
    out_ref[...] = (normed * gain_ref[...] * gate_ref[...].astype(jnp.float32)).astype(jnp.bfloat16)


def shards(
    events,
    owner_id,
    event_bucket,
    cross_weight,
    cross_bias,
    project_weight,
    cache_keys,
    cache_values,
    cache_length,
    cache_bucket,
    time_bias,
    norm_gain,
):
    row_count, width = events.shape
    head_width = width // H
    owner_count = lax.axis_size("users")
    context_count = lax.axis_size("ctx")
    device_count = owner_count * context_count
    inner = H // context_count
    group_count = owner_count // inner
    user_index, context_index = lax.axis_index("users"), lax.axis_index("ctx")
    me = (user_index % inner) * context_count + context_index
    capacity = max(2, (3 * row_count + 2 * owner_count - 1) // (2 * owner_count))
    kv_slots = round_up(inner * capacity, 8)
    slot_stride = context_count * kv_slots
    cache_rows = cache_keys.shape[1]
    group_rows = H * row_count
    core = context_count if inner > 1 else 0
    blocks = project_weight.shape[1] // width

    def swap(block, mask):
        pairs = [(d, d // H * H + (d % H ^ mask)) for d in range(device_count)]
        return lax.ppermute(block, AXES, pairs)

    def spread(block):
        pieces = [block] + [None] * (H - 1)
        for mask in range(1, H):
            if not mask & core:
                pieces[mask] = swap(block, mask)
        for mask in range(H):
            if mask & core:
                pieces[mask] = swap(pieces[mask ^ core], core)
        return pieces

    owners = owner_id[:, 0]
    positions = jnp.arange(row_count, dtype=jnp.int32)
    earlier = (owners[None, :] == owners[:, None]) & (positions[None, :] < positions[:, None])
    ranking = jnp.sum(earlier.astype(jnp.int32), axis=1)
    vmem_spec = pl.BlockSpec(memory_space=VMEM)
    smem_spec = pl.BlockSpec(memory_space=SMEM)
    any_spec = pl.BlockSpec(memory_space=pl.ANY)
    me_scalar = me.astype(jnp.int32).reshape(1)
    context_scalar = context_index.astype(jnp.int32).reshape(1)
    packed_shape = jax.ShapeDtypeStruct((row_count, width + head_width), jnp.bfloat16)
    matrix_rows = cross_weight.shape[0]
    cross_shape = jax.ShapeDtypeStruct((owner_count, matrix_rows, head_width), jnp.bfloat16)
    packed, cross_columns = pl.pallas_call(
        functools.partial(prepare_kernel, inner, context_count),
        out_shape=(packed_shape, cross_shape),
        in_specs=[smem_spec] + [vmem_spec] * 4,
        out_specs=(vmem_spec, vmem_spec),
        name="prepare",
    )(context_scalar, events, owner_id.reshape(1, -1), event_bucket[None, :], cross_weight)
    pieces = spread(packed)
    project_shape = jax.ShapeDtypeStruct(
        (owner_count, matrix_rows, blocks * head_width), jnp.bfloat16
    )
    project_columns = pl.pallas_call(
        functools.partial(spread_columns_kernel, inner, context_count, head_width),
        out_shape=project_shape,
        in_specs=[smem_spec, vmem_spec],
        out_specs=vmem_spec,
        compiler_params=grant(project_shape),
        name="columns",
    )(context_scalar, project_weight)

    cross_columns = lax.all_to_all(cross_columns, "users", split_axis=0, concat_axis=0, tiled=True)
    project_columns = lax.all_to_all(
        project_columns, "users", split_axis=0, concat_axis=0, tiled=True
    )
    project_columns = project_columns.reshape(width, blocks * head_width)
    cross_columns = cross_columns.reshape(width, head_width)

    crossed, group_meta = pl.pallas_call(
        cross_kernel,
        out_shape=(
            jax.ShapeDtypeStruct((group_rows, head_width), jnp.bfloat16),
            jax.ShapeDtypeStruct((group_rows, head_width), jnp.bfloat16),
        ),
        in_specs=[smem_spec] + [vmem_spec] * (H + 2),
        out_specs=(vmem_spec, vmem_spec),
        compiler_params=grant(*pieces, cross_columns),
        name="cross",
    )(me_scalar, *pieces, cross_columns, cross_bias[None, :])
    crossed_pieces = spread(crossed)

    shard = np.arange(group_rows) // row_count
    base = ((shard % context_count) * kv_slots + (shard // context_count) * capacity)[None, :]
    message_rows = slot_stride + 2 * kv_slots + 8
    chunk_users = max(1, min(owner_count, 512 // slot_stride))
    while owner_count % chunk_users:
        chunk_users -= 1
    messages = jax.ShapeDtypeStruct((device_count, message_rows, head_width), jnp.bfloat16)
    *gates, outgoing = pl.pallas_call(
        functools.partial(project_kernel, slot_stride, kv_slots, chunk_users),
        out_shape=[jax.ShapeDtypeStruct((row_count, head_width), jnp.bfloat16)] * H
        + [messages],
        in_specs=[smem_spec] + [vmem_spec] * (H + 3),
        out_specs=[vmem_spec] * (H + 1),
        scratch_shapes=[
            pltpu.VMEM((group_rows, width), jnp.bfloat16),
            pltpu.VMEM((group_rows, head_width), jnp.bfloat16),
        ],
        compiler_params=grant(*crossed_pieces, project_columns, messages, messages),
        name="project",
    )(me_scalar, *crossed_pieces, project_columns, group_meta, jnp.asarray(base, jnp.int32))
    gates = [gates[0]] + [swap(gates[mask], mask) for mask in range(1, H)]

    arrived = lax.all_to_all(outgoing, AXES, split_axis=0, concat_axis=0, tiled=True)
    arrived = arrived.reshape(group_count, H, message_rows, head_width)

    live = jnp.arange(cache_rows, dtype=jnp.int32) < cache_length[0] - context_index * cache_rows
    cache_bias = jnp.where(live[None, :], 0.5 * bias_table(cache_bucket[0], time_bias), DEAD)

    def order_of(group, context, rest):
        member = rest // capacity * context_count + context
        return (group * H + member) * capacity + rest % capacity

    slots = np.arange(group_count * slot_stride)
    query_order = order_of(slots // slot_stride, slots % slot_stride // kv_slots, slots % kv_slots)
    slots = np.arange(group_count * kv_slots)
    key_order = (
        jnp.asarray(order_of(slots // kv_slots, 0, slots % kv_slots), jnp.int32)
        + context_index * capacity
    )
    block_groups = max(1, min(group_count, 256 // slot_stride))
    while group_count % block_groups:
        block_groups -= 1
    block_rows = block_groups * slot_stride
    partials = pl.pallas_call(
        functools.partial(
            attend_kernel, slot_stride, kv_slots, block_groups, 0.5 * head_width**-0.5
        ),
        out_shape=jax.ShapeDtypeStruct((device_count, capacity * H, head_width), jnp.bfloat16),
        in_specs=[any_spec] * 3 + [vmem_spec] * 4,
        out_specs=vmem_spec,
        scratch_shapes=[
            pltpu.VMEM((block_rows * H, head_width), jnp.float32),
            pltpu.VMEM(arrived.shape, arrived.dtype),
            pltpu.VMEM(cache_keys.shape[1:], cache_keys.dtype),
            pltpu.VMEM(cache_values.shape[1:], cache_values.dtype),
            pltpu.SemaphoreType.DMA((3 * H,)),
        ],
        name="attend",
    )(
        arrived,
        cache_keys[0],
        cache_values[0],
        cache_bias,
        time_bias.T,
        key_order[:, None],
        jnp.asarray(query_order, jnp.int32).reshape(-1, block_rows),
    )

    returned = lax.all_to_all(partials, AXES, split_axis=0, concat_axis=0, tiled=True)
    contexts = jnp.arange(context_count, dtype=jnp.int32)[None, :]
    places = (owners[:, None] * context_count + contexts) * capacity + ranking[:, None]
    return pl.pallas_call(
        finish_kernel,
        out_shape=jax.ShapeDtypeStruct((row_count, width), jnp.bfloat16),
        in_specs=[smem_spec] * 2 + [vmem_spec] * (H + 2),
        out_specs=vmem_spec,
        scratch_shapes=[
            pltpu.VMEM((row_count * H, head_width), jnp.float32),
            pltpu.VMEM((row_count, width), jnp.bfloat16),
        ],
        compiler_params=grant(returned, norm_gain),
        name="finish",
    )(
        me_scalar,
        places,
        *gates,
        returned.reshape(device_count * capacity, H, head_width),
        norm_gain[None, :],
    )


def solution(mesh):
    return jax.shard_map(
        shards,
        mesh=mesh,
        in_specs=(
            P(AXES, None),
            P(AXES, None),
            P(AXES),
            P("users", None),
            P(),
            P("users", None),
            P("users", "ctx", None),
            P("users", "ctx", None),
            P("users"),
            P("users", "ctx"),
            P(),
            P(),
        ),
        out_specs=P(AXES, None),
        check_vma=False,
    )
```

profile of v0, /device:TPU:0, one launch (start us, length us, event | category | flops | bytes accessed | tf_op | source)
XLA Modules:
  0.0 112.4 jit_solution(9653497377947026557)
XLA Ops:
  0.0 1.9 %prepare.1 = (bf16[64,1152]{1,0:T(8,128)(2,1)}, bf16[16,64,128]{2,1,0:T(8,128)(2,1)}) custom-call(s32[1]{0:T(128)} %bitcast.3.context_ref, bf16[64,1024]{1,0:T(8,128)(2,1)} %events_ref.1, s32[1,64]{1,0:T(1,128)} %bitcast.34, s32[1,64]{1,0:T(1,128)} %bitcast.33, bf16[64,1024]{1,0:T(8,128)(2,1)} %matrix_ref.2), custom_call_target="tpu_custom_call" | custom-call | tf_op jit(solution)/shard_map/prepare/pallas_call | solution.py:393
  1.9 7.5 %all-to-all-start = ((bf16[16,64,128]{2,1,0:T(8,128)(2,1)}), bf16[16,64,128]{2,1,0:T(8,128)(2,1)S(1)}, u32[]{:S(2)}, u32[]{:S(2)}) async-start(bf16[16,64,128]{2,1,0:T(8,128)(2,1)} %get-tuple-element.19), calls=%async_computation | async-start | bytes 524288 | tf_op jit(solution)/shard_map/all_to_all | solution.py:413
  9.5 0.0 copy-start
  9.5 1.0 copy-done
  10.5 1.1 %columns.1 = bf16[16,64,512]{2,1,0:T(8,128)(2,1)} custom-call(s32[1]{0:T(128)} %bitcast.3.context_ref, bf16[64,4096]{1,0:T(8,128)(2,1)S(1)} %copy-done), custom_call_target="tpu_custom_call" | custom-call | tf_op jit(solution)/shard_map/columns/pallas_call | solution.py:404
  11.6 7.8 %all-to-all-done = bf16[16,64,128]{2,1,0:T(8,128)(2,1)S(1)} async-done(((bf16[16,64,128]{2,1,0:T(8,128)(2,1)}), bf16[16,64,128]{2,1,0:T(8,128)(2,1)S(1)}, u32[]{:S(2)}, u32[]{:S(2)}) %all-to-all-start) | async-done | bytes 262176 | tf_op jit(solution)/shard_map/all_to_all | solution.py:413
  19.5 3.7 %all-to-all-start.1 = ((bf16[16,64,512]{2,1,0:T(8,128)(2,1)}), bf16[16,64,512]{2,1,0:T(8,128)(2,1)S(1)}, u32[]{:S(2)}, u32[]{:S(2)}) async-start(bf16[16,64,512]{2,1,0:T(8,128)(2,1)} %columns.1), calls=%async_computation.1 | async-start | bytes 2097152 | tf_op jit(solution)/shard_map/all_to_all | solution.py:414
  23.1 1.6 %collective-permute-start = (bf16[64,1152]{1,0:T(8,128)(2,1)S(1)}, bf16[64,1152]{1,0:T(8,128)(2,1)S(1)}, u32[]{:S(2)}, u32[]{:S(2)}) collective-permute-start(bf16[64,1152]{1,0:T(8,128)(2,1)S(1)} %copy-done.1), channel_id=1, source_target_pairs={{0,1},{1,0},{2,3},{3,2},{4,5},{5,4},{6,7},{7,6},{8,9},{9,8},{10,11... | collective-permute-start | bytes 442376 | tf_op jit(solution)/shard_map/ppermute | solution.py:369
  24.7 1.8 %collective-permute-start.3 = (bf16[64,1152]{1,0:T(8,128)(2,1)S(1)}, bf16[64,1152]{1,0:T(8,128)(2,1)S(1)}, u32[]{:S(2)}, u32[]{:S(2)}) collective-permute-start(bf16[64,1152]{1,0:T(8,128)(2,1)S(1)} %copy-done.1), channel_id=1, source_target_pairs={{0,4},{1,5},{2,6},{3,7},{4,0},{5,1},{6,2},{7,3},{8,12},{9,13},{10,... | collective-permute-start | bytes 442376 | tf_op jit(solution)/shard_map/ppermute | solution.py:369
  26.5 0.2 collective-permute-start.4
  26.7 0.0 collective-permute-start.1
  26.7 2.5 %collective-permute-done.refs_1_ = bf16[64,1152]{1,0:T(8,128)(2,1)S(1)} collective-permute-done((bf16[64,1152]{1,0:T(8,128)(2,1)S(1)}, bf16[64,1152]{1,0:T(8,128)(2,1)S(1)}, u32[]{:S(2)}, u32[]{:S(2)}) %collective-permute-start) | collective-permute-done | bytes 147488 | tf_op jit(solution)/shard_map/ppermute | solution.py:369
  29.2 9.0 %collective-permute-done.3.refs_4_ = bf16[64,1152]{1,0:T(8,128)(2,1)S(1)} collective-permute-done((bf16[64,1152]{1,0:T(8,128)(2,1)S(1)}, bf16[64,1152]{1,0:T(8,128)(2,1)S(1)}, u32[]{:S(2)}, u32[]{:S(2)}) %collective-permute-start.3) | collective-permute-done | bytes 147488 | tf_op jit(solution)/shard_map/ppermute | solution.py:369
  38.3 3.5 %collective-permute-done.4.refs_5_ = bf16[64,1152]{1,0:T(8,128)(2,1)S(1)} collective-permute-done((bf16[64,1152]{1,0:T(8,128)(2,1)S(1)}, bf16[64,1152]{1,0:T(8,128)(2,1)S(1)}, u32[]{:S(2)}, u32[]{:S(2)}) %collective-permute-start.4) | collective-permute-done | bytes 147488 | tf_op jit(solution)/shard_map/ppermute | solution.py:369
  41.8 1.3 %collective-permute-done.6.refs_7_ = bf16[64,1152]{1,0:T(8,128)(2,1)S(1)} collective-permute-done((bf16[64,1152]{1,0:T(8,128)(2,1)S(1)}, bf16[64,1152]{1,0:T(8,128)(2,1)S(1)}, u32[]{:S(2)}, u32[]{:S(2)}) %collective-permute-start.6) | collective-permute-done | bytes 147488 | tf_op jit(solution)/shard_map/ppermute | solution.py:369
  43.2 0.4 cross.1
  43.6 0.0 copy-start.9
  43.7 0.0 copy-start.6
  43.7 0.0 copy-start.8
  43.7 1.8 %collective-permute-start.10 = (bf16[512,128]{1,0:T(8,128)(2,1)S(1)}, bf16[512,128]{1,0:T(8,128)(2,1)S(1)}, u32[]{:S(2)}, u32[]{:S(2)}) collective-permute-start(bf16[512,128]{1,0:T(8,128)(2,1)S(1)} %get-tuple-element.20.refs_0_), channel_id=1, source_target_pairs={{0,4},{1,5},{2,6},{3,7},{4,0},{5,1},{6,2},{7,3},{8,12},{9,13},{10,... | collective-permute-start | bytes 393224 | tf_op jit(solution)/shard_map/ppermute | solution.py:369
  45.5 0.2 collective-permute-start.11
  45.7 1.5 %collective-permute-start.7 = (bf16[512,128]{1,0:T(8,128)(2,1)S(1)}, bf16[512,128]{1,0:T(8,128)(2,1)S(1)}, u32[]{:S(2)}, u32[]{:S(2)}) collective-permute-start(bf16[512,128]{1,0:T(8,128)(2,1)S(1)} %get-tuple-element.20.refs_0_), channel_id=1, source_target_pairs={{0,1},{1,0},{2,3},{3,2},{4,5},{5,4},{6,7},{7,6},{8,9},{9,8},{10,11... | collective-permute-start | bytes 393224 | tf_op jit(solution)/shard_map/ppermute | solution.py:369
  47.2 2.9 %collective-permute-done.10.refs_4_ = bf16[512,128]{1,0:T(8,128)(2,1)S(1)} collective-permute-done((bf16[512,128]{1,0:T(8,128)(2,1)S(1)}, bf16[512,128]{1,0:T(8,128)(2,1)S(1)}, u32[]{:S(2)}, u32[]{:S(2)}) %collective-permute-start.10) | collective-permute-done | bytes 131104 | tf_op jit(solution)/shard_map/ppermute | solution.py:369
  50.1 3.0 %collective-permute-done.11.refs_5_ = bf16[512,128]{1,0:T(8,128)(2,1)S(1)} collective-permute-done((bf16[512,128]{1,0:T(8,128)(2,1)S(1)}, bf16[512,128]{1,0:T(8,128)(2,1)S(1)}, u32[]{:S(2)}, u32[]{:S(2)}) %collective-permute-start.11) | collective-permute-done | bytes 131104 | tf_op jit(solution)/shard_map/ppermute | solution.py:369
  53.1 0.5 collective-permute-done.7.refs_1_
  53.6 0.8 collective-permute-done.13.refs_7_
  54.4 0.5 collective-permute-done.9.refs_3_
  55.0 2.5 %project.1 = (bf16[64,128]{1,0:T(8,128)(2,1)S(1)}, bf16[64,128]{1,0:T(8,128)(2,1)S(1)}, bf16[64,128]{1,0:T(8,128)(2,1)S(1)}, bf16[64,128]{1,0:T(8,128)(2,1)S(1)}...) custom-call(s32[1]{0:T(128)} %bitcast.me_ref, ...), custom_call_target="tpu_custom_call" | custom-call | tf_op jit(solution)/shard_map/project/pallas_call | solution.py:440
  57.5 5.9 %all-to-all-start.2 = ((bf16[32,104,128]{2,1,0:T(8,128)(2,1)}), bf16[32,104,128]{2,1,0:T(8,128)(2,1)S(1)}, u32[]{:S(2)}, u32[]{:S(2)}) async-start(bf16[32,104,128]{2,1,0:T(8,128)(2,1)} %get-tuple-element.30), calls=%async_computation.2 | async-start | bytes 1703936 | tf_op jit(solution)/shard_map/all_to_all | solution.py:455
  63.5 0.7 copy.19.key_order_ref
  64.9 1.1 fusion.1.cache_bias_ref
  65.9 19.5 %all-to-all-done.2 = bf16[32,104,128]{2,1,0:T(8,128)(2,1)S(1)} async-done(((bf16[32,104,128]{2,1,0:T(8,128)(2,1)}), bf16[32,104,128]{2,1,0:T(8,128)(2,1)S(1)}, u32[]{:S(2)}, u32[]{:S(2)}) %all-to-all-start.2) | async-done | bytes 852000 | tf_op jit(solution)/shard_map/all_to_all | solution.py:455
  85.4 0.9 copy-done.5
  86.3 7.6 %attend.1 = bf16[32,48,128]{2,1,0:T(8,128)(2,1)} custom-call(bf16[4,8,104,128]{3,2,1,0:T(8,128)(2,1)} %bitcast.29, bf16[1024,1024]{1,0:T(8,128)(2,1)} %bitcast.30, bf16[1024,1024]{1,0:T(8,128)(2,1)} %bitcast.31, f32[8,1024]{1,0:T(8,128)} %fusion.1.cache_bias_ref, f32[8,32]{1,0:T(8,128)} %bitcast.32, s32[96,1]{1,0:T(8,128)} %copy.19.key_order_ref, ...), custom_call_target="tpu_custom_call" | custom-call | tf_op jit(solution)/shard_map/attend/pallas_call | solution.py:476
  94.0 3.6 %all-to-all-start.3 = ((bf16[32,48,128]{2,1,0:T(8,128)(2,1)}), bf16[32,48,128]{2,1,0:T(8,128)(2,1)S(1)}, u32[]{:S(2)}, u32[]{:S(2)}) async-start(bf16[32,48,128]{2,1,0:T(8,128)(2,1)} %attend.1), calls=%async_computation.3 | async-start | bytes 786432 | tf_op jit(solution)/shard_map/all_to_all | solution.py:501
  97.6 1.8 %collective-permute-start.14 = (bf16[64,128]{1,0:T(8,128)(2,1)S(1)}, bf16[64,128]{1,0:T(8,128)(2,1)S(1)}, u32[]{:S(2)}, u32[]{:S(2)}) collective-permute-start(bf16[64,128]{1,0:T(8,128)(2,1)S(1)} %get-tuple-element.23), channel_id=1, source_target_pairs={{0,1},{1,0},{2,3},{3,2},{4,5},{5,4},{6,7},{7,6},{8,9},{9,8},{10,11... | collective-permute-start | bytes 49160 | tf_op jit(solution)/shard_map/ppermute | solution.py:369
  99.5 0.2 convert_reduce_fusion
  99.6 0.4 collective-permute-start.16
  100.1 1.8 %collective-permute-start.17 = (bf16[64,128]{1,0:T(8,128)(2,1)S(1)}, bf16[64,128]{1,0:T(8,128)(2,1)S(1)}, u32[]{:S(2)}, u32[]{:S(2)}) collective-permute-start(bf16[64,128]{1,0:T(8,128)(2,1)S(1)} %get-tuple-element.26), channel_id=1, source_target_pairs={{0,4},{1,5},{2,6},{3,7},{4,0},{5,1},{6,2},{7,3},{8,12},{9,13},{10,... | collective-permute-start | bytes 49160 | tf_op jit(solution)/shard_map/ppermute | solution.py:369
  101.8 1.5 %collective-permute-start.18 = (bf16[64,128]{1,0:T(8,128)(2,1)S(1)}, bf16[64,128]{1,0:T(8,128)(2,1)S(1)}, u32[]{:S(2)}, u32[]{:S(2)}) collective-permute-start(bf16[64,128]{1,0:T(8,128)(2,1)S(1)} %get-tuple-element.27), channel_id=1, source_target_pairs={{0,5},{1,4},{2,7},{3,6},{4,1},{5,0},{6,3},{7,2},{8,13},{9,12},{10,... | collective-permute-start | bytes 49160 | tf_op jit(solution)/shard_map/ppermute | solution.py:369
  103.3 0.5 collective-permute-start.19
  103.8 1.5 %collective-permute-start.20 = (bf16[64,128]{1,0:T(8,128)(2,1)S(1)}, bf16[64,128]{1,0:T(8,128)(2,1)S(1)}, u32[]{:S(2)}, u32[]{:S(2)}) collective-permute-start(bf16[64,128]{1,0:T(8,128)(2,1)S(1)} %get-tuple-element.29), channel_id=1, source_target_pairs={{0,7},{1,6},{2,5},{3,4},{4,3},{5,2},{6,1},{7,0},{8,15},{9,14},{10,... | collective-permute-start | bytes 49160 | tf_op jit(solution)/shard_map/ppermute | solution.py:369
  105.3 0.1 multiply_add_fusion.place_ref
  105.4 1.1 %collective-permute-done.18.refs_5_ = bf16[64,128]{1,0:T(8,128)(2,1)S(1)} collective-permute-done((bf16[64,128]{1,0:T(8,128)(2,1)S(1)}, bf16[64,128]{1,0:T(8,128)(2,1)S(1)}, u32[]{:S(2)}, u32[]{:S(2)}) %collective-permute-start.18) | collective-permute-done | bytes 16416 | tf_op jit(solution)/shard_map/ppermute | solution.py:369
  106.5 0.1 collective-permute-done.19.refs_6_
  106.7 1.3 %collective-permute-done.20.refs_7_ = bf16[64,128]{1,0:T(8,128)(2,1)S(1)} collective-permute-done((bf16[64,128]{1,0:T(8,128)(2,1)S(1)}, bf16[64,128]{1,0:T(8,128)(2,1)S(1)}, u32[]{:S(2)}, u32[]{:S(2)}) %collective-permute-start.20) | collective-permute-done | bytes 16416 | tf_op jit(solution)/shard_map/ppermute | solution.py:369
  107.9 2.4 %all-to-all-done.3 = bf16[32,48,128]{2,1,0:T(8,128)(2,1)S(1)} async-done(((bf16[32,48,128]{2,1,0:T(8,128)(2,1)}), bf16[32,48,128]{2,1,0:T(8,128)(2,1)S(1)}, u32[]{:S(2)}, u32[]{:S(2)}) %all-to-all-start.3) | async-done | bytes 393248 | tf_op jit(solution)/shard_map/all_to_all | solution.py:501
  110.3 2.1 %finish.1 = bf16[64,1024]{1,0:T(8,128)(2,1)} custom-call(s32[1]{0:T(128)} %bitcast.me_ref, s32[64,2]{1,0:T(8,128)S(1)} %multiply_add_fusion.place_ref, bf16[64,128]{1,0:T(8,128)(2,1)S(1)} %get-tuple-element.22.refs_0_, bf16[64,128]{1,0:T(8,128)(2,1)S(1)} %collective-permute-done.14.refs_1_, bf16[64,128]{1,0:T(8,128)(2,1)S(1)} %collective-permute-done.15.refs_2_, ...), custom_call_target="tpu_custom_call" | custom-call | tf_op jit(solution)/shard_map/finish/pallas_call | solution.py:504
  (35 shorter events, 0.1 us)
Async XLA Ops:
  1.9 21.2 %copy-start.1 = (bf16[64,1152]{1,0:T(8,128)(2,1)S(1)}, bf16[64,1152]{1,0:T(8,128)(2,1)}, u32[]{:S(2)}) copy-start(bf16[64,1152]{1,0:T(8,128)(2,1)} %get-tuple-element.18.refs_0_) | copy-start | bytes 442372
  1.9 41.3 %copy-start.2 = (f32[1024]{0:T(1024)S(1)}, f32[1024]{0:T(1024)}, u32[]{:S(2)}) copy-start(f32[1024]{0:T(1024)} %param.19) | copy-start | bytes 12292
  1.9 17.5 %all-to-all-start = ((bf16[16,64,128]{2,1,0:T(8,128)(2,1)}), bf16[16,64,128]{2,1,0:T(8,128)(2,1)S(1)}, u32[]{:S(2)}, u32[]{:S(2)}) async-start(bf16[16,64,128]{2,1,0:T(8,128)(2,1)} %get-tuple-element.19), calls=%async_computation | async-start | bytes 524288 | tf_op jit(solution)/shard_map/all_to_all | solution.py:413
  9.5 1.0 copy-start
  11.6 43.4 %copy-start.4 = (s32[1,512]{1,0:T(1,128)S(1)}, s32[1,512]{1,0:T(1,128)}, u32[]{:S(2)}) copy-start(s32[1,512]{1,0:T(1,128)} %constant.40.clone.refs_10_) | copy-start | bytes 6148
  19.5 35.5 %all-to-all-start.1 = ((bf16[16,64,512]{2,1,0:T(8,128)(2,1)}), bf16[16,64,512]{2,1,0:T(8,128)(2,1)S(1)}, u32[]{:S(2)}, u32[]{:S(2)}) async-start(bf16[16,64,512]{2,1,0:T(8,128)(2,1)} %columns.1), calls=%async_computation.1 | async-start | bytes 2097152 | tf_op jit(solution)/shard_map/all_to_all | solution.py:414
  23.1 6.1 %collective-permute-start = (bf16[64,1152]{1,0:T(8,128)(2,1)S(1)}, bf16[64,1152]{1,0:T(8,128)(2,1)S(1)}, u32[]{:S(2)}, u32[]{:S(2)}) collective-permute-start(bf16[64,1152]{1,0:T(8,128)(2,1)S(1)} %copy-done.1), channel_id=1, source_target_pairs={{0,1},{1,0},{2,3},{3,2},{4,5},{5,4},{6,7},{7,6},{8,9},{9,8},{10,11... | collective-permute-start | bytes 442376 | tf_op jit(solution)/shard_map/ppermute | solution.py:369
  24.7 13.5 %collective-permute-start.3 = (bf16[64,1152]{1,0:T(8,128)(2,1)S(1)}, bf16[64,1152]{1,0:T(8,128)(2,1)S(1)}, u32[]{:S(2)}, u32[]{:S(2)}) collective-permute-start(bf16[64,1152]{1,0:T(8,128)(2,1)S(1)} %copy-done.1), channel_id=1, source_target_pairs={{0,4},{1,5},{2,6},{3,7},{4,0},{5,1},{6,2},{7,3},{8,12},{9,13},{10,... | collective-permute-start | bytes 442376 | tf_op jit(solution)/shard_map/ppermute | solution.py:369
  26.5 15.3 %collective-permute-start.4 = (bf16[64,1152]{1,0:T(8,128)(2,1)S(1)}, bf16[64,1152]{1,0:T(8,128)(2,1)S(1)}, u32[]{:S(2)}, u32[]{:S(2)}) collective-permute-start(bf16[64,1152]{1,0:T(8,128)(2,1)S(1)} %copy-done.1), channel_id=1, source_target_pairs={{0,5},{1,4},{2,7},{3,6},{4,1},{5,0},{6,3},{7,2},{8,13},{9,12},{10,... | collective-permute-start | bytes 442376 | tf_op jit(solution)/shard_map/ppermute | solution.py:369
  26.7 15.1 %collective-permute-start.1 = (bf16[64,1152]{1,0:T(8,128)(2,1)S(1)}, bf16[64,1152]{1,0:T(8,128)(2,1)S(1)}, u32[]{:S(2)}, u32[]{:S(2)}) collective-permute-start(bf16[64,1152]{1,0:T(8,128)(2,1)S(1)} %copy-done.1), channel_id=1, source_target_pairs={{0,2},{1,3},{2,0},{3,1},{4,6},{5,7},{6,4},{7,5},{8,10},{9,11},{10,... | collective-permute-start | bytes 442376 | tf_op jit(solution)/shard_map/ppermute | solution.py:369
  29.2 12.6 %collective-permute-start.2 = (bf16[64,1152]{1,0:T(8,128)(2,1)S(1)}, bf16[64,1152]{1,0:T(8,128)(2,1)S(1)}, u32[]{:S(2)}, u32[]{:S(2)}) collective-permute-start(bf16[64,1152]{1,0:T(8,128)(2,1)S(1)} %collective-permute-done.refs_1_), channel_id=1, source_target_pairs={{0,2},{1,3},{2,0},{3,1},{4,6},{5,7},{6,4},{7,5},{8,10},{9,11},{10,... | collective-permute-start | bytes 442376 | tf_op jit(solution)/shard_map/ppermute | solution.py:369
  38.3 3.6 %collective-permute-start.5 = (bf16[64,1152]{1,0:T(8,128)(2,1)S(1)}, bf16[64,1152]{1,0:T(8,128)(2,1)S(1)}, u32[]{:S(2)}, u32[]{:S(2)}) collective-permute-start(bf16[64,1152]{1,0:T(8,128)(2,1)S(1)} %collective-permute-done.3.refs_4_), channel_id=1, source_target_pairs={{0,2},{1,3},{2,0},{3,1},{4,6},{5,7},{6,4},{7,5},{8,10},{9,11},{10,... | collective-permute-start | bytes 442376 | tf_op jit(solution)/shard_map/ppermute | solution.py:369
  41.8 1.4 %collective-permute-start.6 = (bf16[64,1152]{1,0:T(8,128)(2,1)S(1)}, bf16[64,1152]{1,0:T(8,128)(2,1)S(1)}, u32[]{:S(2)}, u32[]{:S(2)}) collective-permute-start(bf16[64,1152]{1,0:T(8,128)(2,1)S(1)} %collective-permute-done.4.refs_5_), channel_id=1, source_target_pairs={{0,2},{1,3},{2,0},{3,1},{4,6},{5,7},{6,4},{7,5},{8,10},{9,11},{10,... | collective-permute-start | bytes 442376 | tf_op jit(solution)/shard_map/ppermute | solution.py:369
  43.6 19.8 %copy-start.9 = (s32[96]{0:T(128)S(1)}, s32[96]{0:T(128)}, u32[]{:S(2)}) copy-start(s32[96]{0:T(128)} %constant.41.clone) | copy-start | bytes 1156
  43.7 21.2 %copy-start.6 = (f32[32,8]{0,1:T(8,128)S(1)}, f32[32,8]{0,1:T(8,128)}, u32[]{:S(2)}) copy-start(f32[32,8]{0,1:T(8,128)} %param.25) | copy-start | bytes 3076
  43.7 21.2 %copy-start.8 = (s32[1,1024]{1,0:T(1,128)S(1)}, s32[1,1024]{1,0:T(1,128)}, u32[]{:S(2)}) copy-start(s32[1,1024]{1,0:T(1,128)} %param.24) | copy-start | bytes 12292
  43.7 6.4 %collective-permute-start.10 = (bf16[512,128]{1,0:T(8,128)(2,1)S(1)}, bf16[512,128]{1,0:T(8,128)(2,1)S(1)}, u32[]{:S(2)}, u32[]{:S(2)}) collective-permute-start(bf16[512,128]{1,0:T(8,128)(2,1)S(1)} %get-tuple-element.20.refs_0_), channel_id=1, source_target_pairs={{0,4},{1,5},{2,6},{3,7},{4,0},{5,1},{6,2},{7,3},{8,12},{9,13},{10,... | collective-permute-start | bytes 393224 | tf_op jit(solution)/shard_map/ppermute | solution.py:369
  45.5 7.6 %collective-permute-start.11 = (bf16[512,128]{1,0:T(8,128)(2,1)S(1)}, bf16[512,128]{1,0:T(8,128)(2,1)S(1)}, u32[]{:S(2)}, u32[]{:S(2)}) collective-permute-start(bf16[512,128]{1,0:T(8,128)(2,1)S(1)} %get-tuple-element.20.refs_0_), channel_id=1, source_target_pairs={{0,5},{1,4},{2,7},{3,6},{4,1},{5,0},{6,3},{7,2},{8,13},{9,12},{10,... | collective-permute-start | bytes 393224 | tf_op jit(solution)/shard_map/ppermute | solution.py:369
  45.7 7.9 %collective-permute-start.7 = (bf16[512,128]{1,0:T(8,128)(2,1)S(1)}, bf16[512,128]{1,0:T(8,128)(2,1)S(1)}, u32[]{:S(2)}, u32[]{:S(2)}) collective-permute-start(bf16[512,128]{1,0:T(8,128)(2,1)S(1)} %get-tuple-element.20.refs_0_), channel_id=1, source_target_pairs={{0,1},{1,0},{2,3},{3,2},{4,5},{5,4},{6,7},{7,6},{8,9},{9,8},{10,11... | collective-permute-start | bytes 393224 | tf_op jit(solution)/shard_map/ppermute | solution.py:369
  47.2 6.4 %collective-permute-start.8 = (bf16[512,128]{1,0:T(8,128)(2,1)S(1)}, bf16[512,128]{1,0:T(8,128)(2,1)S(1)}, u32[]{:S(2)}, u32[]{:S(2)}) collective-permute-start(bf16[512,128]{1,0:T(8,128)(2,1)S(1)} %get-tuple-element.20.refs_0_), channel_id=1, source_target_pairs={{0,2},{1,3},{2,0},{3,1},{4,6},{5,7},{6,4},{7,5},{8,10},{9,11},{10,... | collective-permute-start | bytes 393224 | tf_op jit(solution)/shard_map/ppermute | solution.py:369
  50.1 3.5 %collective-permute-start.12 = (bf16[512,128]{1,0:T(8,128)(2,1)S(1)}, bf16[512,128]{1,0:T(8,128)(2,1)S(1)}, u32[]{:S(2)}, u32[]{:S(2)}) collective-permute-start(bf16[512,128]{1,0:T(8,128)(2,1)S(1)} %collective-permute-done.10.refs_4_), channel_id=1, source_target_pairs={{0,2},{1,3},{2,0},{3,1},{4,6},{5,7},{6,4},{7,5},{8,10},{9,11},{10,... | collective-permute-start | bytes 393224 | tf_op jit(solution)/shard_map/ppermute | solution.py:369
  53.1 1.3 %collective-permute-start.13 = (bf16[512,128]{1,0:T(8,128)(2,1)S(1)}, bf16[512,128]{1,0:T(8,128)(2,1)S(1)}, u32[]{:S(2)}, u32[]{:S(2)}) collective-permute-start(bf16[512,128]{1,0:T(8,128)(2,1)S(1)} %collective-permute-done.11.refs_5_), channel_id=1, source_target_pairs={{0,2},{1,3},{2,0},{3,1},{4,6},{5,7},{6,4},{7,5},{8,10},{9,11},{10,... | collective-permute-start | bytes 393224 | tf_op jit(solution)/shard_map/ppermute | solution.py:369
  53.6 1.3 %collective-permute-start.9 = (bf16[512,128]{1,0:T(8,128)(2,1)S(1)}, bf16[512,128]{1,0:T(8,128)(2,1)S(1)}, u32[]{:S(2)}, u32[]{:S(2)}) collective-permute-start(bf16[512,128]{1,0:T(8,128)(2,1)S(1)} %collective-permute-done.7.refs_1_), channel_id=1, source_target_pairs={{0,2},{1,3},{2,0},{3,1},{4,6},{5,7},{6,4},{7,5},{8,10},{9,11},{10,... | collective-permute-start | bytes 393224 | tf_op jit(solution)/shard_map/ppermute | solution.py:369
  57.5 27.9 %all-to-all-start.2 = ((bf16[32,104,128]{2,1,0:T(8,128)(2,1)}), bf16[32,104,128]{2,1,0:T(8,128)(2,1)S(1)}, u32[]{:S(2)}, u32[]{:S(2)}) async-start(bf16[32,104,128]{2,1,0:T(8,128)(2,1)} %get-tuple-element.30), calls=%async_computation.2 | async-start | bytes 1703936 | tf_op jit(solution)/shard_map/all_to_all | solution.py:455
  85.4 0.9 copy-start.5
  86.3 11.3 %copy-start.7 = (s32[64,1]{0,1:T(1,128)S(1)}, s32[64,1]{0,1:T(1,128)}, u32[]{:S(2)}) copy-start(s32[64,1]{0,1:T(1,128)} %param.16) | copy-start | bytes 772
  86.3 24.0 %copy-start.3 = (f32[1024]{0:T(1024)S(1)}, f32[1024]{0:T(1024)}, u32[]{:S(2)}) copy-start(f32[1024]{0:T(1024)} %param.26) | copy-start | bytes 12292
  94.0 16.4 %all-to-all-start.3 = ((bf16[32,48,128]{2,1,0:T(8,128)(2,1)}), bf16[32,48,128]{2,1,0:T(8,128)(2,1)S(1)}, u32[]{:S(2)}, u32[]{:S(2)}) async-start(bf16[32,48,128]{2,1,0:T(8,128)(2,1)} %attend.1), calls=%async_computation.3 | async-start | bytes 786432 | tf_op jit(solution)/shard_map/all_to_all | solution.py:501
  97.6 5.7 %collective-permute-start.14 = (bf16[64,128]{1,0:T(8,128)(2,1)S(1)}, bf16[64,128]{1,0:T(8,128)(2,1)S(1)}, u32[]{:S(2)}, u32[]{:S(2)}) collective-permute-start(bf16[64,128]{1,0:T(8,128)(2,1)S(1)} %get-tuple-element.23), channel_id=1, source_target_pairs={{0,1},{1,0},{2,3},{3,2},{4,5},{5,4},{6,7},{7,6},{8,9},{9,8},{10,11... | collective-permute-start | bytes 49160 | tf_op jit(solution)/shard_map/ppermute | solution.py:369
  99.5 4.4 %collective-permute-start.15 = (bf16[64,128]{1,0:T(8,128)(2,1)S(1)}, bf16[64,128]{1,0:T(8,128)(2,1)S(1)}, u32[]{:S(2)}, u32[]{:S(2)}) collective-permute-start(bf16[64,128]{1,0:T(8,128)(2,1)S(1)} %get-tuple-element.24), channel_id=1, source_target_pairs={{0,2},{1,3},{2,0},{3,1},{4,6},{5,7},{6,4},{7,5},{8,10},{9,11},{10,... | collective-permute-start | bytes 49160 | tf_op jit(solution)/shard_map/ppermute | solution.py:369
  99.6 5.8 %collective-permute-start.16 = (bf16[64,128]{1,0:T(8,128)(2,1)S(1)}, bf16[64,128]{1,0:T(8,128)(2,1)S(1)}, u32[]{:S(2)}, u32[]{:S(2)}) collective-permute-start(bf16[64,128]{1,0:T(8,128)(2,1)S(1)} %get-tuple-element.25), channel_id=1, source_target_pairs={{0,3},{1,2},{2,1},{3,0},{4,7},{5,6},{6,5},{7,4},{8,11},{9,10},{10,... | collective-permute-start | bytes 49160 | tf_op jit(solution)/shard_map/ppermute | solution.py:369
  100.1 5.3 %collective-permute-start.17 = (bf16[64,128]{1,0:T(8,128)(2,1)S(1)}, bf16[64,128]{1,0:T(8,128)(2,1)S(1)}, u32[]{:S(2)}, u32[]{:S(2)}) collective-permute-start(bf16[64,128]{1,0:T(8,128)(2,1)S(1)} %get-tuple-element.26), channel_id=1, source_target_pairs={{0,4},{1,5},{2,6},{3,7},{4,0},{5,1},{6,2},{7,3},{8,12},{9,13},{10,... | collective-permute-start | bytes 49160 | tf_op jit(solution)/shard_map/ppermute | solution.py:369
  101.8 4.7 %collective-permute-start.18 = (bf16[64,128]{1,0:T(8,128)(2,1)S(1)}, bf16[64,128]{1,0:T(8,128)(2,1)S(1)}, u32[]{:S(2)}, u32[]{:S(2)}) collective-permute-start(bf16[64,128]{1,0:T(8,128)(2,1)S(1)} %get-tuple-element.27), channel_id=1, source_target_pairs={{0,5},{1,4},{2,7},{3,6},{4,1},{5,0},{6,3},{7,2},{8,13},{9,12},{10,... | collective-permute-start | bytes 49160 | tf_op jit(solution)/shard_map/ppermute | solution.py:369
  103.3 3.4 %collective-permute-start.19 = (bf16[64,128]{1,0:T(8,128)(2,1)S(1)}, bf16[64,128]{1,0:T(8,128)(2,1)S(1)}, u32[]{:S(2)}, u32[]{:S(2)}) collective-permute-start(bf16[64,128]{1,0:T(8,128)(2,1)S(1)} %get-tuple-element.28), channel_id=1, source_target_pairs={{0,6},{1,7},{2,4},{3,5},{4,2},{5,3},{6,0},{7,1},{8,14},{9,15},{10,... | collective-permute-start | bytes 49160 | tf_op jit(solution)/shard_map/ppermute | solution.py:369
  103.8 4.1 %collective-permute-start.20 = (bf16[64,128]{1,0:T(8,128)(2,1)S(1)}, bf16[64,128]{1,0:T(8,128)(2,1)S(1)}, u32[]{:S(2)}, u32[]{:S(2)}) collective-permute-start(bf16[64,128]{1,0:T(8,128)(2,1)S(1)} %get-tuple-element.29), channel_id=1, source_target_pairs={{0,7},{1,6},{2,5},{3,4},{4,3},{5,2},{6,1},{7,0},{8,15},{9,14},{10,... | collective-permute-start | bytes 49160 | tf_op jit(solution)/shard_map/ppermute | solution.py:369
where the time goes:
time: 113 us; the launch traced here: 112 us
  waiting for transfers between devices  56.5 us (50%)
  starting transfers between devices  35.4 us (31%)
  Pallas kernels  15.7 us (14%)
  local copies, waits for them, and re-layouts  2.72 us (2%)
    ppermute x21, waiting for transfers between devices, swap(): return lax.ppermute(block, AXES, pairs)  26.7 us
    all_to_all x1, waiting for transfers between devices, shards(): lax.all_to_all(outgoing, AXES, split_axis=0, concat_axis=0, tiled=True)  19.5 us
    ppermute x21, starting transfers between devices, swap(): return lax.ppermute(block, AXES, pairs)  14.6 us
    all_to_all x1, waiting for transfers between devices, shards(): lax.all_to_all(cross_columns, 'users', split_axis=0, concat_axis=0, tiled...  7.83 us
    pallas_call x1, Pallas kernels, shards(): pl.pallas_call(functools.partial(attend_kernel, slot_stride, kv_slots, bl...  7.61 us
    all_to_all x1, starting transfers between devices, shards(): lax.all_to_all(cross_columns, 'users', split_axis=0, concat_axis=0, tiled...  7.52 us
    all_to_all x1, starting transfers between devices, shards(): lax.all_to_all(outgoing, AXES, split_axis=0, concat_axis=0, tiled=True)  5.94 us
    all_to_all x1, starting transfers between devices, shards(): lax.all_to_all(project_columns, 'users', split_axis=0, concat_axis=0, til...  3.65 us
  transfers between devices with their start and end apart: 25, of which 15 were waited for; matrix products, arithmetic and copies ran while one was open for 2% of the time, Pallas kernels for 1%

commit v1 on v0

--- a/solution.py
+++ b/solution.py
@@ -20,12 +20,9 @@
     return -(-value // step) * step
 
 
-def bias_table(buckets, time_bias):
-    levels = jnp.arange(time_bias.shape[0], dtype=jnp.int32)
-    picked = (buckets[:, None] == levels[None, :]).astype(jnp.float32)
-    return lax.dot_general(
-        time_bias, picked, (((0,), (1,)), ((), ())), precision=lax.Precision.HIGHEST
-    )
+def grant(*arrays):
+    held = sum(int(np.prod(a.shape)) * a.dtype.itemsize for a in arrays)
+    return pltpu.CompilerParams(vmem_limit_bytes=min(60 << 20, 2 * held + (6 << 20)))
 
 
 def pick_columns(inner, context_count, head_width, context, matrix_ref, columns_ref):
@@ -77,62 +74,6 @@
     return pltpu.CompilerParams(vmem_limit_bytes=min(60 << 20, 2 * held + (6 << 20)))
 
 
-def pick_columns(inner, context_count, head_width, context, matrix_ref, columns_ref):
-    owner_count, _, picked = columns_ref.shape
-    blocks = picked // head_width
-    width = matrix_ref.shape[1] // blocks
-    for turn in range(inner):
-        for block in range(blocks):
-            start = block * width + (turn * context_count + context) * head_width
-            piece = matrix_ref[:, pl.ds(pl.multiple_of(start, head_width), head_width)]
-            for first in range(0, owner_count, inner):
-                lanes = slice(block * head_width, (block + 1) * head_width)
-                columns_ref[first + turn, :, lanes] = piece
-
-
-def prepare_kernel(
-    inner,
-    context_count,
-    context_ref,
-    events_ref,
-    owner_ref,
-    bucket_ref,
-    matrix_ref,
-    packed_ref,
-    columns_ref,
-):
-    rows, width = events_ref.shape
-    head_width = packed_ref.shape[1] - width
-    across = owner_ref[...].astype(jnp.float32)
-    owners = jnp.broadcast_to(across, (head_width, rows)).T
-    lane = lax.broadcasted_iota(jnp.int32, (rows, rows), 1)
-    line = lax.broadcasted_iota(jnp.int32, (rows, rows), 0)
-    earlier = (across == owners[:, :1]) & (lane < line)
-    ranking = jnp.sum(jnp.where(earlier, 1.0, 0.0), axis=1, keepdims=True)
-    buckets = jnp.broadcast_to(bucket_ref[...].astype(jnp.float32), (head_width, rows)).T
-    lanes = lax.broadcasted_iota(jnp.int32, (rows, head_width), 1)
-    meta = jnp.where(lanes == 0, owners, jnp.where(lanes == 1, ranking, buckets))
-    packed_ref[:, :width] = events_ref[...]
-    packed_ref[:, width:] = jnp.where(lanes < 3, meta, 0.0).astype(jnp.bfloat16)
-    pick_columns(inner, context_count, head_width, context_ref[0], matrix_ref, columns_ref)
-
-
-def spread_columns_kernel(inner, context_count, head_width, context_ref, matrix_ref, columns_ref):
-    pick_columns(inner, context_count, head_width, context_ref[0], matrix_ref, columns_ref)
-
-
-def grant(*arrays):
-    held = sum(int(np.prod(a.shape)) * a.dtype.itemsize for a in arrays)
-    return pltpu.CompilerParams(vmem_limit_bytes=min(60 << 20, 2 * held + (6 << 20)))
-
-
-def fetch(copies, sems):
-    started = [pltpu.make_async_copy(*pair, sems.at[i]) for i, pair in enumerate(copies)]
-    for copy in started:
-        copy.start()
-    return started
-
-
 def cross_kernel(me_ref, *refs):
     head_count = H
     pieces = refs[:head_count]
@@ -158,7 +99,7 @@
     pieces = refs[:head_count]
     matrix_ref, meta_ref, base_ref = refs[head_count : head_count + 3]
     gate_refs = refs[head_count + 3 : 2 * head_count + 3]
-    send_ref, rows_ref, gate_ref = refs[2 * head_count + 3 :]
+    out_ref, rows_ref, gate_ref, send_ref, sems = refs[2 * head_count + 3 :]
     me = me_ref[0]
     head_width = pieces[0].shape[1]
     for mask in range(head_count):
@@ -182,7 +123,8 @@
     user_count = send_ref.shape[0] // context_count
     chunk = chunk_users * slot_stride
     lane = lax.broadcasted_iota(jnp.int32, (8, head_width), 1)
-    for first in range(0, user_count, chunk_users):
+    started = []
+    for turn, first in enumerate(range(0, user_count, chunk_users)):
         slots = lax.broadcasted_iota(jnp.int32, (chunk, slot_of_row.shape[1]), 0)
         picked = (slots + first * slot_stride == slot_of_row).astype(jnp.float32)
         placed = jnp.dot(
@@ -210,6 +152,44 @@
                 for tile in range(1, kv_slots // 8):
                     note = jnp.where(lane == tile, part[tile * 8 : tile * 8 + 8, :head_width], note)
                 send_ref[target, at : at + 8, :] = note.astype(jnp.bfloat16)
+        done = pl.ds(first * context_count, chunk_users * context_count)
+        copy = pltpu.make_async_copy(send_ref.at[done], out_ref.at[done], sems.at[turn])
+        copy.start()
+        started.append(copy)
+    for copy in started:
+        copy.wait()
+
+
+def stage_kernel(
+    live_ref,
+    after_ref,
+    far_ref,
+    bucket_ref,
+    time_bias_ref,
+    key_order_ref,
+    query_order_ref,
+    near_ref,
+    cache_bias_ref,
+    near_time_bias_ref,
+    near_key_order_ref,
+    near_query_order_ref,
+    sem,
+):
+    copy = pltpu.make_async_copy(far_ref, near_ref, sem)
+    copy.start()
+    table = time_bias_ref[...]
+    shape = (table.shape[1], bucket_ref.shape[1])
+    levels = lax.broadcasted_iota(jnp.int32, shape, 0)
+    picked = jnp.where(levels == bucket_ref[...], 1.0, 0.0)
+    bias = jnp.dot(
+        table, picked, precision=lax.Precision.HIGHEST, preferred_element_type=jnp.float32
+    )
+    positions = lax.broadcasted_iota(jnp.int32, bias.shape, 1)
+    cache_bias_ref[...] = jnp.where(positions < live_ref[0], 0.5 * bias, DEAD)
+    near_time_bias_ref[...] = table
+    near_key_order_ref[...] = key_order_ref[...]
+    near_query_order_ref[...] = query_order_ref[...]
+    copy.wait()
 
 
 def attend_kernel(
@@ -217,27 +197,21 @@
     kv_slots,
     block_groups,
     half_scale,
-    arrived_ref,
-    all_keys_ref,
-    all_values_ref,
+    recv_ref,
+    keys_ref,
+    far_values_ref,
     cache_bias_ref,
     time_bias_ref,
     key_order_ref,
     query_order_ref,
     out_ref,
     summed_ref,
-    recv_ref,
-    keys_ref,
     values_ref,
-    sems,
+    weights_ref,
+    sem,
 ):
-    copies = []
-    for head in range(recv_ref.shape[1]):
-        part = pl.ds(head * recv_ref.shape[3], recv_ref.shape[3])
-        copies.append((arrived_ref.at[:, head], recv_ref.at[:, head]))
-        copies.append((all_keys_ref.at[:, part], keys_ref.at[:, part]))
-        copies.append((all_values_ref.at[:, part], values_ref.at[:, part]))
-    started = fetch(copies, sems)
+    copy = pltpu.make_async_copy(far_values_ref, values_ref, sem)
+    copy.start()
     group_count, head_count, _, head_width = recv_ref.shape
     context_count = slot_stride // kv_slots
     inner = head_count // context_count
@@ -247,45 +221,58 @@
     nt = (((1,), (1,)), ((), ()))
     tn = (((0,), (0,)), ((), ()))
 
+    def weigh(first, head):
+        columns = slice(head * head_width, (head + 1) * head_width)
+        queries = recv_ref[pl.ds(first, block_groups), head, 0:slot_stride, :]
+        queries = queries.reshape(block_rows, head_width)
+        scores = lax.dot_general(
+            queries, keys_ref[:, columns], nt, preferred_element_type=jnp.float32
+        )
+        half = scores * half_scale + cache_bias_ref[head : head + 1, :]
+        weights_ref[head] = (half * (1.0 + jnp.tanh(half))).astype(jnp.bfloat16)
+
+    def gather(block, first, head):
+        columns = slice(head * head_width, (head + 1) * head_width)
+        queries = recv_ref[pl.ds(first, block_groups), head, 0:slot_stride, :]
+        queries = queries.reshape(block_rows, head_width)
+        summed = jnp.dot(
+            weights_ref[head], values_ref[:, columns], preferred_element_type=jnp.float32
+        )
+        at = slot_stride
+        new_keys = recv_ref[:, head, at : at + kv_slots, :].reshape(key_count, head_width)
+        at += kv_slots
+        new_values = recv_ref[:, head, at : at + kv_slots, :].reshape(key_count, head_width)
+        at += kv_slots
+        notes = recv_ref[:, head, at : at + 8, :].astype(jnp.float32)
+        buckets = jnp.concatenate(
+            [notes[g, :, t : t + 1] for g in range(group_count) for t in range(kv_slots // 8)],
+            axis=0,
+        ).astype(jnp.int32)
+        table = time_bias_ref[head : head + 1, :]
+        levels = lax.broadcasted_iota(jnp.int32, (key_count, table.shape[1]), 1)
+        new_bias = jnp.sum(jnp.where(levels == buckets, table, 0.0), axis=1, keepdims=True)
+        new_scores = lax.dot_general(new_keys, queries, nt, preferred_element_type=jnp.float32)
+        new_half = new_scores * half_scale + 0.5 * new_bias
+        new_weights = jnp.where(
+            key_order_ref[...] <= query_order_ref[pl.ds(block, 1), :],
+            new_half * (1.0 + jnp.tanh(new_half)),
+            0.0,
+        ).astype(jnp.bfloat16)
+        summed = summed + lax.dot_general(
+            new_weights, new_values, tn, preferred_element_type=jnp.float32
+        )
+        summed_ref[pl.ds(head, block_rows, stride=head_count), :] = summed
+
     def one_block(block, waits):
         first = block * block_groups
-        for head in range(head_count):
-            if waits:
-                for copy in started[3 * head : 3 * head + 3]:
-                    copy.wait()
-            columns = slice(head * head_width, (head + 1) * head_width)
-            queries = recv_ref[pl.ds(first, block_groups), head, 0:slot_stride, :]
-            queries = queries.reshape(block_rows, head_width)
-            scores = lax.dot_general(
-                queries, keys_ref[:, columns], nt, preferred_element_type=jnp.float32
-            )
-            half = scores * half_scale + cache_bias_ref[head : head + 1, :]
-            weights = (half * (1.0 + jnp.tanh(half))).astype(jnp.bfloat16)
-            summed = jnp.dot(weights, values_ref[:, columns], preferred_element_type=jnp.float32)
-            at = slot_stride
-            new_keys = recv_ref[:, head, at : at + kv_slots, :].reshape(key_count, head_width)
-            at += kv_slots
-            new_values = recv_ref[:, head, at : at + kv_slots, :].reshape(key_count, head_width)
-            at += kv_slots
-            notes = recv_ref[:, head, at : at + 8, :].astype(jnp.float32)
-            buckets = jnp.concatenate(
-                [notes[g, :, t : t + 1] for g in range(group_count) for t in range(kv_slots // 8)],
-                axis=0,
-            ).astype(jnp.int32)
-            table = time_bias_ref[head : head + 1, :]
-            levels = lax.broadcasted_iota(jnp.int32, (key_count, table.shape[1]), 1)
-            new_bias = jnp.sum(jnp.where(levels == buckets, table, 0.0), axis=1, keepdims=True)
-            new_scores = lax.dot_general(new_keys, queries, nt, preferred_element_type=jnp.float32)
-            new_half = new_scores * half_scale + 0.5 * new_bias
-            new_weights = jnp.where(
-                key_order_ref[...] <= query_order_ref[pl.ds(block, 1), :],
-                new_half * (1.0 + jnp.tanh(new_half)),
-                0.0,
-            ).astype(jnp.bfloat16)
-            summed = summed + lax.dot_general(
-                new_weights, new_values, tn, preferred_element_type=jnp.float32
-            )
-            summed_ref[pl.ds(head, block_rows, stride=head_count), :] = summed
+        lag = head_count // 2
+        for head in range(head_count + lag):
+            if head < head_count:
+                weigh(first, head)
+            if waits and head == lag:
+                copy.wait()
+            if head >= lag:
+                gather(block, first, head - lag)
         for group in range(block_groups):
             for context in range(context_count):
                 for turn in range(inner):
@@ -298,8 +285,7 @@
     if block_count == 1:
         one_block(0, True)
     else:
-        for copy in started:
-            copy.wait()
+        copy.wait()
 
         def step(block, carry):
             one_block(block, False)
@@ -360,6 +346,7 @@
     kv_slots = round_up(inner * capacity, 8)
     slot_stride = context_count * kv_slots
     cache_rows = cache_keys.shape[1]
+    bucket_count = time_bias.shape[0]
     group_rows = H * row_count
     core = context_count if inner > 1 else 0
     blocks = project_weight.shape[1] // width
@@ -384,7 +371,7 @@
     ranking = jnp.sum(earlier.astype(jnp.int32), axis=1)
     vmem_spec = pl.BlockSpec(memory_space=VMEM)
     smem_spec = pl.BlockSpec(memory_space=SMEM)
-    any_spec = pl.BlockSpec(memory_space=pl.ANY)
+    hbm_spec = pl.BlockSpec(memory_space=pltpu.MemorySpace.HBM)
     me_scalar = me.astype(jnp.int32).reshape(1)
     context_scalar = context_index.astype(jnp.int32).reshape(1)
     packed_shape = jax.ShapeDtypeStruct((row_count, width + head_width), jnp.bfloat16)
@@ -442,10 +429,12 @@
         out_shape=[jax.ShapeDtypeStruct((row_count, head_width), jnp.bfloat16)] * H
         + [messages],
         in_specs=[smem_spec] + [vmem_spec] * (H + 3),
-        out_specs=[vmem_spec] * (H + 1),
+        out_specs=[vmem_spec] * H + [hbm_spec],
         scratch_shapes=[
             pltpu.VMEM((group_rows, width), jnp.bfloat16),
             pltpu.VMEM((group_rows, head_width), jnp.bfloat16),
+            pltpu.VMEM(messages.shape, messages.dtype),
+            pltpu.SemaphoreType.DMA((owner_count // chunk_users,)),
         ],
         compiler_params=grant(*crossed_pieces, project_columns, messages, messages),
         name="project",
@@ -454,9 +443,6 @@
 
     arrived = lax.all_to_all(outgoing, AXES, split_axis=0, concat_axis=0, tiled=True)
     arrived = arrived.reshape(group_count, H, message_rows, head_width)
-
-    live = jnp.arange(cache_rows, dtype=jnp.int32) < cache_length[0] - context_index * cache_rows
-    cache_bias = jnp.where(live[None, :], 0.5 * bias_table(cache_bucket[0], time_bias), DEAD)
 
     def order_of(group, context, rest):
         member = rest // capacity * context_count + context
@@ -473,30 +459,44 @@
     while group_count % block_groups:
         block_groups -= 1
     block_rows = block_groups * slot_stride
+    live = (cache_length[0] - context_index * cache_rows).astype(jnp.int32).reshape(1)
+    query_order = jnp.asarray(query_order, jnp.int32).reshape(-1, block_rows)
+
+    def far(cache):
+        return pltpu.with_memory_space_constraint(cache[0], pltpu.MemorySpace.HBM)
+
+    near = pl.pallas_call(
+        stage_kernel,
+        out_shape=(
+            jax.ShapeDtypeStruct(cache_keys.shape[1:], cache_keys.dtype),
+            jax.ShapeDtypeStruct((H, cache_rows), jnp.float32),
+            jax.ShapeDtypeStruct((H, bucket_count), jnp.float32),
+            jax.ShapeDtypeStruct((group_count * kv_slots, 1), jnp.int32),
+            jax.ShapeDtypeStruct(query_order.shape, jnp.int32),
+        ),
+        in_specs=[smem_spec, vmem_spec, hbm_spec] + [vmem_spec] * 4,
+        out_specs=[vmem_spec] * 5,
+        scratch_shapes=[pltpu.SemaphoreType.DMA(())],
+        compiler_params=grant(cache_keys),
+        name="stage",
+    )(live, gates[0], far(cache_keys), cache_bucket, time_bias.T, key_order[:, None], query_order)
+
     partials = pl.pallas_call(
         functools.partial(
             attend_kernel, slot_stride, kv_slots, block_groups, 0.5 * head_width**-0.5
         ),
         out_shape=jax.ShapeDtypeStruct((device_count, capacity * H, head_width), jnp.bfloat16),
-        in_specs=[any_spec] * 3 + [vmem_spec] * 4,
+        in_specs=[vmem_spec] * 2 + [hbm_spec] + [vmem_spec] * 4,
         out_specs=vmem_spec,
         scratch_shapes=[
             pltpu.VMEM((block_rows * H, head_width), jnp.float32),
-            pltpu.VMEM(arrived.shape, arrived.dtype),
-            pltpu.VMEM(cache_keys.shape[1:], cache_keys.dtype),
             pltpu.VMEM(cache_values.shape[1:], cache_values.dtype),
-            pltpu.SemaphoreType.DMA((3 * H,)),
+            pltpu.VMEM((H, block_rows, cache_rows), jnp.bfloat16),
+            pltpu.SemaphoreType.DMA(()),
         ],
+        compiler_params=grant(arrived, cache_keys, cache_values, query_order),
         name="attend",
-    )(
-        arrived,
-        cache_keys[0],
-        cache_values[0],
-        cache_bias,
-        time_bias.T,
-        key_order[:, None],
-        jnp.asarray(query_order, jnp.int32).reshape(-1, block_rows),
-    )
+    )(arrived, near[0], far(cache_values), *near[1:])
 
     returned = lax.all_to_all(partials, AXES, split_axis=0, concat_axis=0, tiled=True)
     contexts = jnp.arange(context_count, dtype=jnp.int32)[None, :]

time: 113 us -> 108 us (0.956)
  local copies, waits for them, and re-layouts: 2.72 us -> 1.19 us
  Pallas kernels: 15.7 us -> 14.2 us
    pallas_call x1, Pallas kernels: 7.61 us -> 4.68 us  [shards(): pl.pallas_call(functools.partial(attend_kernel, slot_stride, kv_slots, bl...]
    pallas_call x0 -> x1, Pallas kernels: none -> 1.6 us  [shards(): pl.pallas_call(stage_kernel, out_shape=(jax.ShapeDtypeStruct(cache_keys.s...]
    ppermute x21, waiting for transfers between devices: 26.7 us -> 25.6 us  [swap(): return lax.ppermute(block, AXES, pairs)]
  transfers between devices with their start and end apart: 25 -> 25, of which waited for: 15 -> 15; matrix products, arithmetic and copies ran while one was open for 2% -> 0% of each run, Pallas kernels for 1% -> 3%
where the time goes in v1:
time: 108 us
  waiting for transfers between devices  55.4 us (51%)
  starting transfers between devices  35.7 us (33%)
  Pallas kernels  14.2 us (13%)
  local copies, waits for them, and re-layouts  1.19 us (1%)
    ppermute x21, waiting for transfers between devices, swap(): return lax.ppermute(block, AXES, pairs)  25.6 us
    all_to_all x1, waiting for transfers between devices, shards(): lax.all_to_all(outgoing, AXES, split_axis=0, concat_axis=0, tiled=True)  19.6 us
    ppermute x21, starting transfers between devices, swap(): return lax.ppermute(block, AXES, pairs)  15.1 us
    all_to_all x1, waiting for transfers between devices, shards(): lax.all_to_all(cross_columns, 'users', split_axis=0, concat_axis=0, tiled...  7.84 us
    all_to_all x1, starting transfers between devices, shards(): lax.all_to_all(cross_columns, 'users', split_axis=0, concat_axis=0, tiled...  7.52 us
    all_to_all x1, starting transfers between devices, shards(): lax.all_to_all(outgoing, AXES, split_axis=0, concat_axis=0, tiled=True)  5.76 us
    pallas_call x1, Pallas kernels, shards(): pl.pallas_call(functools.partial(attend_kernel, slot_stride, kv_slots, bl...  4.68 us
    all_to_all x1, starting transfers between devices, shards(): lax.all_to_all(project_columns, 'users', split_axis=0, concat_axis=0, til...  3.65 us
  transfers between devices with their start and end apart: 25, of which 15 were waited for; matrix products, arithmetic and copies ran while one was open for 0% of the time, Pallas kernels for 3%

profile of v1, /device:TPU:0, one launch (start us, length us, event | category | flops | bytes accessed | tf_op | source)
XLA Modules:
  0.0 107.6 jit_solution(8432329380750413018)
XLA Ops:
  0.0 1.9 %prepare.1 = (bf16[64,1152]{1,0:T(8,128)(2,1)}, bf16[16,64,128]{2,1,0:T(8,128)(2,1)}) custom-call(s32[1]{0:T(128)} %bitcast.3.context_ref, bf16[64,1024]{1,0:T(8,128)(2,1)} %events_ref.1, s32[1,64]{1,0:T(1,128)} %bitcast.31, s32[1,64]{1,0:T(1,128)} %bitcast.30, bf16[64,1024]{1,0:T(8,128)(2,1)} %matrix_ref.2), custom_call_target="tpu_custom_call" | custom-call | tf_op jit(solution)/shard_map/prepare/pallas_call | solution.py:380
  1.9 7.5 %all-to-all-start = ((bf16[16,64,128]{2,1,0:T(8,128)(2,1)}), bf16[16,64,128]{2,1,0:T(8,128)(2,1)S(1)}, u32[]{:S(2)}, u32[]{:S(2)}) async-start(bf16[16,64,128]{2,1,0:T(8,128)(2,1)} %get-tuple-element.24), calls=%async_computation | async-start | bytes 524288 | tf_op jit(solution)/shard_map/all_to_all | solution.py:400
  9.5 0.0 copy-start
  9.5 1.0 copy-done
  10.5 1.1 %columns.1 = bf16[16,64,512]{2,1,0:T(8,128)(2,1)} custom-call(s32[1]{0:T(128)} %bitcast.3.context_ref, bf16[64,4096]{1,0:T(8,128)(2,1)S(1)} %copy-done), custom_call_target="tpu_custom_call" | custom-call | tf_op jit(solution)/shard_map/columns/pallas_call | solution.py:391
  11.6 7.8 %all-to-all-done = bf16[16,64,128]{2,1,0:T(8,128)(2,1)S(1)} async-done(((bf16[16,64,128]{2,1,0:T(8,128)(2,1)}), bf16[16,64,128]{2,1,0:T(8,128)(2,1)S(1)}, u32[]{:S(2)}, u32[]{:S(2)}) %all-to-all-start) | async-done | bytes 262176 | tf_op jit(solution)/shard_map/all_to_all | solution.py:400
  19.5 3.7 %all-to-all-start.1 = ((bf16[16,64,512]{2,1,0:T(8,128)(2,1)}), bf16[16,64,512]{2,1,0:T(8,128)(2,1)S(1)}, u32[]{:S(2)}, u32[]{:S(2)}) async-start(bf16[16,64,512]{2,1,0:T(8,128)(2,1)} %columns.1), calls=%async_computation.1 | async-start | bytes 2097152 | tf_op jit(solution)/shard_map/all_to_all | solution.py:401
  23.1 2.8 %collective-permute-start.4 = (bf16[64,1152]{1,0:T(8,128)(2,1)S(1)}, bf16[64,1152]{1,0:T(8,128)(2,1)S(1)}, u32[]{:S(2)}, u32[]{:S(2)}) collective-permute-start(bf16[64,1152]{1,0:T(8,128)(2,1)S(1)} %copy-done.1), channel_id=1, source_target_pairs={{0,5},{1,4},{2,7},{3,6},{4,1},{5,0},{6,3},{7,2},{8,13},{9,12},{10,... | collective-permute-start | bytes 442376 | tf_op jit(solution)/shard_map/ppermute | solution.py:356
  26.0 0.2 collective-permute-start.3
  26.2 0.5 collective-permute-start
  26.7 12.5 %collective-permute-done.4.refs_5_ = bf16[64,1152]{1,0:T(8,128)(2,1)S(1)} collective-permute-done((bf16[64,1152]{1,0:T(8,128)(2,1)S(1)}, bf16[64,1152]{1,0:T(8,128)(2,1)S(1)}, u32[]{:S(2)}, u32[]{:S(2)}) %collective-permute-start.4) | collective-permute-done | bytes 147488 | tf_op jit(solution)/shard_map/ppermute | solution.py:356
  39.2 1.6 %collective-permute-done.3.refs_4_ = bf16[64,1152]{1,0:T(8,128)(2,1)S(1)} collective-permute-done((bf16[64,1152]{1,0:T(8,128)(2,1)S(1)}, bf16[64,1152]{1,0:T(8,128)(2,1)S(1)}, u32[]{:S(2)}, u32[]{:S(2)}) %collective-permute-start.3) | collective-permute-done | bytes 147488 | tf_op jit(solution)/shard_map/ppermute | solution.py:356
  40.9 0.5 collective-permute-start.2
  41.4 0.9 collective-permute-done.5.refs_6_
  42.2 0.2 collective-permute-done.2.refs_3_
  42.4 0.4 cross.1
  42.9 0.0 copy-start.9
  42.9 0.0 copy-start.4
  42.9 0.0 copy-start.7
  42.9 2.8 %collective-permute-start.11 = (bf16[512,128]{1,0:T(8,128)(2,1)S(1)}, bf16[512,128]{1,0:T(8,128)(2,1)S(1)}, u32[]{:S(2)}, u32[]{:S(2)}) collective-permute-start(bf16[512,128]{1,0:T(8,128)(2,1)S(1)} %get-tuple-element.25.refs_0_), channel_id=1, source_target_pairs={{0,5},{1,4},{2,7},{3,6},{4,1},{5,0},{6,3},{7,2},{8,13},{9,12},{10,... | collective-permute-start | bytes 393224 | tf_op jit(solution)/shard_map/ppermute | solution.py:356
  45.7 0.2 collective-permute-start.10
  46.0 0.5 collective-permute-start.7
  46.5 3.9 %collective-permute-done.11.refs_5_ = bf16[512,128]{1,0:T(8,128)(2,1)S(1)} collective-permute-done((bf16[512,128]{1,0:T(8,128)(2,1)S(1)}, bf16[512,128]{1,0:T(8,128)(2,1)S(1)}, u32[]{:S(2)}, u32[]{:S(2)}) %collective-permute-start.11) | collective-permute-done | bytes 131104 | tf_op jit(solution)/shard_map/ppermute | solution.py:356
  50.4 2.0 %collective-permute-done.10.refs_4_ = bf16[512,128]{1,0:T(8,128)(2,1)S(1)} collective-permute-done((bf16[512,128]{1,0:T(8,128)(2,1)S(1)}, bf16[512,128]{1,0:T(8,128)(2,1)S(1)}, u32[]{:S(2)}, u32[]{:S(2)}) %collective-permute-start.10) | collective-permute-done | bytes 131104 | tf_op jit(solution)/shard_map/ppermute | solution.py:356
  52.5 0.5 collective-permute-done.7.refs_1_
  53.0 0.0 collective-permute-start.9
  53.0 0.8 collective-permute-done.12.refs_6_
  53.8 0.5 collective-permute-done.9.refs_3_
  54.3 2.4 %project.1 = (bf16[64,128]{1,0:T(8,128)(2,1)S(1)}, bf16[64,128]{1,0:T(8,128)(2,1)S(1)}, bf16[64,128]{1,0:T(8,128)(2,1)S(1)}, bf16[64,128]{1,0:T(8,128)(2,1)S(1)}...) custom-call(s32[1]{0:T(128)} %bitcast.me_ref, ...), custom_call_target="tpu_custom_call" | custom-call | tf_op jit(solution)/shard_map/project/pallas_call | solution.py:427
  56.7 5.8 %all-to-all-start.2 = ((bf16[32,104,128]{2,1,0:T(8,128)(2,1)}), bf16[32,104,128]{2,1,0:T(8,128)(2,1)S(1)}, u32[]{:S(2)}, u32[]{:S(2)}) async-start(bf16[32,104,128]{2,1,0:T(8,128)(2,1)} %get-tuple-element.35), calls=%async_computation.2 | async-start | bytes 1703936 | tf_op jit(solution)/shard_map/all_to_all | solution.py:444
  63.1 0.1 copy.19.key_order_ref
  63.3 1.6 %stage.1 = (bf16[1024,1024]{1,0:T(8,128)(2,1)S(1)}, f32[8,1024]{1,0:T(8,128)S(1)}, f32[8,32]{1,0:T(8,128)S(1)}, s32[96,1]{1,0:T(8,128)S(1)}, s32[1,192]{1,0:T(1,128)S(1)}) custom-call(s32[1]{0:T(128)} %bitcast.11.live_ref, bf16[64,128]{1,0:T(8,128)(2,1)S(1)} %get-tuple-element.27.after_ref.refs_0_, bf16[1024,1024]{1,0:T(8,128)(2,1)} %bitcast.28, ...), custom_call_target="tpu_custom_call" | custom-call | tf_op jit(solution)/shard_map/stage/pallas_call | solution.py:468
  64.9 19.6 %all-to-all-done.2 = bf16[32,104,128]{2,1,0:T(8,128)(2,1)S(1)} async-done(((bf16[32,104,128]{2,1,0:T(8,128)(2,1)}), bf16[32,104,128]{2,1,0:T(8,128)(2,1)S(1)}, u32[]{:S(2)}, u32[]{:S(2)}) %all-to-all-start.2) | async-done | bytes 852000 | tf_op jit(solution)/shard_map/all_to_all | solution.py:444
  84.5 4.7 %attend.1 = bf16[32,48,128]{2,1,0:T(8,128)(2,1)} custom-call(bf16[4,8,104,128]{3,2,1,0:T(8,128)(2,1)S(1)} %bitcast.22, bf16[1024,1024]{1,0:T(8,128)(2,1)S(1)} %get-tuple-element.36.keys_ref, bf16[1024,1024]{1,0:T(8,128)(2,1)} %bitcast.29, f32[8,1024]{1,0:T(8,128)S(1)} %get-tuple-element.37.cache_bias_ref, f32[8,32]{1,0:T(8,128)S(1)} %get-tuple-element.38.time_bias_ref, ...), custom_call_target="tpu_custom_call" | custom-call | tf_op jit(solution)/shard_map/attend/pallas_call | solution.py:484
  89.2 3.6 %all-to-all-start.3 = ((bf16[32,48,128]{2,1,0:T(8,128)(2,1)}), bf16[32,48,128]{2,1,0:T(8,128)(2,1)S(1)}, u32[]{:S(2)}, u32[]{:S(2)}) async-start(bf16[32,48,128]{2,1,0:T(8,128)(2,1)} %attend.1), calls=%async_computation.3 | async-start | bytes 786432 | tf_op jit(solution)/shard_map/all_to_all | solution.py:501
  92.8 1.8 %collective-permute-start.14 = (bf16[64,128]{1,0:T(8,128)(2,1)S(1)}, bf16[64,128]{1,0:T(8,128)(2,1)S(1)}, u32[]{:S(2)}, u32[]{:S(2)}) collective-permute-start(bf16[64,128]{1,0:T(8,128)(2,1)S(1)} %get-tuple-element.28), channel_id=1, source_target_pairs={{0,1},{1,0},{2,3},{3,2},{4,5},{5,4},{6,7},{7,6},{8,9},{9,8},{10,11... | collective-permute-start | bytes 49160 | tf_op jit(solution)/shard_map/ppermute | solution.py:356
  94.6 0.2 convert_reduce_fusion
  94.8 0.4 collective-permute-start.16
  95.3 1.8 %collective-permute-start.17 = (bf16[64,128]{1,0:T(8,128)(2,1)S(1)}, bf16[64,128]{1,0:T(8,128)(2,1)S(1)}, u32[]{:S(2)}, u32[]{:S(2)}) collective-permute-start(bf16[64,128]{1,0:T(8,128)(2,1)S(1)} %get-tuple-element.31), channel_id=1, source_target_pairs={{0,4},{1,5},{2,6},{3,7},{4,0},{5,1},{6,2},{7,3},{8,12},{9,13},{10,... | collective-permute-start | bytes 49160 | tf_op jit(solution)/shard_map/ppermute | solution.py:356
  97.0 1.5 %collective-permute-start.18 = (bf16[64,128]{1,0:T(8,128)(2,1)S(1)}, bf16[64,128]{1,0:T(8,128)(2,1)S(1)}, u32[]{:S(2)}, u32[]{:S(2)}) collective-permute-start(bf16[64,128]{1,0:T(8,128)(2,1)S(1)} %get-tuple-element.32), channel_id=1, source_target_pairs={{0,5},{1,4},{2,7},{3,6},{4,1},{5,0},{6,3},{7,2},{8,13},{9,12},{10,... | collective-permute-start | bytes 49160 | tf_op jit(solution)/shard_map/ppermute | solution.py:356
  98.5 0.5 collective-permute-start.19
  99.0 1.5 %collective-permute-start.20 = (bf16[64,128]{1,0:T(8,128)(2,1)S(1)}, bf16[64,128]{1,0:T(8,128)(2,1)S(1)}, u32[]{:S(2)}, u32[]{:S(2)}) collective-permute-start(bf16[64,128]{1,0:T(8,128)(2,1)S(1)} %get-tuple-element.34), channel_id=1, source_target_pairs={{0,7},{1,6},{2,5},{3,4},{4,3},{5,2},{6,1},{7,0},{8,15},{9,14},{10,... | collective-permute-start | bytes 49160 | tf_op jit(solution)/shard_map/ppermute | solution.py:356
  100.5 0.1 multiply_add_fusion.place_ref
  100.6 1.1 %collective-permute-done.18.refs_5_ = bf16[64,128]{1,0:T(8,128)(2,1)S(1)} collective-permute-done((bf16[64,128]{1,0:T(8,128)(2,1)S(1)}, bf16[64,128]{1,0:T(8,128)(2,1)S(1)}, u32[]{:S(2)}, u32[]{:S(2)}) %collective-permute-start.18) | collective-permute-done | bytes 16416 | tf_op jit(solution)/shard_map/ppermute | solution.py:356
  101.7 0.1 collective-permute-done.19.refs_6_
  101.8 1.3 %collective-permute-done.20.refs_7_ = bf16[64,128]{1,0:T(8,128)(2,1)S(1)} collective-permute-done((bf16[64,128]{1,0:T(8,128)(2,1)S(1)}, bf16[64,128]{1,0:T(8,128)(2,1)S(1)}, u32[]{:S(2)}, u32[]{:S(2)}) %collective-permute-start.20) | collective-permute-done | bytes 16416 | tf_op jit(solution)/shard_map/ppermute | solution.py:356
  103.1 2.4 %all-to-all-done.3 = bf16[32,48,128]{2,1,0:T(8,128)(2,1)S(1)} async-done(((bf16[32,48,128]{2,1,0:T(8,128)(2,1)}), bf16[32,48,128]{2,1,0:T(8,128)(2,1)S(1)}, u32[]{:S(2)}, u32[]{:S(2)}) %all-to-all-start.3) | async-done | bytes 393248 | tf_op jit(solution)/shard_map/all_to_all | solution.py:501
  105.5 2.1 %finish.1 = bf16[64,1024]{1,0:T(8,128)(2,1)} custom-call(s32[1]{0:T(128)} %bitcast.me_ref, s32[64,2]{1,0:T(8,128)S(1)} %multiply_add_fusion.place_ref, bf16[64,128]{1,0:T(8,128)(2,1)S(1)} %get-tuple-element.27.after_ref.refs_0_, bf16[64,128]{1,0:T(8,128)(2,1)S(1)} %collective-permute-done.14.refs_1_, bf16[64,128]{1,0:T(8,128)(2,1)S(1)} %collective-permute-done.15.refs_2_, ...), custom_call_target="tpu_custom_call" | custom-call | tf_op jit(solution)/shard_map/finish/pallas_call | solution.py:504
  (34 shorter events, 0.1 us)
Async XLA Ops:
  1.9 21.2 %copy-start.1 = (bf16[64,1152]{1,0:T(8,128)(2,1)S(1)}, bf16[64,1152]{1,0:T(8,128)(2,1)}, u32[]{:S(2)}) copy-start(bf16[64,1152]{1,0:T(8,128)(2,1)} %get-tuple-element.23.refs_0_) | copy-start | bytes 442372
  1.9 40.5 %copy-start.2 = (f32[1024]{0:T(1024)S(1)}, f32[1024]{0:T(1024)}, u32[]{:S(2)}) copy-start(f32[1024]{0:T(1024)} %param.19) | copy-start | bytes 12292
  1.9 17.5 %all-to-all-start = ((bf16[16,64,128]{2,1,0:T(8,128)(2,1)}), bf16[16,64,128]{2,1,0:T(8,128)(2,1)S(1)}, u32[]{:S(2)}, u32[]{:S(2)}) async-start(bf16[16,64,128]{2,1,0:T(8,128)(2,1)} %get-tuple-element.24), calls=%async_computation | async-start | bytes 524288 | tf_op jit(solution)/shard_map/all_to_all | solution.py:400
  9.5 1.0 copy-start
  11.6 42.7 %copy-start.6 = (s32[1,512]{1,0:T(1,128)S(1)}, s32[1,512]{1,0:T(1,128)}, u32[]{:S(2)}) copy-start(s32[1,512]{1,0:T(1,128)} %constant.36.clone.refs_10_) | copy-start | bytes 6148
  19.5 34.9 %all-to-all-start.1 = ((bf16[16,64,512]{2,1,0:T(8,128)(2,1)}), bf16[16,64,512]{2,1,0:T(8,128)(2,1)S(1)}, u32[]{:S(2)}, u32[]{:S(2)}) async-start(bf16[16,64,512]{2,1,0:T(8,128)(2,1)} %columns.1), calls=%async_computation.1 | async-start | bytes 2097152 | tf_op jit(solution)/shard_map/all_to_all | solution.py:401
  23.1 16.1 %collective-permute-start.4 = (bf16[64,1152]{1,0:T(8,128)(2,1)S(1)}, bf16[64,1152]{1,0:T(8,128)(2,1)S(1)}, u32[]{:S(2)}, u32[]{:S(2)}) collective-permute-start(bf16[64,1152]{1,0:T(8,128)(2,1)S(1)} %copy-done.1), channel_id=1, source_target_pairs={{0,5},{1,4},{2,7},{3,6},{4,1},{5,0},{6,3},{7,2},{8,13},{9,12},{10,... | collective-permute-start | bytes 442376 | tf_op jit(solution)/shard_map/ppermute | solution.py:356
  26.0 14.9 %collective-permute-start.3 = (bf16[64,1152]{1,0:T(8,128)(2,1)S(1)}, bf16[64,1152]{1,0:T(8,128)(2,1)S(1)}, u32[]{:S(2)}, u32[]{:S(2)}) collective-permute-start(bf16[64,1152]{1,0:T(8,128)(2,1)S(1)} %copy-done.1), channel_id=1, source_target_pairs={{0,4},{1,5},{2,6},{3,7},{4,0},{5,1},{6,2},{7,3},{8,12},{9,13},{10,... | collective-permute-start | bytes 442376 | tf_op jit(solution)/shard_map/ppermute | solution.py:356
  26.2 14.7 %collective-permute-start = (bf16[64,1152]{1,0:T(8,128)(2,1)S(1)}, bf16[64,1152]{1,0:T(8,128)(2,1)S(1)}, u32[]{:S(2)}, u32[]{:S(2)}) collective-permute-start(bf16[64,1152]{1,0:T(8,128)(2,1)S(1)} %copy-done.1), channel_id=1, source_target_pairs={{0,1},{1,0},{2,3},{3,2},{4,5},{5,4},{6,7},{7,6},{8,9},{9,8},{10,11... | collective-permute-start | bytes 442376 | tf_op jit(solution)/shard_map/ppermute | solution.py:356
  26.7 14.7 %collective-permute-start.1 = (bf16[64,1152]{1,0:T(8,128)(2,1)S(1)}, bf16[64,1152]{1,0:T(8,128)(2,1)S(1)}, u32[]{:S(2)}, u32[]{:S(2)}) collective-permute-start(bf16[64,1152]{1,0:T(8,128)(2,1)S(1)} %copy-done.1), channel_id=1, source_target_pairs={{0,2},{1,3},{2,0},{3,1},{4,6},{5,7},{6,4},{7,5},{8,10},{9,11},{10,... | collective-permute-start | bytes 442376 | tf_op jit(solution)/shard_map/ppermute | solution.py:356
  39.2 2.2 %collective-permute-start.6 = (bf16[64,1152]{1,0:T(8,128)(2,1)S(1)}, bf16[64,1152]{1,0:T(8,128)(2,1)S(1)}, u32[]{:S(2)}, u32[]{:S(2)}) collective-permute-start(bf16[64,1152]{1,0:T(8,128)(2,1)S(1)} %collective-permute-done.4.refs_5_), channel_id=1, source_target_pairs={{0,2},{1,3},{2,0},{3,1},{4,6},{5,7},{6,4},{7,5},{8,10},{9,11},{10,... | collective-permute-start | bytes 442376 | tf_op jit(solution)/shard_map/ppermute | solution.py:356
  40.9 1.4 %collective-permute-start.5 = (bf16[64,1152]{1,0:T(8,128)(2,1)S(1)}, bf16[64,1152]{1,0:T(8,128)(2,1)S(1)}, u32[]{:S(2)}, u32[]{:S(2)}) collective-permute-start(bf16[64,1152]{1,0:T(8,128)(2,1)S(1)} %collective-permute-done.3.refs_4_), channel_id=1, source_target_pairs={{0,2},{1,3},{2,0},{3,1},{4,6},{5,7},{6,4},{7,5},{8,10},{9,11},{10,... | collective-permute-start | bytes 442376 | tf_op jit(solution)/shard_map/ppermute | solution.py:356
  40.9 1.6 %collective-permute-start.2 = (bf16[64,1152]{1,0:T(8,128)(2,1)S(1)}, bf16[64,1152]{1,0:T(8,128)(2,1)S(1)}, u32[]{:S(2)}, u32[]{:S(2)}) collective-permute-start(bf16[64,1152]{1,0:T(8,128)(2,1)S(1)} %collective-permute-done.refs_1_), channel_id=1, source_target_pairs={{0,2},{1,3},{2,0},{3,1},{4,6},{5,7},{6,4},{7,5},{8,10},{9,11},{10,... | collective-permute-start | bytes 442376 | tf_op jit(solution)/shard_map/ppermute | solution.py:356
  42.9 20.2 %copy-start.9 = (s32[96]{0:T(128)S(1)}, s32[96]{0:T(128)}, u32[]{:S(2)}) copy-start(s32[96]{0:T(128)} %constant.37.clone) | copy-start | bytes 1156
  42.9 20.3 %copy-start.3 = (s32[1,1024]{1,0:T(1,128)S(1)}, s32[1,1024]{1,0:T(1,128)}, u32[]{:S(2)}) copy-start(s32[1,1024]{1,0:T(1,128)} %bucket_ref.1) | copy-start | bytes 12292
  42.9 20.3 %copy-start.4 = (f32[32,8]{0,1:T(8,128)S(1)}, f32[32,8]{0,1:T(8,128)}, u32[]{:S(2)}) copy-start(f32[32,8]{0,1:T(8,128)} %param.25) | copy-start | bytes 3076
  42.9 20.3 %copy-start.7 = (s32[1,192]{1,0:T(1,128)S(1)}, s32[1,192]{1,0:T(1,128)}, u32[]{:S(2)}) copy-start(s32[1,192]{1,0:T(1,128)} %constant.43.query_order_ref) | copy-start | bytes 2308
  42.9 7.5 %collective-permute-start.11 = (bf16[512,128]{1,0:T(8,128)(2,1)S(1)}, bf16[512,128]{1,0:T(8,128)(2,1)S(1)}, u32[]{:S(2)}, u32[]{:S(2)}) collective-permute-start(bf16[512,128]{1,0:T(8,128)(2,1)S(1)} %get-tuple-element.25.refs_0_), channel_id=1, source_target_pairs={{0,5},{1,4},{2,7},{3,6},{4,1},{5,0},{6,3},{7,2},{8,13},{9,12},{10,... | collective-permute-start | bytes 393224 | tf_op jit(solution)/shard_map/ppermute | solution.py:356
  45.7 6.7 %collective-permute-start.10 = (bf16[512,128]{1,0:T(8,128)(2,1)S(1)}, bf16[512,128]{1,0:T(8,128)(2,1)S(1)}, u32[]{:S(2)}, u32[]{:S(2)}) collective-permute-start(bf16[512,128]{1,0:T(8,128)(2,1)S(1)} %get-tuple-element.25.refs_0_), channel_id=1, source_target_pairs={{0,4},{1,5},{2,6},{3,7},{4,0},{5,1},{6,2},{7,3},{8,12},{9,13},{10,... | collective-permute-start | bytes 393224 | tf_op jit(solution)/shard_map/ppermute | solution.py:356
  46.0 7.0 %collective-permute-start.7 = (bf16[512,128]{1,0:T(8,128)(2,1)S(1)}, bf16[512,128]{1,0:T(8,128)(2,1)S(1)}, u32[]{:S(2)}, u32[]{:S(2)}) collective-permute-start(bf16[512,128]{1,0:T(8,128)(2,1)S(1)} %get-tuple-element.25.refs_0_), channel_id=1, source_target_pairs={{0,1},{1,0},{2,3},{3,2},{4,5},{5,4},{6,7},{7,6},{8,9},{9,8},{10,11... | collective-permute-start | bytes 393224 | tf_op jit(solution)/shard_map/ppermute | solution.py:356
  46.5 6.5 %collective-permute-start.8 = (bf16[512,128]{1,0:T(8,128)(2,1)S(1)}, bf16[512,128]{1,0:T(8,128)(2,1)S(1)}, u32[]{:S(2)}, u32[]{:S(2)}) collective-permute-start(bf16[512,128]{1,0:T(8,128)(2,1)S(1)} %get-tuple-element.25.refs_0_), channel_id=1, source_target_pairs={{0,2},{1,3},{2,0},{3,1},{4,6},{5,7},{6,4},{7,5},{8,10},{9,11},{10,... | collective-permute-start | bytes 393224 | tf_op jit(solution)/shard_map/ppermute | solution.py:356
  50.4 2.6 %collective-permute-start.13 = (bf16[512,128]{1,0:T(8,128)(2,1)S(1)}, bf16[512,128]{1,0:T(8,128)(2,1)S(1)}, u32[]{:S(2)}, u32[]{:S(2)}) collective-permute-start(bf16[512,128]{1,0:T(8,128)(2,1)S(1)} %collective-permute-done.11.refs_5_), channel_id=1, source_target_pairs={{0,2},{1,3},{2,0},{3,1},{4,6},{5,7},{6,4},{7,5},{8,10},{9,11},{10,... | collective-permute-start | bytes 393224 | tf_op jit(solution)/shard_map/ppermute | solution.py:356
  52.5 1.3 %collective-permute-start.12 = (bf16[512,128]{1,0:T(8,128)(2,1)S(1)}, bf16[512,128]{1,0:T(8,128)(2,1)S(1)}, u32[]{:S(2)}, u32[]{:S(2)}) collective-permute-start(bf16[512,128]{1,0:T(8,128)(2,1)S(1)} %collective-permute-done.10.refs_4_), channel_id=1, source_target_pairs={{0,2},{1,3},{2,0},{3,1},{4,6},{5,7},{6,4},{7,5},{8,10},{9,11},{10,... | collective-permute-start | bytes 393224 | tf_op jit(solution)/shard_map/ppermute | solution.py:356
  53.0 1.3 %collective-permute-start.9 = (bf16[512,128]{1,0:T(8,128)(2,1)S(1)}, bf16[512,128]{1,0:T(8,128)(2,1)S(1)}, u32[]{:S(2)}, u32[]{:S(2)}) collective-permute-start(bf16[512,128]{1,0:T(8,128)(2,1)S(1)} %collective-permute-done.7.refs_1_), channel_id=1, source_target_pairs={{0,2},{1,3},{2,0},{3,1},{4,6},{5,7},{6,4},{7,5},{8,10},{9,11},{10,... | collective-permute-start | bytes 393224 | tf_op jit(solution)/shard_map/ppermute | solution.py:356
  56.7 27.8 %all-to-all-start.2 = ((bf16[32,104,128]{2,1,0:T(8,128)(2,1)}), bf16[32,104,128]{2,1,0:T(8,128)(2,1)S(1)}, u32[]{:S(2)}, u32[]{:S(2)}) async-start(bf16[32,104,128]{2,1,0:T(8,128)(2,1)} %get-tuple-element.35), calls=%async_computation.2 | async-start | bytes 1703936 | tf_op jit(solution)/shard_map/all_to_all | solution.py:444
  84.5 8.3 %copy-start.8 = (s32[64,1]{0,1:T(1,128)S(1)}, s32[64,1]{0,1:T(1,128)}, u32[]{:S(2)}) copy-start(s32[64,1]{0,1:T(1,128)} %param.16) | copy-start | bytes 772
  84.5 21.1 %copy-start.5 = (f32[1024]{0:T(1024)S(1)}, f32[1024]{0:T(1024)}, u32[]{:S(2)}) copy-start(f32[1024]{0:T(1024)} %param.26) | copy-start | bytes 12292
  89.2 16.4 %all-to-all-start.3 = ((bf16[32,48,128]{2,1,0:T(8,128)(2,1)}), bf16[32,48,128]{2,1,0:T(8,128)(2,1)S(1)}, u32[]{:S(2)}, u32[]{:S(2)}) async-start(bf16[32,48,128]{2,1,0:T(8,128)(2,1)} %attend.1), calls=%async_computation.3 | async-start | bytes 786432 | tf_op jit(solution)/shard_map/all_to_all | solution.py:501
  92.8 5.7 %collective-permute-start.14 = (bf16[64,128]{1,0:T(8,128)(2,1)S(1)}, bf16[64,128]{1,0:T(8,128)(2,1)S(1)}, u32[]{:S(2)}, u32[]{:S(2)}) collective-permute-start(bf16[64,128]{1,0:T(8,128)(2,1)S(1)} %get-tuple-element.28), channel_id=1, source_target_pairs={{0,1},{1,0},{2,3},{3,2},{4,5},{5,4},{6,7},{7,6},{8,9},{9,8},{10,11... | collective-permute-start | bytes 49160 | tf_op jit(solution)/shard_map/ppermute | solution.py:356
  94.6 4.4 %collective-permute-start.15 = (bf16[64,128]{1,0:T(8,128)(2,1)S(1)}, bf16[64,128]{1,0:T(8,128)(2,1)S(1)}, u32[]{:S(2)}, u32[]{:S(2)}) collective-permute-start(bf16[64,128]{1,0:T(8,128)(2,1)S(1)} %get-tuple-element.29), channel_id=1, source_target_pairs={{0,2},{1,3},{2,0},{3,1},{4,6},{5,7},{6,4},{7,5},{8,10},{9,11},{10,... | collective-permute-start | bytes 49160 | tf_op jit(solution)/shard_map/ppermute | solution.py:356
  94.8 5.8 %collective-permute-start.16 = (bf16[64,128]{1,0:T(8,128)(2,1)S(1)}, bf16[64,128]{1,0:T(8,128)(2,1)S(1)}, u32[]{:S(2)}, u32[]{:S(2)}) collective-permute-start(bf16[64,128]{1,0:T(8,128)(2,1)S(1)} %get-tuple-element.30), channel_id=1, source_target_pairs={{0,3},{1,2},{2,1},{3,0},{4,7},{5,6},{6,5},{7,4},{8,11},{9,10},{10,... | collective-permute-start | bytes 49160 | tf_op jit(solution)/shard_map/ppermute | solution.py:356
  95.3 5.3 %collective-permute-start.17 = (bf16[64,128]{1,0:T(8,128)(2,1)S(1)}, bf16[64,128]{1,0:T(8,128)(2,1)S(1)}, u32[]{:S(2)}, u32[]{:S(2)}) collective-permute-start(bf16[64,128]{1,0:T(8,128)(2,1)S(1)} %get-tuple-element.31), channel_id=1, source_target_pairs={{0,4},{1,5},{2,6},{3,7},{4,0},{5,1},{6,2},{7,3},{8,12},{9,13},{10,... | collective-permute-start | bytes 49160 | tf_op jit(solution)/shard_map/ppermute | solution.py:356
  97.0 4.7 %collective-permute-start.18 = (bf16[64,128]{1,0:T(8,128)(2,1)S(1)}, bf16[64,128]{1,0:T(8,128)(2,1)S(1)}, u32[]{:S(2)}, u32[]{:S(2)}) collective-permute-start(bf16[64,128]{1,0:T(8,128)(2,1)S(1)} %get-tuple-element.32), channel_id=1, source_target_pairs={{0,5},{1,4},{2,7},{3,6},{4,1},{5,0},{6,3},{7,2},{8,13},{9,12},{10,... | collective-permute-start | bytes 49160 | tf_op jit(solution)/shard_map/ppermute | solution.py:356
  98.5 3.4 %collective-permute-start.19 = (bf16[64,128]{1,0:T(8,128)(2,1)S(1)}, bf16[64,128]{1,0:T(8,128)(2,1)S(1)}, u32[]{:S(2)}, u32[]{:S(2)}) collective-permute-start(bf16[64,128]{1,0:T(8,128)(2,1)S(1)} %get-tuple-element.33), channel_id=1, source_target_pairs={{0,6},{1,7},{2,4},{3,5},{4,2},{5,3},{6,0},{7,1},{8,14},{9,15},{10,... | collective-permute-start | bytes 49160 | tf_op jit(solution)/shard_map/ppermute | solution.py:356
  99.0 4.1 %collective-permute-start.20 = (bf16[64,128]{1,0:T(8,128)(2,1)S(1)}, bf16[64,128]{1,0:T(8,128)(2,1)S(1)}, u32[]{:S(2)}, u32[]{:S(2)}) collective-permute-start(bf16[64,128]{1,0:T(8,128)(2,1)S(1)} %get-tuple-element.34), channel_id=1, source_target_pairs={{0,7},{1,6},{2,5},{3,4},{4,3},{5,2},{6,1},{7,0},{8,15},{9,14},{10,... | collective-permute-start | bytes 49160 | tf_op jit(solution)/shard_map/ppermute | solution.py:356

commit v2 on v1

--- a/solution.py
+++ b/solution.py
@@ -20,18 +20,22 @@
     return -(-value // step) * step
 
 
+def seat(inner, context_count):
+    return lax.axis_index("users") % inner * context_count + lax.axis_index("ctx")
+
+
 def grant(*arrays):
     held = sum(int(np.prod(a.shape)) * a.dtype.itemsize for a in arrays)
     return pltpu.CompilerParams(vmem_limit_bytes=min(60 << 20, 2 * held + (6 << 20)))
 
 
-def pick_columns(inner, context_count, head_width, context, matrix_ref, columns_ref):
+def pick_columns(inner, context_count, head_width, context, matrix_ref, columns_ref, skip=0):
     owner_count, _, picked = columns_ref.shape
     blocks = picked // head_width
-    width = matrix_ref.shape[1] // blocks
+    width = matrix_ref.shape[1] // (blocks + skip)
     for turn in range(inner):
         for block in range(blocks):
-            start = block * width + (turn * context_count + context) * head_width
+            start = (skip + block) * width + (turn * context_count + context) * head_width
             piece = matrix_ref[:, pl.ds(pl.multiple_of(start, head_width), head_width)]
             for first in range(0, owner_count, inner):
                 lanes = slice(block * head_width, (block + 1) * head_width)
@@ -41,7 +45,6 @@
 def prepare_kernel(
     inner,
     context_count,
-    context_ref,
     events_ref,
     owner_ref,
     bucket_ref,
@@ -62,23 +65,58 @@
     meta = jnp.where(lanes == 0, owners, jnp.where(lanes == 1, ranking, buckets))
     packed_ref[:, :width] = events_ref[...]
     packed_ref[:, width:] = jnp.where(lanes < 3, meta, 0.0).astype(jnp.bfloat16)
-    pick_columns(inner, context_count, head_width, context_ref[0], matrix_ref, columns_ref)
-
-
-def spread_columns_kernel(inner, context_count, head_width, context_ref, matrix_ref, columns_ref):
-    pick_columns(inner, context_count, head_width, context_ref[0], matrix_ref, columns_ref)
-
-
-def grant(*arrays):
-    held = sum(int(np.prod(a.shape)) * a.dtype.itemsize for a in arrays)
-    return pltpu.CompilerParams(vmem_limit_bytes=min(60 << 20, 2 * held + (6 << 20)))
-
-
-def cross_kernel(me_ref, *refs):
+    context = lax.axis_index("ctx")
+    pick_columns(inner, context_count, head_width, context, matrix_ref, columns_ref)
+
+
+def spread_columns_kernel(
+    inner, context_count, head_width, matrix_ref, columns_ref, *refs
+):
+    context, user = lax.axis_index("ctx"), lax.axis_index("users")
+    pick_columns(inner, context_count, head_width, context, matrix_ref, columns_ref, skip=1)
+    half = len(refs) // 2
+    for turn in range(half):
+        for own, ref in ((user, refs[turn]), (user ^ 1, refs[half + turn])):
+            seat = (own & (inner - 1)) ^ (2 * turn & (inner - 1))
+            start = (seat * context_count + context) * head_width
+            ref[...] = matrix_ref[:, pl.ds(pl.multiple_of(start, head_width), head_width)]
+
+
+def pair_kernel(*refs):
+    count = len(refs) // 3
+    rows = refs[0].shape[0]
+    mine = lax.axis_index("users") & 1
+    for turn in range(count):
+        out_ref = refs[2 * count + turn]
+        out_ref[pl.ds(pl.multiple_of(mine * rows, rows), rows), :] = refs[turn][...]
+        out_ref[pl.ds(pl.multiple_of((1 - mine) * rows, rows), rows), :] = refs[count + turn][...]
+
+
+def gate_kernel(inner, context_count, crossed_ref, *refs):
+    head_count = H
+    pieces = refs[: -head_count - 3]
+    outs = refs[-head_count - 3 : -3]
+    rows_ref, weights_ref, sem = refs[-3:]
+    copy = pltpu.make_async_copy(crossed_ref, rows_ref, sem)
+    copy.start()
+    me, pair = seat(inner, context_count), lax.axis_index("users") >> 1
+    depth = pieces[0].shape[0]
+    for far, piece in enumerate(pieces):
+        weights_ref[pl.ds(pl.multiple_of((pair ^ far) * depth, depth), depth), :] = piece[...]
+    copy.wait()
+    weights = weights_ref[...]
+    rows = outs[0].shape[0]
+    for mask in range(head_count):
+        source = pl.ds(pl.multiple_of((me ^ mask) * rows, rows), rows)
+        half = 0.5 * jnp.dot(rows_ref[source, :], weights, preferred_element_type=jnp.float32)
+        outs[mask][...] = (half * (1.0 + jnp.tanh(half))).astype(jnp.bfloat16)
+
+
+def cross_kernel(inner, context_count, *refs):
     head_count = H
     pieces = refs[:head_count]
     matrix_ref, bias_ref, crossed_ref, meta_ref = refs[head_count:]
-    me = me_ref[0]
+    me = seat(inner, context_count)
     rows = pieces[0].shape[0]
     width = bias_ref.shape[1]
     head_width = width // head_count
@@ -94,17 +132,20 @@
         meta_ref[target, :] = piece[:, width:]
 
 
-def project_kernel(slot_stride, kv_slots, chunk_users, me_ref, *refs):
+def project_kernel(inner, context_count, slot_stride, kv_slots, chunk_users, *refs):
     head_count = H
     pieces = refs[:head_count]
     matrix_ref, meta_ref, base_ref = refs[head_count : head_count + 3]
-    gate_refs = refs[head_count + 3 : 2 * head_count + 3]
-    out_ref, rows_ref, gate_ref, send_ref, sems = refs[2 * head_count + 3 :]
-    me = me_ref[0]
+    token_ref, far_rows_ref, out_ref, rows_ref, send_ref, sems = refs[head_count + 3 :]
+    token_ref[...] = jnp.zeros_like(token_ref)
+    me = seat(inner, context_count)
     head_width = pieces[0].shape[1]
     for mask in range(head_count):
         columns = pl.ds(pl.multiple_of((me ^ mask) * head_width, head_width), head_width)
         rows_ref[:, columns] = pieces[mask][...]
+    copy = pltpu.make_async_copy(rows_ref, far_rows_ref, sems.at[0])
+    copy.start()
+    started = [copy]
     meta = meta_ref[...]
     turned = meta.astype(jnp.float32).T
     owner = turned[0:1, :].astype(jnp.int32)
@@ -113,17 +154,10 @@
     labels = jnp.broadcast_to(meta[:, 2:3].astype(jnp.float32), meta.shape).astype(jnp.bfloat16)
     half = 0.5 * jnp.dot(rows_ref[...], matrix_ref[...], preferred_element_type=jnp.float32)
     activated = (half * (1.0 + jnp.tanh(half))).astype(jnp.bfloat16)
-    gate_ref[...] = activated[:, :head_width]
-    shard_rows = gate_refs[0].shape[0]
-    for mask in range(head_count):
-        source = pl.ds(pl.multiple_of((me ^ mask) * shard_rows, shard_rows), shard_rows)
-        gate_refs[mask][...] = gate_ref[source, :]
-    carried = jnp.concatenate([labels, activated[:, head_width:]], axis=1)
-    context_count = slot_stride // kv_slots
+    carried = jnp.concatenate([labels, activated], axis=1)
     user_count = send_ref.shape[0] // context_count
     chunk = chunk_users * slot_stride
     lane = lax.broadcasted_iota(jnp.int32, (8, head_width), 1)
-    started = []
     for turn, first in enumerate(range(0, user_count, chunk_users)):
         slots = lax.broadcasted_iota(jnp.int32, (chunk, slot_of_row.shape[1]), 0)
         picked = (slots + first * slot_stride == slot_of_row).astype(jnp.float32)
@@ -153,7 +187,7 @@
                     note = jnp.where(lane == tile, part[tile * 8 : tile * 8 + 8, :head_width], note)
                 send_ref[target, at : at + 8, :] = note.astype(jnp.bfloat16)
         done = pl.ds(first * context_count, chunk_users * context_count)
-        copy = pltpu.make_async_copy(send_ref.at[done], out_ref.at[done], sems.at[turn])
+        copy = pltpu.make_async_copy(send_ref.at[done], out_ref.at[done], sems.at[turn + 1])
         copy.start()
         started.append(copy)
     for copy in started:
@@ -161,7 +195,8 @@
 
 
 def stage_kernel(
-    live_ref,
+    capacity,
+    length_ref,
     after_ref,
     far_ref,
     bucket_ref,
@@ -185,9 +220,11 @@
         table, picked, precision=lax.Precision.HIGHEST, preferred_element_type=jnp.float32
     )
     positions = lax.broadcasted_iota(jnp.int32, bias.shape, 1)
-    cache_bias_ref[...] = jnp.where(positions < live_ref[0], 0.5 * bias, DEAD)
+    context = lax.axis_index("ctx")
+    live = length_ref[0] - context * bias.shape[1]
+    cache_bias_ref[...] = jnp.where(positions < live, 0.5 * bias, DEAD)
     near_time_bias_ref[...] = table
-    near_key_order_ref[...] = key_order_ref[...]
+    near_key_order_ref[...] = key_order_ref[...] + context * capacity
     near_query_order_ref[...] = query_order_ref[...]
     copy.wait()
 
@@ -294,11 +331,11 @@
         lax.fori_loop(0, block_count, step, 0)
 
 
-def finish_kernel(me_ref, place_ref, *refs):
+def finish_kernel(inner, context_count, place_ref, *refs):
     head_count = H
     gates = refs[:head_count]
     returned_ref, gain_ref, out_ref, tall_ref, gate_ref = refs[head_count:]
-    me = me_ref[0]
+    me = seat(inner, context_count)
     rows, width = out_ref.shape
     head_width = width // head_count
     for mask in range(head_count):
@@ -340,8 +377,6 @@
     device_count = owner_count * context_count
     inner = H // context_count
     group_count = owner_count // inner
-    user_index, context_index = lax.axis_index("users"), lax.axis_index("ctx")
-    me = (user_index % inner) * context_count + context_index
     capacity = max(2, (3 * row_count + 2 * owner_count - 1) // (2 * owner_count))
     kv_slots = round_up(inner * capacity, 8)
     slot_stride = context_count * kv_slots
@@ -372,49 +407,71 @@
     vmem_spec = pl.BlockSpec(memory_space=VMEM)
     smem_spec = pl.BlockSpec(memory_space=SMEM)
     hbm_spec = pl.BlockSpec(memory_space=pltpu.MemorySpace.HBM)
-    me_scalar = me.astype(jnp.int32).reshape(1)
-    context_scalar = context_index.astype(jnp.int32).reshape(1)
     packed_shape = jax.ShapeDtypeStruct((row_count, width + head_width), jnp.bfloat16)
     matrix_rows = cross_weight.shape[0]
     cross_shape = jax.ShapeDtypeStruct((owner_count, matrix_rows, head_width), jnp.bfloat16)
     packed, cross_columns = pl.pallas_call(
         functools.partial(prepare_kernel, inner, context_count),
         out_shape=(packed_shape, cross_shape),
-        in_specs=[smem_spec] + [vmem_spec] * 4,
+        in_specs=[vmem_spec] * 4,
         out_specs=(vmem_spec, vmem_spec),
         name="prepare",
-    )(context_scalar, events, owner_id.reshape(1, -1), event_bucket[None, :], cross_weight)
+    )(events, owner_id.reshape(1, -1), event_bucket[None, :], cross_weight)
     pieces = spread(packed)
     project_shape = jax.ShapeDtypeStruct(
-        (owner_count, matrix_rows, blocks * head_width), jnp.bfloat16
-    )
-    project_columns = pl.pallas_call(
+        (owner_count, matrix_rows, (blocks - 1) * head_width), jnp.bfloat16
+    )
+    gate_kinds = max(1, inner // 2)
+    gate_shape = jax.ShapeDtypeStruct((matrix_rows, head_width), jnp.bfloat16)
+    project_columns, *gate_columns = pl.pallas_call(
         functools.partial(spread_columns_kernel, inner, context_count, head_width),
-        out_shape=project_shape,
-        in_specs=[smem_spec, vmem_spec],
-        out_specs=vmem_spec,
+        out_shape=[project_shape] + [gate_shape] * (2 * gate_kinds),
+        in_specs=[vmem_spec],
+        out_specs=[vmem_spec] * (1 + 2 * gate_kinds),
         compiler_params=grant(project_shape),
         name="columns",
-    )(context_scalar, project_weight)
+    )(project_weight)
 
     cross_columns = lax.all_to_all(cross_columns, "users", split_axis=0, concat_axis=0, tiled=True)
     project_columns = lax.all_to_all(
         project_columns, "users", split_axis=0, concat_axis=0, tiled=True
     )
-    project_columns = project_columns.reshape(width, blocks * head_width)
+    project_columns = project_columns.reshape(width, (blocks - 1) * head_width)
     cross_columns = cross_columns.reshape(width, head_width)
 
+    def trade(block, mask):
+        pairs = [
+            (u * context_count + c, (u ^ mask) * context_count + c)
+            for u in range(owner_count)
+            for c in range(context_count)
+        ]
+        return lax.ppermute(block, AXES, pairs)
+
+    gate_other = [trade(block, 1) for block in gate_columns[gate_kinds:]]
+    gate_pairs = pl.pallas_call(
+        pair_kernel,
+        out_shape=[jax.ShapeDtypeStruct((2 * matrix_rows, head_width), jnp.bfloat16)]
+        * gate_kinds,
+        in_specs=[vmem_spec] * (2 * gate_kinds),
+        out_specs=[vmem_spec] * gate_kinds,
+        compiler_params=grant(project_shape),
+        name="pair",
+    )(*gate_columns[:gate_kinds], *gate_other)
+    gate_pieces = [gate_pairs[0]] + [
+        trade(gate_pairs[mask // 2 % gate_kinds], mask) for mask in range(2, owner_count, 2)
+    ]
+
     crossed, group_meta = pl.pallas_call(
-        cross_kernel,
+        functools.partial(cross_kernel, inner, context_count),
         out_shape=(
             jax.ShapeDtypeStruct((group_rows, head_width), jnp.bfloat16),
             jax.ShapeDtypeStruct((group_rows, head_width), jnp.bfloat16),
         ),
-        in_specs=[smem_spec] + [vmem_spec] * (H + 2),
+        in_specs=[vmem_spec] * (H + 2),
         out_specs=(vmem_spec, vmem_spec),
         compiler_params=grant(*pieces, cross_columns),
         name="cross",
-    )(me_scalar, *pieces, cross_columns, cross_bias[None, :])
+    )(*pieces, cross_columns, cross_bias[None, :])
     crossed_pieces = spread(crossed)
 
     shard = np.arange(group_rows) // row_count
@@ -424,21 +481,39 @@
     while owner_count % chunk_users:
         chunk_users -= 1
     messages = jax.ShapeDtypeStruct((device_count, message_rows, head_width), jnp.bfloat16)
-    *gates, outgoing = pl.pallas_call(
-        functools.partial(project_kernel, slot_stride, kv_slots, chunk_users),
-        out_shape=[jax.ShapeDtypeStruct((row_count, head_width), jnp.bfloat16)] * H
-        + [messages],
-        in_specs=[smem_spec] + [vmem_spec] * (H + 3),
-        out_specs=[vmem_spec] * H + [hbm_spec],
+    token, far_rows, outgoing = pl.pallas_call(
+        functools.partial(project_kernel, inner, context_count, slot_stride, kv_slots, chunk_users),
+        out_shape=[
+            jax.ShapeDtypeStruct((8, head_width), jnp.float32),
+            pltpu.MemorySpace.HBM((group_rows, width), jnp.bfloat16),
+            messages,
+        ],
+        in_specs=[vmem_spec] * (H + 3),
+        out_specs=[vmem_spec] + [hbm_spec] * 2,
         scratch_shapes=[
             pltpu.VMEM((group_rows, width), jnp.bfloat16),
-            pltpu.VMEM((group_rows, head_width), jnp.bfloat16),
             pltpu.VMEM(messages.shape, messages.dtype),
-            pltpu.SemaphoreType.DMA((owner_count // chunk_users,)),
+            pltpu.SemaphoreType.DMA((owner_count // chunk_users + 1,)),
         ],
         compiler_params=grant(*crossed_pieces, project_columns, messages, messages),
         name="project",
-    )(me_scalar, *crossed_pieces, project_columns, group_meta, jnp.asarray(base, jnp.int32))
+    )(*crossed_pieces, project_columns, group_meta, jnp.asarray(base, jnp.int32))
+    gates = pl.pallas_call(
+        functools.partial(gate_kernel, inner, context_count),
+        out_shape=[jax.ShapeDtypeStruct((row_count, head_width), jnp.bfloat16)] * H,
+        in_specs=[hbm_spec] + [vmem_spec] * len(gate_pieces),
+        out_specs=[vmem_spec] * H,
+        scratch_shapes=[
+            pltpu.VMEM((group_rows, width), jnp.bfloat16),
+            pltpu.VMEM((width, head_width), jnp.bfloat16),
+            pltpu.SemaphoreType.DMA(()),
+        ],
+        compiler_params=grant(far_rows),
+        name="gate",
+    )(
+        pltpu.with_memory_space_constraint(far_rows, pltpu.MemorySpace.HBM),
+        *gate_pieces,
+    )
     gates = [gates[0]] + [swap(gates[mask], mask) for mask in range(1, H)]
 
     arrived = lax.all_to_all(outgoing, AXES, split_axis=0, concat_axis=0, tiled=True)
@@ -451,22 +526,18 @@
     slots = np.arange(group_count * slot_stride)
     query_order = order_of(slots // slot_stride, slots % slot_stride // kv_slots, slots % kv_slots)
     slots = np.arange(group_count * kv_slots)
-    key_order = (
-        jnp.asarray(order_of(slots // kv_slots, 0, slots % kv_slots), jnp.int32)
-        + context_index * capacity
-    )
+    key_order = jnp.asarray(order_of(slots // kv_slots, 0, slots % kv_slots), jnp.int32)
     block_groups = max(1, min(group_count, 256 // slot_stride))
     while group_count % block_groups:
         block_groups -= 1
     block_rows = block_groups * slot_stride
-    live = (cache_length[0] - context_index * cache_rows).astype(jnp.int32).reshape(1)
     query_order = jnp.asarray(query_order, jnp.int32).reshape(-1, block_rows)
 
     def far(cache):
         return pltpu.with_memory_space_constraint(cache[0], pltpu.MemorySpace.HBM)
 
     near = pl.pallas_call(
-        stage_kernel,
+        functools.partial(stage_kernel, capacity),
         out_shape=(
             jax.ShapeDtypeStruct(cache_keys.shape[1:], cache_keys.dtype),
             jax.ShapeDtypeStruct((H, cache_rows), jnp.float32),
@@ -479,7 +550,15 @@
         scratch_shapes=[pltpu.SemaphoreType.DMA(())],
         compiler_params=grant(cache_keys),
         name="stage",
-    )(live, gates[0], far(cache_keys), cache_bucket, time_bias.T, key_order[:, None], query_order)
+    )(
+        cache_length,
+        token,
+        far(cache_keys),
+        cache_bucket,
+        time_bias.T,
+        key_order[:, None],
+        query_order,
+    )
 
     partials = pl.pallas_call(
         functools.partial(
@@ -502,9 +581,9 @@
     contexts = jnp.arange(context_count, dtype=jnp.int32)[None, :]
     places = (owners[:, None] * context_count + contexts) * capacity + ranking[:, None]
     return pl.pallas_call(
-        finish_kernel,
+        functools.partial(finish_kernel, inner, context_count),
         out_shape=jax.ShapeDtypeStruct((row_count, width), jnp.bfloat16),
-        in_specs=[smem_spec] * 2 + [vmem_spec] * (H + 2),
+        in_specs=[smem_spec] + [vmem_spec] * (H + 2),
         out_specs=vmem_spec,
         scratch_shapes=[
             pltpu.VMEM((row_count * H, head_width), jnp.float32),
@@ -513,7 +592,6 @@
         compiler_params=grant(returned, norm_gain),
         name="finish",
     )(
-        me_scalar,
         places,
         *gates,
         returned.reshape(device_count * capacity, H, head_width),

time: 108 us -> 124 us (1.15)
  starting transfers between devices: 35.7 us -> 45.9 us
  waiting for transfers between devices: 55.4 us -> 59 us
  Pallas kernels: 14.2 us -> 15.7 us
    ppermute x0 -> x9, starting transfers between devices: none -> 11.8 us  [trade(): return lax.ppermute(block, AXES, pairs)]
    ppermute x0 -> x9, waiting for transfers between devices: none -> 7.24 us  [trade(): return lax.ppermute(block, AXES, pairs)]
    all_to_all x1, waiting for transfers between devices: 2.4 us -> 0.01 us  [shards(): lax.all_to_all(partials, AXES, split_axis=0, concat_axis=0, tiled=True)]
    pallas_call x4 -> x6, Pallas kernels: 6.46 us -> 8.11 us  [the longest x1 2.32 us: shards(): pl.pallas_call(functools.partial(project_kernel, inner, context_count, sl...]
    ppermute x21, waiting for transfers between devices: 25.6 us -> 24.1 us  [swap(): return lax.ppermute(block, AXES, pairs)]
  transfers between devices with their start and end apart: 25 -> 34, of which waited for: 15 -> 18; matrix products, arithmetic and copies ran while one was open for 0% -> 0% of each run, Pallas kernels for 3% -> 4%
where the time goes in v2:
time: 124 us; the launch traced here: 123 us
  waiting for transfers between devices  59 us (48%)
  starting transfers between devices  45.9 us (37%)
  Pallas kernels  15.7 us (13%)
    ppermute x21, waiting for transfers between devices, swap(): return lax.ppermute(block, AXES, pairs)  24.1 us
    all_to_all x1, waiting for transfers between devices, shards(): lax.all_to_all(outgoing, AXES, split_axis=0, concat_axis=0, tiled=True)  19.7 us
    ppermute x21, starting transfers between devices, swap(): return lax.ppermute(block, AXES, pairs)  14.1 us
    ppermute x9, starting transfers between devices, trade(): return lax.ppermute(block, AXES, pairs)  11.8 us
    all_to_all x1, waiting for transfers between devices, shards(): lax.all_to_all(cross_columns, 'users', split_axis=0, concat_axis=0, tiled...  7.97 us
    all_to_all x1, starting transfers between devices, shards(): lax.all_to_all(cross_columns, 'users', split_axis=0, concat_axis=0, tiled...  7.52 us
    ppermute x9, waiting for transfers between devices, trade(): return lax.ppermute(block, AXES, pairs)  7.24 us
    all_to_all x1, starting transfers between devices, shards(): lax.all_to_all(outgoing, AXES, split_axis=0, concat_axis=0, tiled=True)  5.3 us
  transfers between devices with their start and end apart: 34, of which 18 were waited for; matrix products, arithmetic and copies ran while one was open for 0% of the time, Pallas kernels for 4%

profile of v2, /device:TPU:0, one launch (start us, length us, event | category | flops | bytes accessed | tf_op | source)
XLA Modules:
  0.0 122.8 jit_solution(7251677818903644093)
XLA Ops:
  0.0 1.9 %prepare.1 = (bf16[64,1152]{1,0:T(8,128)(2,1)}, bf16[16,64,128]{2,1,0:T(8,128)(2,1)}) custom-call(bf16[64,1024]{1,0:T(8,128)(2,1)} %events_ref.1, s32[1,64]{1,0:T(1,128)} %bitcast.24, s32[1,64]{1,0:T(1,128)} %bitcast.23, bf16[64,1024]{1,0:T(8,128)(2,1)} %matrix_ref.2), custom_call_target="tpu_custom_call" | custom-call | tf_op jit(solution)/shard_map/prepare/pallas_call | solution.py:413
  2.0 7.5 %all-to-all-start = ((bf16[16,64,128]{2,1,0:T(8,128)(2,1)}), bf16[16,64,128]{2,1,0:T(8,128)(2,1)S(1)}, u32[]{:S(2)}, u32[]{:S(2)}) async-start(bf16[16,64,128]{2,1,0:T(8,128)(2,1)} %get-tuple-element.33), calls=%async_computation | async-start | bytes 524288 | tf_op jit(solution)/shard_map/all_to_all | solution.py:435
  9.5 1.0 copy-done
  10.5 1.0 columns.1
  11.5 8.0 %all-to-all-done = bf16[16,64,128]{2,1,0:T(8,128)(2,1)S(1)} async-done(((bf16[16,64,128]{2,1,0:T(8,128)(2,1)}), bf16[16,64,128]{2,1,0:T(8,128)(2,1)S(1)}, u32[]{:S(2)}, u32[]{:S(2)}) %all-to-all-start) | async-done | bytes 262176 | tf_op jit(solution)/shard_map/all_to_all | solution.py:435
  19.5 3.6 %all-to-all-start.1 = ((bf16[16,64,384]{2,1,0:T(8,128)(2,1)}), bf16[16,64,384]{2,1,0:T(8,128)(2,1)S(1)}, u32[]{:S(2)}, u32[]{:S(2)}) async-start(bf16[16,64,384]{2,1,0:T(8,128)(2,1)} %get-tuple-element.35), calls=%async_computation.1 | async-start | bytes 1572864 | tf_op jit(solution)/shard_map/all_to_all | solution.py:436
  23.1 1.6 %collective-permute-start = (bf16[64,1152]{1,0:T(8,128)(2,1)S(1)}, bf16[64,1152]{1,0:T(8,128)(2,1)S(1)}, u32[]{:S(2)}, u32[]{:S(2)}) collective-permute-start(bf16[64,1152]{1,0:T(8,128)(2,1)S(1)} %copy-done.1), channel_id=1, source_target_pairs={{0,1},{1,0},{2,3},{3,2},{4,5},{5,4},{6,7},{7,6},{8,9},{9,8},{10,11... | collective-permute-start | bytes 442376 | tf_op jit(solution)/shard_map/ppermute | solution.py:391
  24.7 1.8 %collective-permute-start.3 = (bf16[64,1152]{1,0:T(8,128)(2,1)S(1)}, bf16[64,1152]{1,0:T(8,128)(2,1)S(1)}, u32[]{:S(2)}, u32[]{:S(2)}) collective-permute-start(bf16[64,1152]{1,0:T(8,128)(2,1)S(1)} %copy-done.1), channel_id=1, source_target_pairs={{0,4},{1,5},{2,6},{3,7},{4,0},{5,1},{6,2},{7,3},{8,12},{9,13},{10,... | collective-permute-start | bytes 442376 | tf_op jit(solution)/shard_map/ppermute | solution.py:391
  26.7 2.5 %collective-permute-done.refs_1_ = bf16[64,1152]{1,0:T(8,128)(2,1)S(1)} collective-permute-done((bf16[64,1152]{1,0:T(8,128)(2,1)S(1)}, bf16[64,1152]{1,0:T(8,128)(2,1)S(1)}, u32[]{:S(2)}, u32[]{:S(2)}) %collective-permute-start) | collective-permute-done | bytes 147488 | tf_op jit(solution)/shard_map/ppermute | solution.py:391
  29.2 6.9 %collective-permute-done.3.refs_4_ = bf16[64,1152]{1,0:T(8,128)(2,1)S(1)} collective-permute-done((bf16[64,1152]{1,0:T(8,128)(2,1)S(1)}, bf16[64,1152]{1,0:T(8,128)(2,1)S(1)}, u32[]{:S(2)}, u32[]{:S(2)}) %collective-permute-start.3) | collective-permute-done | bytes 147488 | tf_op jit(solution)/shard_map/ppermute | solution.py:391
  36.1 3.5 %collective-permute-done.4.refs_5_ = bf16[64,1152]{1,0:T(8,128)(2,1)S(1)} collective-permute-done((bf16[64,1152]{1,0:T(8,128)(2,1)S(1)}, bf16[64,1152]{1,0:T(8,128)(2,1)S(1)}, u32[]{:S(2)}, u32[]{:S(2)}) %collective-permute-start.4) | collective-permute-done | bytes 147488 | tf_op jit(solution)/shard_map/ppermute | solution.py:391
  39.7 1.3 %collective-permute-done.6.refs_7_ = bf16[64,1152]{1,0:T(8,128)(2,1)S(1)} collective-permute-done((bf16[64,1152]{1,0:T(8,128)(2,1)S(1)}, bf16[64,1152]{1,0:T(8,128)(2,1)S(1)}, u32[]{:S(2)}, u32[]{:S(2)}) %collective-permute-start.6) | collective-permute-done | bytes 147488 | tf_op jit(solution)/shard_map/ppermute | solution.py:391
  41.1 0.4 cross.1
  41.6 0.6 collective-permute-start.7
  42.1 1.5 %collective-permute-start.10 = (bf16[512,128]{1,0:T(8,128)(2,1)S(1)}, bf16[512,128]{1,0:T(8,128)(2,1)S(1)}, u32[]{:S(2)}, u32[]{:S(2)}) collective-permute-start(bf16[512,128]{1,0:T(8,128)(2,1)S(1)} %get-tuple-element.34.refs_0_), channel_id=1, source_target_pairs={{0,4},{1,5},{2,6},{3,7},{4,0},{5,1},{6,2},{7,3},{8,12},{9,13},{10,... | collective-permute-start | bytes 393224 | tf_op jit(solution)/shard_map/ppermute | solution.py:391
  43.7 1.4 %collective-permute-start.11 = (bf16[512,128]{1,0:T(8,128)(2,1)S(1)}, bf16[512,128]{1,0:T(8,128)(2,1)S(1)}, u32[]{:S(2)}, u32[]{:S(2)}) collective-permute-start(bf16[512,128]{1,0:T(8,128)(2,1)S(1)} %get-tuple-element.34.refs_0_), channel_id=1, source_target_pairs={{0,5},{1,4},{2,7},{3,6},{4,1},{5,0},{6,3},{7,2},{8,13},{9,12},{10,... | collective-permute-start | bytes 393224 | tf_op jit(solution)/shard_map/ppermute | solution.py:391
  45.1 2.1 %collective-permute-done.7.refs_1_ = bf16[512,128]{1,0:T(8,128)(2,1)S(1)} collective-permute-done((bf16[512,128]{1,0:T(8,128)(2,1)S(1)}, bf16[512,128]{1,0:T(8,128)(2,1)S(1)}, u32[]{:S(2)}, u32[]{:S(2)}) %collective-permute-start.7) | collective-permute-done | bytes 131104 | tf_op jit(solution)/shard_map/ppermute | solution.py:391
  47.2 0.9 collective-permute-done.10.refs_4_
  48.1 3.1 %collective-permute-done.11.refs_5_ = bf16[512,128]{1,0:T(8,128)(2,1)S(1)} collective-permute-done((bf16[512,128]{1,0:T(8,128)(2,1)S(1)}, bf16[512,128]{1,0:T(8,128)(2,1)S(1)}, u32[]{:S(2)}, u32[]{:S(2)}) %collective-permute-start.11) | collective-permute-done | bytes 131104 | tf_op jit(solution)/shard_map/ppermute | solution.py:391
  51.2 1.3 %collective-permute-done.13.refs_7_ = bf16[512,128]{1,0:T(8,128)(2,1)S(1)} collective-permute-done((bf16[512,128]{1,0:T(8,128)(2,1)S(1)}, bf16[512,128]{1,0:T(8,128)(2,1)S(1)}, u32[]{:S(2)}, u32[]{:S(2)}) %collective-permute-start.13) | collective-permute-done | bytes 131104 | tf_op jit(solution)/shard_map/ppermute | solution.py:391
  52.5 2.3 %project.1 = (f32[8,128]{1,0:T(8,128)S(1)}, bf16[512,1024]{1,0:T(8,128)(2,1)}, bf16[32,104,128]{2,1,0:T(8,128)(2,1)}) custom-call(bf16[512,128]{1,0:T(8,128)(2,1)S(1)} %get-tuple-element.34.refs_0_, bf16[512,128]{1,0:T(8,128)(2,1)S(1)} %collective-permute-done.7.refs_1_, bf16[512,128]{1,0:T(8,128)(2,1)S(1)} %collective-permute-done.8.refs_2_, ...), custom_call_target="tpu_custom_call" | custom-call | tf_op jit(solution)/shard_map/project/pallas_call | solution.py:484
  54.8 5.3 %all-to-all-start.2 = ((bf16[32,104,128]{2,1,0:T(8,128)(2,1)}), bf16[32,104,128]{2,1,0:T(8,128)(2,1)S(1)}, u32[]{:S(2)}, u32[]{:S(2)}) async-start(bf16[32,104,128]{2,1,0:T(8,128)(2,1)} %get-tuple-element.52), calls=%async_computation.2 | async-start | bytes 1703936 | tf_op jit(solution)/shard_map/all_to_all | solution.py:519
  60.8 1.6 %stage.1 = (bf16[1024,1024]{1,0:T(8,128)(2,1)S(1)}, f32[8,1024]{1,0:T(8,128)S(1)}, f32[8,32]{1,0:T(8,128)S(1)}, s32[96,1]{1,0:T(8,128)S(1)}, s32[1,192]{1,0:T(1,128)S(1)}) custom-call(s32[1]{0:T(128)S(6)} %copy.17.length_ref, f32[8,128]{1,0:T(8,128)S(1)} %get-tuple-element.53.after_ref, bf16[1024,1024]{1,0:T(8,128)(2,1)} %bitcast.21, ...), custom_call_target="tpu_custom_call" | custom-call | tf_op jit(solution)/shard_map/stage/pallas_call | solution.py:539
  62.5 19.7 %all-to-all-done.2 = bf16[32,104,128]{2,1,0:T(8,128)(2,1)S(1)} async-done(((bf16[32,104,128]{2,1,0:T(8,128)(2,1)}), bf16[32,104,128]{2,1,0:T(8,128)(2,1)S(1)}, u32[]{:S(2)}, u32[]{:S(2)}) %all-to-all-start.2) | async-done | bytes 852000 | tf_op jit(solution)/shard_map/all_to_all | solution.py:519
  82.1 4.6 %attend.1 = bf16[32,48,128]{2,1,0:T(8,128)(2,1)} custom-call(bf16[4,8,104,128]{3,2,1,0:T(8,128)(2,1)S(1)} %bitcast.14, bf16[1024,1024]{1,0:T(8,128)(2,1)S(1)} %get-tuple-element.54.keys_ref, bf16[1024,1024]{1,0:T(8,128)(2,1)} %bitcast.22, f32[8,1024]{1,0:T(8,128)S(1)} %get-tuple-element.55.cache_bias_ref, f32[8,32]{1,0:T(8,128)S(1)} %get-tuple-element.56.time_bias_ref, ...), custom_call_target="tpu_custom_call" | custom-call | tf_op jit(solution)/shard_map/attend/pallas_call | solution.py:563
  86.8 3.6 %all-to-all-start.3 = ((bf16[32,48,128]{2,1,0:T(8,128)(2,1)}), bf16[32,48,128]{2,1,0:T(8,128)(2,1)S(1)}, u32[]{:S(2)}, u32[]{:S(2)}) async-start(bf16[32,48,128]{2,1,0:T(8,128)(2,1)} %attend.1), calls=%async_computation.3 | async-start | bytes 786432 | tf_op jit(solution)/shard_map/all_to_all | solution.py:580
  90.4 0.3 collective-permute-start.14
  91.0 0.7 collective-permute-done.14.refs_2_
  91.9 1.7 %collective-permute-start.16 = (bf16[128,128]{1,0:T(8,128)(2,1)S(1)}, bf16[128,128]{1,0:T(8,128)(2,1)S(1)}, u32[]{:S(2)}, u32[]{:S(2)}) collective-permute-start(bf16[128,128]{1,0:T(8,128)(2,1)S(1)} %get-tuple-element.43), channel_id=1, source_target_pairs={{0,4},{1,5},{2,6},{3,7},{4,0},{5,1},{6,2},{7,3},{8,12},{9,13},{10,... | collective-permute-start | bytes 98312 | tf_op jit(solution)/shard_map/ppermute | solution.py:448
  93.7 1.5 %collective-permute-start.17 = (bf16[128,128]{1,0:T(8,128)(2,1)S(1)}, bf16[128,128]{1,0:T(8,128)(2,1)S(1)}, u32[]{:S(2)}, u32[]{:S(2)}) collective-permute-start(bf16[128,128]{1,0:T(8,128)(2,1)S(1)} %get-tuple-element.42.refs_0_), channel_id=1, source_target_pairs={{0,8},{1,9},{2,10},{3,11},{4,12},{5,13},{6,14},{7,15},{8,0},{9,1},... | collective-permute-start | bytes 98312 | tf_op jit(solution)/shard_map/ppermute | solution.py:448
  95.2 0.3 collective-permute-start.18
  95.5 2.6 %collective-permute-start.19 = (bf16[128,128]{1,0:T(8,128)(2,1)S(1)}, bf16[128,128]{1,0:T(8,128)(2,1)S(1)}, u32[]{:S(2)}, u32[]{:S(2)}) collective-permute-start(bf16[128,128]{1,0:T(8,128)(2,1)S(1)} %get-tuple-element.42.refs_0_), channel_id=1, source_target_pairs={{0,16},{1,17},{2,18},{3,19},{4,20},{5,21},{6,22},{7,23},{8,24},{9,... | collective-permute-start | bytes 98312 | tf_op jit(solution)/shard_map/ppermute | solution.py:448
  98.1 1.5 %collective-permute-start.20 = (bf16[128,128]{1,0:T(8,128)(2,1)S(1)}, bf16[128,128]{1,0:T(8,128)(2,1)S(1)}, u32[]{:S(2)}, u32[]{:S(2)}) collective-permute-start(bf16[128,128]{1,0:T(8,128)(2,1)S(1)} %get-tuple-element.43), channel_id=1, source_target_pairs={{0,20},{1,21},{2,22},{3,23},{4,16},{5,17},{6,18},{7,19},{8,28},{9,... | collective-permute-start | bytes 98312 | tf_op jit(solution)/shard_map/ppermute | solution.py:448
  99.5 3.3 %collective-permute-start.21 = (bf16[128,128]{1,0:T(8,128)(2,1)S(1)}, bf16[128,128]{1,0:T(8,128)(2,1)S(1)}, u32[]{:S(2)}, u32[]{:S(2)}) collective-permute-start(bf16[128,128]{1,0:T(8,128)(2,1)S(1)} %get-tuple-element.42.refs_0_), channel_id=1, source_target_pairs={{0,24},{1,25},{2,26},{3,27},{4,28},{5,29},{6,30},{7,31},{8,16},{9,... | collective-permute-start | bytes 98312 | tf_op jit(solution)/shard_map/ppermute | solution.py:448
  102.9 0.3 collective-permute-start.22
  103.2 2.8 %collective-permute-done.19.refs_4_ = bf16[128,128]{1,0:T(8,128)(2,1)S(1)} collective-permute-done((bf16[128,128]{1,0:T(8,128)(2,1)S(1)}, bf16[128,128]{1,0:T(8,128)(2,1)S(1)}, u32[]{:S(2)}, u32[]{:S(2)}) %collective-permute-start.19) | collective-permute-done | bytes 32800 | tf_op jit(solution)/shard_map/ppermute | solution.py:448
  106.0 1.9 %collective-permute-done.20.refs_5_ = bf16[128,128]{1,0:T(8,128)(2,1)S(1)} collective-permute-done((bf16[128,128]{1,0:T(8,128)(2,1)S(1)}, bf16[128,128]{1,0:T(8,128)(2,1)S(1)}, u32[]{:S(2)}, u32[]{:S(2)}) %collective-permute-start.20) | collective-permute-done | bytes 32800 | tf_op jit(solution)/shard_map/ppermute | solution.py:448
  107.9 1.6 %collective-permute-done.22.refs_7_ = bf16[128,128]{1,0:T(8,128)(2,1)S(1)} collective-permute-done((bf16[128,128]{1,0:T(8,128)(2,1)S(1)}, bf16[128,128]{1,0:T(8,128)(2,1)S(1)}, u32[]{:S(2)}, u32[]{:S(2)}) %collective-permute-start.22) | collective-permute-done | bytes 32800 | tf_op jit(solution)/shard_map/ppermute | solution.py:448
  109.5 1.7 %gate.1 = (bf16[64,128]{1,0:T(8,128)(2,1)S(1)}, bf16[64,128]{1,0:T(8,128)(2,1)S(1)}, bf16[64,128]{1,0:T(8,128)(2,1)S(1)}, bf16[64,128]{1,0:T(8,128)(2,1)S(1)}, b...) custom-call(bf16[512,1024]{1,0:T(8,128)(2,1)} %get-tuple-element.37., ...), custom_call_target="tpu_custom_call" | custom-call | tf_op jit(solution)/shard_map/gate/pallas_call | solution.py:501
  111.2 1.6 %collective-permute-start.23 = (bf16[64,128]{1,0:T(8,128)(2,1)S(1)}, bf16[64,128]{1,0:T(8,128)(2,1)S(1)}, u32[]{:S(2)}, u32[]{:S(2)}) collective-permute-start(bf16[64,128]{1,0:T(8,128)(2,1)S(1)} %get-tuple-element.45), channel_id=1, source_target_pairs={{0,1},{1,0},{2,3},{3,2},{4,5},{5,4},{6,7},{7,6},{8,9},{9,8},{10,11... | collective-permute-start | bytes 49160 | tf_op jit(solution)/shard_map/ppermute | solution.py:391
  112.9 0.7 collective-permute-start.25
  113.6 0.5 collective-permute-start.26
  114.2 2.4 %collective-permute-start.27 = (bf16[64,128]{1,0:T(8,128)(2,1)S(1)}, bf16[64,128]{1,0:T(8,128)(2,1)S(1)}, u32[]{:S(2)}, u32[]{:S(2)}) collective-permute-start(bf16[64,128]{1,0:T(8,128)(2,1)S(1)} %get-tuple-element.49), channel_id=1, source_target_pairs={{0,5},{1,4},{2,7},{3,6},{4,1},{5,0},{6,3},{7,2},{8,13},{9,12},{10,... | collective-permute-start | bytes 49160 | tf_op jit(solution)/shard_map/ppermute | solution.py:391
  116.6 1.7 %collective-permute-start.29 = (bf16[64,128]{1,0:T(8,128)(2,1)S(1)}, bf16[64,128]{1,0:T(8,128)(2,1)S(1)}, u32[]{:S(2)}, u32[]{:S(2)}) collective-permute-start(bf16[64,128]{1,0:T(8,128)(2,1)S(1)} %get-tuple-element.51), channel_id=1, source_target_pairs={{0,7},{1,6},{2,5},{3,4},{4,3},{5,2},{6,1},{7,0},{8,15},{9,14},{10,... | collective-permute-start | bytes 49160 | tf_op jit(solution)/shard_map/ppermute | solution.py:391
  118.4 0.4 collective-permute-done.27.refs_5_
  118.8 0.9 collective-permute-done.28.refs_6_
  119.8 1.0 collective-permute-done.29.refs_7_
  120.7 2.1 %finish.1 = bf16[64,1024]{1,0:T(8,128)(2,1)} custom-call(s32[64,2]{1,0:T(8,128)S(1)} %multiply_add_fusion.place_ref, bf16[64,128]{1,0:T(8,128)(2,1)S(1)} %get-tuple-element.44.refs_0_, bf16[64,128]{1,0:T(8,128)(2,1)S(1)} %collective-permute-done.23.refs_1_, bf16[64,128]{1,0:T(8,128)(2,1)S(1)} %collective-permute-done.24.refs_2_, ...), custom_call_target="tpu_custom_call" | custom-call | tf_op jit(solution)/shard_map/finish/pallas_call | solution.py:583
  (52 shorter events, 1.1 us)
Async XLA Ops:
  0.0 41.1 %copy-start.3 = (f32[1024]{0:T(1024)S(1)}, f32[1024]{0:T(1024)}, u32[]{:S(2)}) copy-start(f32[1024]{0:T(1024)} %param.19) | copy-start | bytes 12292
  1.9 21.2 %copy-start.1 = (bf16[64,1152]{1,0:T(8,128)(2,1)S(1)}, bf16[64,1152]{1,0:T(8,128)(2,1)}, u32[]{:S(2)}) copy-start(bf16[64,1152]{1,0:T(8,128)(2,1)} %get-tuple-element.32.refs_0_) | copy-start | bytes 442372
  1.9 50.6 %copy-start.7 = (s32[1,512]{1,0:T(1,128)S(1)}, s32[1,512]{1,0:T(1,128)}, u32[]{:S(2)}) copy-start(s32[1,512]{1,0:T(1,128)} %constant.12.clone.refs_10_) | copy-start | bytes 6148
  2.0 17.5 %all-to-all-start = ((bf16[16,64,128]{2,1,0:T(8,128)(2,1)}), bf16[16,64,128]{2,1,0:T(8,128)(2,1)S(1)}, u32[]{:S(2)}, u32[]{:S(2)}) async-start(bf16[16,64,128]{2,1,0:T(8,128)(2,1)} %get-tuple-element.33), calls=%async_computation | async-start | bytes 524288 | tf_op jit(solution)/shard_map/all_to_all | solution.py:435
  9.5 1.0 copy-start
  19.5 33.0 %all-to-all-start.1 = ((bf16[16,64,384]{2,1,0:T(8,128)(2,1)}), bf16[16,64,384]{2,1,0:T(8,128)(2,1)S(1)}, u32[]{:S(2)}, u32[]{:S(2)}) async-start(bf16[16,64,384]{2,1,0:T(8,128)(2,1)} %get-tuple-element.35), calls=%async_computation.1 | async-start | bytes 1572864 | tf_op jit(solution)/shard_map/all_to_all | solution.py:436
  23.1 6.1 %collective-permute-start = (bf16[64,1152]{1,0:T(8,128)(2,1)S(1)}, bf16[64,1152]{1,0:T(8,128)(2,1)S(1)}, u32[]{:S(2)}, u32[]{:S(2)}) collective-permute-start(bf16[64,1152]{1,0:T(8,128)(2,1)S(1)} %copy-done.1), channel_id=1, source_target_pairs={{0,1},{1,0},{2,3},{3,2},{4,5},{5,4},{6,7},{7,6},{8,9},{9,8},{10,11... | collective-permute-start | bytes 442376 | tf_op jit(solution)/shard_map/ppermute | solution.py:391
  24.7 11.4 %collective-permute-start.3 = (bf16[64,1152]{1,0:T(8,128)(2,1)S(1)}, bf16[64,1152]{1,0:T(8,128)(2,1)S(1)}, u32[]{:S(2)}, u32[]{:S(2)}) collective-permute-start(bf16[64,1152]{1,0:T(8,128)(2,1)S(1)} %copy-done.1), channel_id=1, source_target_pairs={{0,4},{1,5},{2,6},{3,7},{4,0},{5,1},{6,2},{7,3},{8,12},{9,13},{10,... | collective-permute-start | bytes 442376 | tf_op jit(solution)/shard_map/ppermute | solution.py:391
  26.5 13.2 %collective-permute-start.4 = (bf16[64,1152]{1,0:T(8,128)(2,1)S(1)}, bf16[64,1152]{1,0:T(8,128)(2,1)S(1)}, u32[]{:S(2)}, u32[]{:S(2)}) collective-permute-start(bf16[64,1152]{1,0:T(8,128)(2,1)S(1)} %copy-done.1), channel_id=1, source_target_pairs={{0,5},{1,4},{2,7},{3,6},{4,1},{5,0},{6,3},{7,2},{8,13},{9,12},{10,... | collective-permute-start | bytes 442376 | tf_op jit(solution)/shard_map/ppermute | solution.py:391
  26.7 13.0 %collective-permute-start.1 = (bf16[64,1152]{1,0:T(8,128)(2,1)S(1)}, bf16[64,1152]{1,0:T(8,128)(2,1)S(1)}, u32[]{:S(2)}, u32[]{:S(2)}) collective-permute-start(bf16[64,1152]{1,0:T(8,128)(2,1)S(1)} %copy-done.1), channel_id=1, source_target_pairs={{0,2},{1,3},{2,0},{3,1},{4,6},{5,7},{6,4},{7,5},{8,10},{9,11},{10,... | collective-permute-start | bytes 442376 | tf_op jit(solution)/shard_map/ppermute | solution.py:391
  29.2 10.5 %collective-permute-start.2 = (bf16[64,1152]{1,0:T(8,128)(2,1)S(1)}, bf16[64,1152]{1,0:T(8,128)(2,1)S(1)}, u32[]{:S(2)}, u32[]{:S(2)}) collective-permute-start(bf16[64,1152]{1,0:T(8,128)(2,1)S(1)} %collective-permute-done.refs_1_), channel_id=1, source_target_pairs={{0,2},{1,3},{2,0},{3,1},{4,6},{5,7},{6,4},{7,5},{8,10},{9,11},{10,... | collective-permute-start | bytes 442376 | tf_op jit(solution)/shard_map/ppermute | solution.py:391
  36.1 3.6 %collective-permute-start.5 = (bf16[64,1152]{1,0:T(8,128)(2,1)S(1)}, bf16[64,1152]{1,0:T(8,128)(2,1)S(1)}, u32[]{:S(2)}, u32[]{:S(2)}) collective-permute-start(bf16[64,1152]{1,0:T(8,128)(2,1)S(1)} %collective-permute-done.3.refs_4_), channel_id=1, source_target_pairs={{0,2},{1,3},{2,0},{3,1},{4,6},{5,7},{6,4},{7,5},{8,10},{9,11},{10,... | collective-permute-start | bytes 442376 | tf_op jit(solution)/shard_map/ppermute | solution.py:391
  39.7 1.4 %collective-permute-start.6 = (bf16[64,1152]{1,0:T(8,128)(2,1)S(1)}, bf16[64,1152]{1,0:T(8,128)(2,1)S(1)}, u32[]{:S(2)}, u32[]{:S(2)}) collective-permute-start(bf16[64,1152]{1,0:T(8,128)(2,1)S(1)} %collective-permute-done.4.refs_5_), channel_id=1, source_target_pairs={{0,2},{1,3},{2,0},{3,1},{4,6},{5,7},{6,4},{7,5},{8,10},{9,11},{10,... | collective-permute-start | bytes 442376 | tf_op jit(solution)/shard_map/ppermute | solution.py:391
  41.5 19.3 %copy-start.2 = (s32[96,1]{1,0:T(8,128)S(1)}, s32[96,1]{1,0:T(8,128)}, u32[]{:S(2)}) copy-start(s32[96,1]{1,0:T(8,128)} %constant.19.key_order_ref) | copy-start | bytes 1156
  41.5 19.3 %copy-start.4 = (s32[1,1024]{1,0:T(1,128)S(1)}, s32[1,1024]{1,0:T(1,128)}, u32[]{:S(2)}) copy-start(s32[1,1024]{1,0:T(1,128)} %bucket_ref.1) | copy-start | bytes 12292
  41.5 19.3 %copy-start.5 = (f32[32,8]{0,1:T(8,128)S(1)}, f32[32,8]{0,1:T(8,128)}, u32[]{:S(2)}) copy-start(f32[32,8]{0,1:T(8,128)} %param.25) | copy-start | bytes 3076
  41.5 19.3 %copy-start.8 = (s32[1,192]{1,0:T(1,128)S(1)}, s32[1,192]{1,0:T(1,128)}, u32[]{:S(2)}) copy-start(s32[1,192]{1,0:T(1,128)} %constant.20.query_order_ref) | copy-start | bytes 2308
  41.6 5.6 %collective-permute-start.7 = (bf16[512,128]{1,0:T(8,128)(2,1)S(1)}, bf16[512,128]{1,0:T(8,128)(2,1)S(1)}, u32[]{:S(2)}, u32[]{:S(2)}) collective-permute-start(bf16[512,128]{1,0:T(8,128)(2,1)S(1)} %get-tuple-element.34.refs_0_), channel_id=1, source_target_pairs={{0,1},{1,0},{2,3},{3,2},{4,5},{5,4},{6,7},{7,6},{8,9},{9,8},{10,11... | collective-permute-start | bytes 393224 | tf_op jit(solution)/shard_map/ppermute | solution.py:391
  42.1 6.0 %collective-permute-start.10 = (bf16[512,128]{1,0:T(8,128)(2,1)S(1)}, bf16[512,128]{1,0:T(8,128)(2,1)S(1)}, u32[]{:S(2)}, u32[]{:S(2)}) collective-permute-start(bf16[512,128]{1,0:T(8,128)(2,1)S(1)} %get-tuple-element.34.refs_0_), channel_id=1, source_target_pairs={{0,4},{1,5},{2,6},{3,7},{4,0},{5,1},{6,2},{7,3},{8,12},{9,13},{10,... | collective-permute-start | bytes 393224 | tf_op jit(solution)/shard_map/ppermute | solution.py:391
  43.7 7.5 %collective-permute-start.11 = (bf16[512,128]{1,0:T(8,128)(2,1)S(1)}, bf16[512,128]{1,0:T(8,128)(2,1)S(1)}, u32[]{:S(2)}, u32[]{:S(2)}) collective-permute-start(bf16[512,128]{1,0:T(8,128)(2,1)S(1)} %get-tuple-element.34.refs_0_), channel_id=1, source_target_pairs={{0,5},{1,4},{2,7},{3,6},{4,1},{5,0},{6,3},{7,2},{8,13},{9,12},{10,... | collective-permute-start | bytes 393224 | tf_op jit(solution)/shard_map/ppermute | solution.py:391
  45.1 6.1 %collective-permute-start.8 = (bf16[512,128]{1,0:T(8,128)(2,1)S(1)}, bf16[512,128]{1,0:T(8,128)(2,1)S(1)}, u32[]{:S(2)}, u32[]{:S(2)}) collective-permute-start(bf16[512,128]{1,0:T(8,128)(2,1)S(1)} %get-tuple-element.34.refs_0_), channel_id=1, source_target_pairs={{0,2},{1,3},{2,0},{3,1},{4,6},{5,7},{6,4},{7,5},{8,10},{9,11},{10,... | collective-permute-start | bytes 393224 | tf_op jit(solution)/shard_map/ppermute | solution.py:391
  47.2 4.0 %collective-permute-start.9 = (bf16[512,128]{1,0:T(8,128)(2,1)S(1)}, bf16[512,128]{1,0:T(8,128)(2,1)S(1)}, u32[]{:S(2)}, u32[]{:S(2)}) collective-permute-start(bf16[512,128]{1,0:T(8,128)(2,1)S(1)} %collective-permute-done.7.refs_1_), channel_id=1, source_target_pairs={{0,2},{1,3},{2,0},{3,1},{4,6},{5,7},{6,4},{7,5},{8,10},{9,11},{10,... | collective-permute-start | bytes 393224 | tf_op jit(solution)/shard_map/ppermute | solution.py:391
  48.1 3.1 %collective-permute-start.12 = (bf16[512,128]{1,0:T(8,128)(2,1)S(1)}, bf16[512,128]{1,0:T(8,128)(2,1)S(1)}, u32[]{:S(2)}, u32[]{:S(2)}) collective-permute-start(bf16[512,128]{1,0:T(8,128)(2,1)S(1)} %collective-permute-done.10.refs_4_), channel_id=1, source_target_pairs={{0,2},{1,3},{2,0},{3,1},{4,6},{5,7},{6,4},{7,5},{8,10},{9,11},{10,... | collective-permute-start | bytes 393224 | tf_op jit(solution)/shard_map/ppermute | solution.py:391
  51.2 1.3 %collective-permute-start.13 = (bf16[512,128]{1,0:T(8,128)(2,1)S(1)}, bf16[512,128]{1,0:T(8,128)(2,1)S(1)}, u32[]{:S(2)}, u32[]{:S(2)}) collective-permute-start(bf16[512,128]{1,0:T(8,128)(2,1)S(1)} %collective-permute-done.11.refs_5_), channel_id=1, source_target_pairs={{0,2},{1,3},{2,0},{3,1},{4,6},{5,7},{6,4},{7,5},{8,10},{9,11},{10,... | collective-permute-start | bytes 393224 | tf_op jit(solution)/shard_map/ppermute | solution.py:391
  54.8 27.3 %all-to-all-start.2 = ((bf16[32,104,128]{2,1,0:T(8,128)(2,1)}), bf16[32,104,128]{2,1,0:T(8,128)(2,1)S(1)}, u32[]{:S(2)}, u32[]{:S(2)}) async-start(bf16[32,104,128]{2,1,0:T(8,128)(2,1)} %get-tuple-element.52), calls=%async_computation.2 | async-start | bytes 1703936 | tf_op jit(solution)/shard_map/all_to_all | solution.py:519
  82.1 21.0 %copy-start.9 = (s32[64,1]{0,1:T(1,128)S(1)}, s32[64,1]{0,1:T(1,128)}, u32[]{:S(2)}) copy-start(s32[64,1]{0,1:T(1,128)} %param.16) | copy-start | bytes 772
  86.8 33.9 %copy-start.6 = (f32[1024]{0:T(1024)S(1)}, f32[1024]{0:T(1024)}, u32[]{:S(2)}) copy-start(f32[1024]{0:T(1024)} %param.26) | copy-start | bytes 12292
  86.8 33.9 %all-to-all-start.3 = ((bf16[32,48,128]{2,1,0:T(8,128)(2,1)}), bf16[32,48,128]{2,1,0:T(8,128)(2,1)S(1)}, u32[]{:S(2)}, u32[]{:S(2)}) async-start(bf16[32,48,128]{2,1,0:T(8,128)(2,1)} %attend.1), calls=%async_computation.3 | async-start | bytes 786432 | tf_op jit(solution)/shard_map/all_to_all | solution.py:580
  90.4 1.2 %collective-permute-start.14 = (bf16[64,128]{1,0:T(8,128)(2,1)S(1)}, bf16[64,128]{1,0:T(8,128)(2,1)S(1)}, u32[]{:S(2)}, u32[]{:S(2)}) collective-permute-start(bf16[64,128]{1,0:T(8,128)(2,1)S(1)} %get-tuple-element.40), channel_id=1, source_target_pairs={{0,2},{1,3},{2,0},{3,1},{4,6},{5,7},{6,4},{7,5},{8,10},{9,11},{10,... | collective-permute-start | bytes 49160 | tf_op jit(solution)/shard_map/ppermute | solution.py:448
  90.8 1.2 collective-permute-start.15
  91.9 7.6 %collective-permute-start.16 = (bf16[128,128]{1,0:T(8,128)(2,1)S(1)}, bf16[128,128]{1,0:T(8,128)(2,1)S(1)}, u32[]{:S(2)}, u32[]{:S(2)}) collective-permute-start(bf16[128,128]{1,0:T(8,128)(2,1)S(1)} %get-tuple-element.43), channel_id=1, source_target_pairs={{0,4},{1,5},{2,6},{3,7},{4,0},{5,1},{6,2},{7,3},{8,12},{9,13},{10,... | collective-permute-start | bytes 98312 | tf_op jit(solution)/shard_map/ppermute | solution.py:448
  93.7 9.2 %collective-permute-start.17 = (bf16[128,128]{1,0:T(8,128)(2,1)S(1)}, bf16[128,128]{1,0:T(8,128)(2,1)S(1)}, u32[]{:S(2)}, u32[]{:S(2)}) collective-permute-start(bf16[128,128]{1,0:T(8,128)(2,1)S(1)} %get-tuple-element.42.refs_0_), channel_id=1, source_target_pairs={{0,8},{1,9},{2,10},{3,11},{4,12},{5,13},{6,14},{7,15},{8,0},{9,1},... | collective-permute-start | bytes 98312 | tf_op jit(solution)/shard_map/ppermute | solution.py:448
  95.2 8.0 %collective-permute-start.18 = (bf16[128,128]{1,0:T(8,128)(2,1)S(1)}, bf16[128,128]{1,0:T(8,128)(2,1)S(1)}, u32[]{:S(2)}, u32[]{:S(2)}) collective-permute-start(bf16[128,128]{1,0:T(8,128)(2,1)S(1)} %get-tuple-element.43), channel_id=1, source_target_pairs={{0,12},{1,13},{2,14},{3,15},{4,8},{5,9},{6,10},{7,11},{8,4},{9,5},... | collective-permute-start | bytes 98312 | tf_op jit(solution)/shard_map/ppermute | solution.py:448
  95.5 10.5 %collective-permute-start.19 = (bf16[128,128]{1,0:T(8,128)(2,1)S(1)}, bf16[128,128]{1,0:T(8,128)(2,1)S(1)}, u32[]{:S(2)}, u32[]{:S(2)}) collective-permute-start(bf16[128,128]{1,0:T(8,128)(2,1)S(1)} %get-tuple-element.42.refs_0_), channel_id=1, source_target_pairs={{0,16},{1,17},{2,18},{3,19},{4,20},{5,21},{6,22},{7,23},{8,24},{9,... | collective-permute-start | bytes 98312 | tf_op jit(solution)/shard_map/ppermute | solution.py:448
  98.1 9.8 %collective-permute-start.20 = (bf16[128,128]{1,0:T(8,128)(2,1)S(1)}, bf16[128,128]{1,0:T(8,128)(2,1)S(1)}, u32[]{:S(2)}, u32[]{:S(2)}) collective-permute-start(bf16[128,128]{1,0:T(8,128)(2,1)S(1)} %get-tuple-element.43), channel_id=1, source_target_pairs={{0,20},{1,21},{2,22},{3,23},{4,16},{5,17},{6,18},{7,19},{8,28},{9,... | collective-permute-start | bytes 98312 | tf_op jit(solution)/shard_map/ppermute | solution.py:448
  99.5 8.4 %collective-permute-start.21 = (bf16[128,128]{1,0:T(8,128)(2,1)S(1)}, bf16[128,128]{1,0:T(8,128)(2,1)S(1)}, u32[]{:S(2)}, u32[]{:S(2)}) collective-permute-start(bf16[128,128]{1,0:T(8,128)(2,1)S(1)} %get-tuple-element.42.refs_0_), channel_id=1, source_target_pairs={{0,24},{1,25},{2,26},{3,27},{4,28},{5,29},{6,30},{7,31},{8,16},{9,... | collective-permute-start | bytes 98312 | tf_op jit(solution)/shard_map/ppermute | solution.py:448
  102.9 6.6 %collective-permute-start.22 = (bf16[128,128]{1,0:T(8,128)(2,1)S(1)}, bf16[128,128]{1,0:T(8,128)(2,1)S(1)}, u32[]{:S(2)}, u32[]{:S(2)}) collective-permute-start(bf16[128,128]{1,0:T(8,128)(2,1)S(1)} %get-tuple-element.43), channel_id=1, source_target_pairs={{0,28},{1,29},{2,30},{3,31},{4,24},{5,25},{6,26},{7,27},{8,20},{9,... | collective-permute-start | bytes 98312 | tf_op jit(solution)/shard_map/ppermute | solution.py:448
  111.2 5.4 %collective-permute-start.23 = (bf16[64,128]{1,0:T(8,128)(2,1)S(1)}, bf16[64,128]{1,0:T(8,128)(2,1)S(1)}, u32[]{:S(2)}, u32[]{:S(2)}) collective-permute-start(bf16[64,128]{1,0:T(8,128)(2,1)S(1)} %get-tuple-element.45), channel_id=1, source_target_pairs={{0,1},{1,0},{2,3},{3,2},{4,5},{5,4},{6,7},{7,6},{8,9},{9,8},{10,11... | collective-permute-start | bytes 49160 | tf_op jit(solution)/shard_map/ppermute | solution.py:391
  112.7 3.9 %collective-permute-start.24 = (bf16[64,128]{1,0:T(8,128)(2,1)S(1)}, bf16[64,128]{1,0:T(8,128)(2,1)S(1)}, u32[]{:S(2)}, u32[]{:S(2)}) collective-permute-start(bf16[64,128]{1,0:T(8,128)(2,1)S(1)} %get-tuple-element.46), channel_id=1, source_target_pairs={{0,2},{1,3},{2,0},{3,1},{4,6},{5,7},{6,4},{7,5},{8,10},{9,11},{10,... | collective-permute-start | bytes 49160 | tf_op jit(solution)/shard_map/ppermute | solution.py:391
  112.9 5.5 %collective-permute-start.25 = (bf16[64,128]{1,0:T(8,128)(2,1)S(1)}, bf16[64,128]{1,0:T(8,128)(2,1)S(1)}, u32[]{:S(2)}, u32[]{:S(2)}) collective-permute-start(bf16[64,128]{1,0:T(8,128)(2,1)S(1)} %get-tuple-element.47), channel_id=1, source_target_pairs={{0,3},{1,2},{2,1},{3,0},{4,7},{5,6},{6,5},{7,4},{8,11},{9,10},{10,... | collective-permute-start | bytes 49160 | tf_op jit(solution)/shard_map/ppermute | solution.py:391
  113.6 4.8 %collective-permute-start.26 = (bf16[64,128]{1,0:T(8,128)(2,1)S(1)}, bf16[64,128]{1,0:T(8,128)(2,1)S(1)}, u32[]{:S(2)}, u32[]{:S(2)}) collective-permute-start(bf16[64,128]{1,0:T(8,128)(2,1)S(1)} %get-tuple-element.48), channel_id=1, source_target_pairs={{0,4},{1,5},{2,6},{3,7},{4,0},{5,1},{6,2},{7,3},{8,12},{9,13},{10,... | collective-permute-start | bytes 49160 | tf_op jit(solution)/shard_map/ppermute | solution.py:391
  114.2 4.6 %collective-permute-start.27 = (bf16[64,128]{1,0:T(8,128)(2,1)S(1)}, bf16[64,128]{1,0:T(8,128)(2,1)S(1)}, u32[]{:S(2)}, u32[]{:S(2)}) collective-permute-start(bf16[64,128]{1,0:T(8,128)(2,1)S(1)} %get-tuple-element.49), channel_id=1, source_target_pairs={{0,5},{1,4},{2,7},{3,6},{4,1},{5,0},{6,3},{7,2},{8,13},{9,12},{10,... | collective-permute-start | bytes 49160 | tf_op jit(solution)/shard_map/ppermute | solution.py:391
  116.6 3.2 %collective-permute-start.28 = (bf16[64,128]{1,0:T(8,128)(2,1)S(1)}, bf16[64,128]{1,0:T(8,128)(2,1)S(1)}, u32[]{:S(2)}, u32[]{:S(2)}) collective-permute-start(bf16[64,128]{1,0:T(8,128)(2,1)S(1)} %get-tuple-element.50), channel_id=1, source_target_pairs={{0,6},{1,7},{2,4},{3,5},{4,2},{5,3},{6,0},{7,1},{8,14},{9,15},{10,... | collective-permute-start | bytes 49160 | tf_op jit(solution)/shard_map/ppermute | solution.py:391
  116.6 4.1 %collective-permute-start.29 = (bf16[64,128]{1,0:T(8,128)(2,1)S(1)}, bf16[64,128]{1,0:T(8,128)(2,1)S(1)}, u32[]{:S(2)}, u32[]{:S(2)}) collective-permute-start(bf16[64,128]{1,0:T(8,128)(2,1)S(1)} %get-tuple-element.51), channel_id=1, source_target_pairs={{0,7},{1,6},{2,5},{3,4},{4,3},{5,2},{6,1},{7,0},{8,15},{9,14},{10,... | collective-permute-start | bytes 49160 | tf_op jit(solution)/shard_map/ppermute | solution.py:391

commit v3 on v2

--- a/solution.py
+++ b/solution.py
@@ -42,16 +42,7 @@
                 columns_ref[first + turn, :, lanes] = piece
 
 
-def prepare_kernel(
-    inner,
-    context_count,
-    events_ref,
-    owner_ref,
-    bucket_ref,
-    matrix_ref,
-    packed_ref,
-    columns_ref,
-):
+def prepare_kernel(events_ref, owner_ref, bucket_ref, packed_ref):
     rows, width = events_ref.shape
     head_width = packed_ref.shape[1] - width
     across = owner_ref[...].astype(jnp.float32)
@@ -65,6 +56,9 @@
     meta = jnp.where(lanes == 0, owners, jnp.where(lanes == 1, ranking, buckets))
     packed_ref[:, :width] = events_ref[...]
     packed_ref[:, width:] = jnp.where(lanes < 3, meta, 0.0).astype(jnp.bfloat16)
+
+
+def cross_columns_kernel(inner, context_count, head_width, matrix_ref, columns_ref):
     context = lax.axis_index("ctx")
     pick_columns(inner, context_count, head_width, context, matrix_ref, columns_ref)
 
@@ -115,7 +109,7 @@
 def cross_kernel(inner, context_count, *refs):
     head_count = H
     pieces = refs[:head_count]
-    matrix_ref, bias_ref, crossed_ref, meta_ref = refs[head_count:]
+    matrix_ref, bias_ref, crossed_ref, turned_ref, meta_ref = refs[head_count:]
     me = seat(inner, context_count)
     rows = pieces[0].shape[0]
     width = bias_ref.shape[1]
@@ -129,7 +123,8 @@
         crossing = jnp.dot(piece[:, :width], matrix, preferred_element_type=jnp.float32)
         source = piece[:, columns].astype(jnp.float32)
         crossed_ref[target, :] = (source * (crossing + bias) + source).astype(jnp.bfloat16)
-        meta_ref[target, :] = piece[:, width:]
+        meta_ref[target, :] = piece[:, width:].astype(jnp.float32)
+    turned_ref[...] = meta_ref[...].T[: turned_ref.shape[0], :]
 
 
 def project_kernel(inner, context_count, slot_stride, kv_slots, chunk_users, *refs):
@@ -146,27 +141,22 @@
     copy = pltpu.make_async_copy(rows_ref, far_rows_ref, sems.at[0])
     copy.start()
     started = [copy]
-    meta = meta_ref[...]
-    turned = meta.astype(jnp.float32).T
-    owner = turned[0:1, :].astype(jnp.int32)
-    rank = turned[1:2, :].astype(jnp.int32)
+    owner = meta_ref[0:1, :].astype(jnp.int32)
+    rank = meta_ref[1:2, :].astype(jnp.int32)
     slot_of_row = owner * slot_stride + rank + base_ref[...]
-    labels = jnp.broadcast_to(meta[:, 2:3].astype(jnp.float32), meta.shape).astype(jnp.bfloat16)
     half = 0.5 * jnp.dot(rows_ref[...], matrix_ref[...], preferred_element_type=jnp.float32)
     activated = (half * (1.0 + jnp.tanh(half))).astype(jnp.bfloat16)
-    carried = jnp.concatenate([labels, activated], axis=1)
     user_count = send_ref.shape[0] // context_count
     chunk = chunk_users * slot_stride
-    lane = lax.broadcasted_iota(jnp.int32, (8, head_width), 1)
     for turn, first in enumerate(range(0, user_count, chunk_users)):
         slots = lax.broadcasted_iota(jnp.int32, (chunk, slot_of_row.shape[1]), 0)
         picked = (slots + first * slot_stride == slot_of_row).astype(jnp.float32)
         placed = jnp.dot(
-            picked.astype(jnp.bfloat16), carried, preferred_element_type=jnp.float32
+            picked.astype(jnp.bfloat16), activated, preferred_element_type=jnp.float32
         )
         for user in range(chunk_users):
             low = user * slot_stride
-            queries = placed[low : low + slot_stride, 2 * head_width : 3 * head_width]
+            queries = placed[low : low + slot_stride, head_width : 2 * head_width]
             queries = queries.astype(jnp.bfloat16)
             for context in range(context_count):
                 target = (first + user) * context_count + context
@@ -174,18 +164,13 @@
                 part = placed[start : start + kv_slots]
                 send_ref[target, 0:slot_stride, :] = queries
                 at = slot_stride
-                send_ref[target, at : at + kv_slots, :] = part[:, 3 * head_width :].astype(
+                send_ref[target, at : at + kv_slots, :] = part[:, 2 * head_width :].astype(
                     jnp.bfloat16
                 )
                 at += kv_slots
-                send_ref[target, at : at + kv_slots, :] = part[
-                    :, head_width : 2 * head_width
-                ].astype(jnp.bfloat16)
-                at += kv_slots
-                note = part[0:8, :head_width]
-                for tile in range(1, kv_slots // 8):
-                    note = jnp.where(lane == tile, part[tile * 8 : tile * 8 + 8, :head_width], note)
-                send_ref[target, at : at + 8, :] = note.astype(jnp.bfloat16)
+                send_ref[target, at : at + kv_slots, :] = part[:, :head_width].astype(
+                    jnp.bfloat16
+                )
         done = pl.ds(first * context_count, chunk_users * context_count)
         copy = pltpu.make_async_copy(send_ref.at[done], out_ref.at[done], sems.at[turn + 1])
         copy.start()
@@ -194,24 +179,14 @@
         copy.wait()
 
 
-def stage_kernel(
-    capacity,
-    length_ref,
-    after_ref,
-    far_ref,
-    bucket_ref,
-    time_bias_ref,
-    key_order_ref,
-    query_order_ref,
-    near_ref,
-    cache_bias_ref,
-    near_time_bias_ref,
-    near_key_order_ref,
-    near_query_order_ref,
-    sem,
-):
+def stage_kernel(inner, capacity, kv_slots, length_ref, after_ref, far_ref, *refs):
+    bucket_ref, time_bias_ref, key_order_ref, query_order_ref, base_ref = refs[:5]
+    metas = refs[5:-7]
+    near_ref, cache_bias_ref, new_bias_ref, near_key_order_ref, near_query_order_ref = refs[-7:-2]
+    found_ref, sem = refs[-2:]
     copy = pltpu.make_async_copy(far_ref, near_ref, sem)
     copy.start()
+    user, context = lax.axis_index("users"), lax.axis_index("ctx")
     table = time_bias_ref[...]
     shape = (table.shape[1], bucket_ref.shape[1])
     levels = lax.broadcasted_iota(jnp.int32, shape, 0)
@@ -220,10 +195,25 @@
         table, picked, precision=lax.Precision.HIGHEST, preferred_element_type=jnp.float32
     )
     positions = lax.broadcasted_iota(jnp.int32, bias.shape, 1)
-    context = lax.axis_index("ctx")
     live = length_ref[0] - context * bias.shape[1]
     cache_bias_ref[...] = jnp.where(positions < live, 0.5 * bias, DEAD)
-    near_time_bias_ref[...] = table
+    group = user // inner
+    for mask, meta_ref in enumerate(metas):
+        place = meta_ref[1:2, :].astype(jnp.int32) + base_ref[...] - context * kv_slots
+        place = jnp.where(meta_ref[0:1, :].astype(jnp.int32) == user, place, -1)
+        slots = lax.broadcasted_iota(jnp.int32, (kv_slots, place.shape[1]), 0)
+        found = jnp.sum(jnp.where(slots == place, meta_ref[2:3, :], 0.0), axis=1, keepdims=True)
+        target = pl.ds(pl.multiple_of((group ^ mask) * kv_slots, 8), kv_slots)
+        found_ref[target, :] = jnp.broadcast_to(found, (kv_slots, found_ref.shape[1]))
+    levels = lax.broadcasted_iota(jnp.int32, (found_ref.shape[0], table.shape[1]), 1)
+    hits = jnp.where(levels == found_ref[:, 0:1].astype(jnp.int32), 1.0, 0.0)
+    new_bias_ref[...] = 0.5 * lax.dot_general(
+        hits,
+        table,
+        (((1,), (1,)), ((), ())),
+        precision=lax.Precision.HIGHEST,
+        preferred_element_type=jnp.float32,
+    )
     near_key_order_ref[...] = key_order_ref[...] + context * capacity
     near_query_order_ref[...] = query_order_ref[...]
     copy.wait()
@@ -238,7 +228,7 @@
     keys_ref,
     far_values_ref,
     cache_bias_ref,
-    time_bias_ref,
+    new_bias_ref,
     key_order_ref,
     query_order_ref,
     out_ref,
@@ -279,17 +269,8 @@
         new_keys = recv_ref[:, head, at : at + kv_slots, :].reshape(key_count, head_width)
         at += kv_slots
         new_values = recv_ref[:, head, at : at + kv_slots, :].reshape(key_count, head_width)
-        at += kv_slots
-        notes = recv_ref[:, head, at : at + 8, :].astype(jnp.float32)
-        buckets = jnp.concatenate(
-            [notes[g, :, t : t + 1] for g in range(group_count) for t in range(kv_slots // 8)],
-            axis=0,
-        ).astype(jnp.int32)
-        table = time_bias_ref[head : head + 1, :]
-        levels = lax.broadcasted_iota(jnp.int32, (key_count, table.shape[1]), 1)
-        new_bias = jnp.sum(jnp.where(levels == buckets, table, 0.0), axis=1, keepdims=True)
         new_scores = lax.dot_general(new_keys, queries, nt, preferred_element_type=jnp.float32)
-        new_half = new_scores * half_scale + 0.5 * new_bias
+        new_half = new_scores * half_scale + new_bias_ref[:, head : head + 1]
         new_weights = jnp.where(
             key_order_ref[...] <= query_order_ref[pl.ds(block, 1), :],
             new_half * (1.0 + jnp.tanh(new_half)),
@@ -342,9 +323,9 @@
         columns = pl.ds(pl.multiple_of((me ^ mask) * head_width, head_width), head_width)
         gate_ref[:, columns] = gates[mask][...]
     for row in range(rows):
-        total = returned_ref[place_ref[row, 0]].astype(jnp.float32)
-        for context in range(1, place_ref.shape[1]):
-            total = total + returned_ref[place_ref[row, context]].astype(jnp.float32)
+        total = returned_ref[place_ref[0, row]].astype(jnp.float32)
+        for context in range(1, context_count):
+            total = total + returned_ref[place_ref[context, row]].astype(jnp.float32)
         tall_ref[row * head_count : (row + 1) * head_count, :] = total
     attended = jnp.concatenate(
         [tall_ref[pl.ds(head, rows, stride=head_count), :] for head in range(head_count)], axis=1
@@ -381,7 +362,6 @@
     kv_slots = round_up(inner * capacity, 8)
     slot_stride = context_count * kv_slots
     cache_rows = cache_keys.shape[1]
-    bucket_count = time_bias.shape[0]
     group_rows = H * row_count
     core = context_count if inner > 1 else 0
     blocks = project_weight.shape[1] // width
@@ -410,13 +390,20 @@
     packed_shape = jax.ShapeDtypeStruct((row_count, width + head_width), jnp.bfloat16)
     matrix_rows = cross_weight.shape[0]
     cross_shape = jax.ShapeDtypeStruct((owner_count, matrix_rows, head_width), jnp.bfloat16)
-    packed, cross_columns = pl.pallas_call(
-        functools.partial(prepare_kernel, inner, context_count),
-        out_shape=(packed_shape, cross_shape),
-        in_specs=[vmem_spec] * 4,
-        out_specs=(vmem_spec, vmem_spec),
+    cross_columns = pl.pallas_call(
+        functools.partial(cross_columns_kernel, inner, context_count, head_width),
+        out_shape=cross_shape,
+        in_specs=[vmem_spec],
+        out_specs=vmem_spec,
+        name="cross_columns",
+    )(cross_weight)
+    packed = pl.pallas_call(
+        prepare_kernel,
+        out_shape=packed_shape,
+        in_specs=[vmem_spec] * 3,
+        out_specs=vmem_spec,
         name="prepare",
-    )(events, owner_id.reshape(1, -1), event_bucket[None, :], cross_weight)
+    )(events, owner_id.reshape(1, -1), event_bucket[None, :])
     pieces = spread(packed)
     project_shape = jax.ShapeDtypeStruct(
         (owner_count, matrix_rows, (blocks - 1) * head_width), jnp.bfloat16
@@ -461,23 +448,34 @@
         trade(gate_pairs[mask // 2 % gate_kinds], mask) for mask in range(2, owner_count, 2)
     ]
 
+    meta_shape = jax.ShapeDtypeStruct((8, group_rows), jnp.float32)
     crossed, group_meta = pl.pallas_call(
         functools.partial(cross_kernel, inner, context_count),
         out_shape=(
             jax.ShapeDtypeStruct((group_rows, head_width), jnp.bfloat16),
-            jax.ShapeDtypeStruct((group_rows, head_width), jnp.bfloat16),
+            meta_shape,
         ),
         in_specs=[vmem_spec] * (H + 2),
         out_specs=(vmem_spec, vmem_spec),
+        scratch_shapes=[pltpu.VMEM((group_rows, head_width), jnp.float32)],
         compiler_params=grant(*pieces, cross_columns),
         name="cross",
     )(*pieces, cross_columns, cross_bias[None, :])
     crossed_pieces = spread(crossed)
+    metas = [group_meta]
+    for mask in range(1, group_count):
+        pairs = [
+            (g * H + member, (g ^ mask) * H + member)
+            for g in range(group_count)
+            for member in range(H)
+        ]
+        metas.append(lax.ppermute(group_meta, AXES, pairs))
 
     shard = np.arange(group_rows) // row_count
     base = ((shard % context_count) * kv_slots + (shard // context_count) * capacity)[None, :]
-    message_rows = slot_stride + 2 * kv_slots + 8
-    chunk_users = max(1, min(owner_count, 512 // slot_stride))
+    message_rows = slot_stride + 2 * kv_slots
+    base = jnp.asarray(base, jnp.int32)
+    chunk_users = max(1, min(owner_count, 256 // slot_stride))
     while owner_count % chunk_users:
         chunk_users -= 1
     messages = jax.ShapeDtypeStruct((device_count, message_rows, head_width), jnp.bfloat16)
@@ -497,7 +495,7 @@
         ],
         compiler_params=grant(*crossed_pieces, project_columns, messages, messages),
         name="project",
-    )(*crossed_pieces, project_columns, group_meta, jnp.asarray(base, jnp.int32))
+    )(*crossed_pieces, project_columns, group_meta, base)
     gates = pl.pallas_call(
         functools.partial(gate_kernel, inner, context_count),
         out_shape=[jax.ShapeDtypeStruct((row_count, head_width), jnp.bfloat16)] * H,
@@ -537,17 +535,20 @@
         return pltpu.with_memory_space_constraint(cache[0], pltpu.MemorySpace.HBM)
 
     near = pl.pallas_call(
-        functools.partial(stage_kernel, capacity),
+        functools.partial(stage_kernel, inner, capacity, kv_slots),
         out_shape=(
             jax.ShapeDtypeStruct(cache_keys.shape[1:], cache_keys.dtype),
             jax.ShapeDtypeStruct((H, cache_rows), jnp.float32),
-            jax.ShapeDtypeStruct((H, bucket_count), jnp.float32),
+            jax.ShapeDtypeStruct((group_count * kv_slots, H), jnp.float32),
             jax.ShapeDtypeStruct((group_count * kv_slots, 1), jnp.int32),
             jax.ShapeDtypeStruct(query_order.shape, jnp.int32),
         ),
-        in_specs=[smem_spec, vmem_spec, hbm_spec] + [vmem_spec] * 4,
+        in_specs=[smem_spec, vmem_spec, hbm_spec] + [vmem_spec] * (5 + group_count),
         out_specs=[vmem_spec] * 5,
-        scratch_shapes=[pltpu.SemaphoreType.DMA(())],
+        scratch_shapes=[
+            pltpu.VMEM((group_count * kv_slots, head_width), jnp.float32),
+            pltpu.SemaphoreType.DMA(()),
+        ],
         compiler_params=grant(cache_keys),
         name="stage",
     )(
@@ -558,6 +559,8 @@
         time_bias.T,
         key_order[:, None],
         query_order,
+        base,
+        *metas,
     )
 
     partials = pl.pallas_call(
@@ -578,8 +581,8 @@
     )(arrived, near[0], far(cache_values), *near[1:])
 
     returned = lax.all_to_all(partials, AXES, split_axis=0, concat_axis=0, tiled=True)
-    contexts = jnp.arange(context_count, dtype=jnp.int32)[None, :]
-    places = (owners[:, None] * context_count + contexts) * capacity + ranking[:, None]
+    contexts = jnp.arange(context_count, dtype=jnp.int32)[:, None]
+    places = (owners[None, :] * context_count + contexts) * capacity + ranking[None, :]
     return pl.pallas_call(
         functools.partial(finish_kernel, inner, context_count),
         out_shape=jax.ShapeDtypeStruct((row_count, width), jnp.bfloat16),

time: 124 us -> 125 us (level)
  waiting for transfers between devices: 59 us -> 54.6 us
  starting transfers between devices: 45.9 us -> 49.9 us
    all_to_all x1, waiting for transfers between devices: 19.7 us -> 0.01 us  [shards(): lax.all_to_all(outgoing, AXES, split_axis=0, concat_axis=0, tiled=True)]
    ppermute x0 -> x3, waiting for transfers between devices: none -> 16.7 us  [shards(): metas.append(lax.ppermute(group_meta, AXES, pairs))]
    ppermute x0 -> x3, starting transfers between devices: none -> 4.45 us  [shards(): metas.append(lax.ppermute(group_meta, AXES, pairs))]
    pallas_call x2 -> x3, Pallas kernels: 3.55 us -> 5.23 us  [the longest x1 1.85 us: shards(): pl.pallas_call(prepare_kernel, out_shape=packed_shape, in_specs=[vmem_spe...]
    ppermute x21, waiting for transfers between devices: 24.1 us -> 22.7 us  [swap(): return lax.ppermute(block, AXES, pairs)]
  transfers between devices with their start and end apart: 34 -> 37, of which waited for: 18 -> 19; matrix products, arithmetic and copies ran while one was open for 0% -> 0% of each run, Pallas kernels for 4% -> 5%
where the time goes in v3:
time: 125 us; the launch traced here: 124 us
  waiting for transfers between devices  54.6 us (44%)
  starting transfers between devices  49.9 us (40%)
  Pallas kernels  16.6 us (13%)
  local copies, waits for them, and re-layouts  1.98 us (2%)
    ppermute x21, waiting for transfers between devices, swap(): return lax.ppermute(block, AXES, pairs)  22.7 us
    ppermute x3, waiting for transfers between devices, shards(): metas.append(lax.ppermute(group_meta, AXES, pairs))  16.7 us
    ppermute x21, starting transfers between devices, swap(): return lax.ppermute(block, AXES, pairs)  14.2 us
    ppermute x9, starting transfers between devices, trade(): return lax.ppermute(block, AXES, pairs)  11.8 us
    all_to_all x1, waiting for transfers between devices, shards(): lax.all_to_all(cross_columns, 'users', split_axis=0, concat_axis=0, tiled...  7.98 us
    all_to_all x1, starting transfers between devices, shards(): lax.all_to_all(cross_columns, 'users', split_axis=0, concat_axis=0, tiled...  7.52 us
    ppermute x9, waiting for transfers between devices, trade(): return lax.ppermute(block, AXES, pairs)  7.24 us
    all_to_all x1, starting transfers between devices, shards(): lax.all_to_all(outgoing, AXES, split_axis=0, concat_axis=0, tiled=True)  4.81 us
  transfers between devices with their start and end apart: 37, of which 19 were waited for; matrix products, arithmetic and copies ran while one was open for 0% of the time, Pallas kernels for 5%

profile of v3, /device:TPU:0, one launch (start us, length us, event | category | flops | bytes accessed | tf_op | source)
XLA Modules:
  0.0 124.1 jit_solution(16221139163582933194)
XLA Ops:
  0.0 1.6 %cross_columns.1 = bf16[16,64,128]{2,1,0:T(8,128)(2,1)} custom-call(bf16[64,1024]{1,0:T(8,128)(2,1)} %matrix_ref.2), custom_call_target="tpu_custom_call" | custom-call | tf_op jit(solution)/shard_map/cross_columns/pallas_call | solution.py:393
  1.6 7.5 %all-to-all-start = ((bf16[16,64,128]{2,1,0:T(8,128)(2,1)}), bf16[16,64,128]{2,1,0:T(8,128)(2,1)S(1)}, u32[]{:S(2)}, u32[]{:S(2)}) async-start(bf16[16,64,128]{2,1,0:T(8,128)(2,1)} %cross_columns.1), calls=%async_computation | async-start | bytes 524288 | tf_op jit(solution)/shard_map/all_to_all | solution.py:422
  9.2 1.0 copy-done.1
  10.2 1.0 columns.1
  11.2 8.0 %all-to-all-done = bf16[16,64,128]{2,1,0:T(8,128)(2,1)S(1)} async-done(((bf16[16,64,128]{2,1,0:T(8,128)(2,1)}), bf16[16,64,128]{2,1,0:T(8,128)(2,1)S(1)}, u32[]{:S(2)}, u32[]{:S(2)}) %all-to-all-start) | async-done | bytes 262176 | tf_op jit(solution)/shard_map/all_to_all | solution.py:422
  19.2 3.6 %all-to-all-start.1 = ((bf16[16,64,384]{2,1,0:T(8,128)(2,1)}), bf16[16,64,384]{2,1,0:T(8,128)(2,1)S(1)}, u32[]{:S(2)}, u32[]{:S(2)}) async-start(bf16[16,64,384]{2,1,0:T(8,128)(2,1)} %get-tuple-element.31), calls=%async_computation.1 | async-start | bytes 1572864 | tf_op jit(solution)/shard_map/all_to_all | solution.py:423
  22.8 1.8 %prepare.1.refs_0_ = bf16[64,1152]{1,0:T(8,128)(2,1)} custom-call(bf16[64,1024]{1,0:T(8,128)(2,1)} %events_ref.1, s32[1,64]{1,0:T(1,128)} %bitcast.23, s32[1,64]{1,0:T(1,128)} %bitcast.22), custom_call_target="tpu_custom_call" | custom-call | tf_op jit(solution)/shard_map/prepare/pallas_call | solution.py:400
  24.7 1.5 %collective-permute-start = (bf16[64,1152]{1,0:T(8,128)(2,1)}, bf16[64,1152]{1,0:T(8,128)(2,1)S(1)}, u32[]{:S(2)}, u32[]{:S(2)}) collective-permute-start(bf16[64,1152]{1,0:T(8,128)(2,1)} %prepare.1.refs_0_), channel_id=1, source_target_pairs={{0,1},{1,0},{2,3},{3,2},{4,5},{5,4},{6,7},{7,6},{8,9},{9,8},{10,11... | collective-permute-start | bytes 442376 | tf_op jit(solution)/shard_map/ppermute | solution.py:371
  26.2 1.8 %collective-permute-start.3 = (bf16[64,1152]{1,0:T(8,128)(2,1)}, bf16[64,1152]{1,0:T(8,128)(2,1)S(1)}, u32[]{:S(2)}, u32[]{:S(2)}) collective-permute-start(bf16[64,1152]{1,0:T(8,128)(2,1)} %prepare.1.refs_0_), channel_id=1, source_target_pairs={{0,4},{1,5},{2,6},{3,7},{4,0},{5,1},{6,2},{7,3},{8,12},{9,13},{10,... | collective-permute-start | bytes 442376 | tf_op jit(solution)/shard_map/ppermute | solution.py:371
  28.1 2.8 %collective-permute-done.refs_1_ = bf16[64,1152]{1,0:T(8,128)(2,1)S(1)} collective-permute-done((bf16[64,1152]{1,0:T(8,128)(2,1)}, bf16[64,1152]{1,0:T(8,128)(2,1)S(1)}, u32[]{:S(2)}, u32[]{:S(2)}) %collective-permute-start) | collective-permute-done | bytes 147488 | tf_op jit(solution)/shard_map/ppermute | solution.py:371
  30.9 4.9 %collective-permute-done.3.refs_4_ = bf16[64,1152]{1,0:T(8,128)(2,1)S(1)} collective-permute-done((bf16[64,1152]{1,0:T(8,128)(2,1)}, bf16[64,1152]{1,0:T(8,128)(2,1)S(1)}, u32[]{:S(2)}, u32[]{:S(2)}) %collective-permute-start.3) | collective-permute-done | bytes 147488 | tf_op jit(solution)/shard_map/ppermute | solution.py:371
  35.8 3.6 %collective-permute-done.4.refs_5_ = bf16[64,1152]{1,0:T(8,128)(2,1)S(1)} collective-permute-done((bf16[64,1152]{1,0:T(8,128)(2,1)}, bf16[64,1152]{1,0:T(8,128)(2,1)S(1)}, u32[]{:S(2)}, u32[]{:S(2)}) %collective-permute-start.4) | collective-permute-done | bytes 147488 | tf_op jit(solution)/shard_map/ppermute | solution.py:371
  39.4 1.3 %collective-permute-done.6.refs_7_ = bf16[64,1152]{1,0:T(8,128)(2,1)S(1)} collective-permute-done((bf16[64,1152]{1,0:T(8,128)(2,1)S(1)}, bf16[64,1152]{1,0:T(8,128)(2,1)S(1)}, u32[]{:S(2)}, u32[]{:S(2)}) %collective-permute-start.6) | collective-permute-done | bytes 147488 | tf_op jit(solution)/shard_map/ppermute | solution.py:371
  40.8 0.9 copy-done
  42.2 0.6 collective-permute-start.7
  42.7 2.8 %collective-permute-start.10 = (bf16[512,128]{1,0:T(8,128)(2,1)S(1)}, bf16[512,128]{1,0:T(8,128)(2,1)S(1)}, u32[]{:S(2)}, u32[]{:S(2)}) collective-permute-start(bf16[512,128]{1,0:T(8,128)(2,1)S(1)} %get-tuple-element.30.refs_0_), channel_id=1, source_target_pairs={{0,4},{1,5},{2,6},{3,7},{4,0},{5,1},{6,2},{7,3},{8,12},{9,13},{10,... | collective-permute-start | bytes 393224 | tf_op jit(solution)/shard_map/ppermute | solution.py:371
  45.9 1.8 %collective-permute-done.7.refs_1_ = bf16[512,128]{1,0:T(8,128)(2,1)S(1)} collective-permute-done((bf16[512,128]{1,0:T(8,128)(2,1)S(1)}, bf16[512,128]{1,0:T(8,128)(2,1)S(1)}, u32[]{:S(2)}, u32[]{:S(2)}) %collective-permute-start.7) | collective-permute-done | bytes 131104 | tf_op jit(solution)/shard_map/ppermute | solution.py:371
  47.8 2.1 %collective-permute-done.10.refs_4_ = bf16[512,128]{1,0:T(8,128)(2,1)S(1)} collective-permute-done((bf16[512,128]{1,0:T(8,128)(2,1)S(1)}, bf16[512,128]{1,0:T(8,128)(2,1)S(1)}, u32[]{:S(2)}, u32[]{:S(2)}) %collective-permute-start.10) | collective-permute-done | bytes 131104 | tf_op jit(solution)/shard_map/ppermute | solution.py:371
  49.9 2.3 %collective-permute-done.11.refs_5_ = bf16[512,128]{1,0:T(8,128)(2,1)S(1)} collective-permute-done((bf16[512,128]{1,0:T(8,128)(2,1)S(1)}, bf16[512,128]{1,0:T(8,128)(2,1)S(1)}, u32[]{:S(2)}, u32[]{:S(2)}) %collective-permute-start.11) | collective-permute-done | bytes 131104 | tf_op jit(solution)/shard_map/ppermute | solution.py:371
  52.3 1.3 %collective-permute-done.13.refs_7_ = bf16[512,128]{1,0:T(8,128)(2,1)S(1)} collective-permute-done((bf16[512,128]{1,0:T(8,128)(2,1)S(1)}, bf16[512,128]{1,0:T(8,128)(2,1)S(1)}, u32[]{:S(2)}, u32[]{:S(2)}) %collective-permute-start.13) | collective-permute-done | bytes 131104 | tf_op jit(solution)/shard_map/ppermute | solution.py:371
  53.6 2.3 %project.1 = (f32[8,128]{1,0:T(8,128)S(1)}, bf16[512,1024]{1,0:T(8,128)(2,1)}, bf16[32,96,128]{2,1,0:T(8,128)(2,1)}) custom-call(bf16[512,128]{1,0:T(8,128)(2,1)S(1)} %get-tuple-element.30.refs_0_, bf16[512,128]{1,0:T(8,128)(2,1)S(1)} %collective-permute-done.7.refs_1_, bf16[512,128]{1,0:T(8,128)(2,1)S(1)} %collective-permute-done.8.refs_2_, ...), custom_call_target="tpu_custom_call" | custom-call | tf_op jit(solution)/shard_map/project/pallas_call | solution.py:482
  55.9 4.8 %all-to-all-start.2 = ((bf16[32,96,128]{2,1,0:T(8,128)(2,1)}), bf16[32,96,128]{2,1,0:T(8,128)(2,1)S(1)}, u32[]{:S(2)}, u32[]{:S(2)}) async-start(bf16[32,96,128]{2,1,0:T(8,128)(2,1)} %get-tuple-element.48), calls=%async_computation.2 | async-start | bytes 1572864 | tf_op jit(solution)/shard_map/all_to_all | solution.py:517
  60.7 1.8 %collective-permute-start.30 = (f32[8,512]{1,0:T(8,128)S(1)}, f32[8,512]{1,0:T(8,128)S(1)}, u32[]{:S(2)}, u32[]{:S(2)}) collective-permute-start(f32[8,512]{1,0:T(8,128)S(1)} %get-tuple-element.32.refs_9_.refs_5_), channel_id=1, source_target_pairs={{0,8},{1,9},{2,10},{3,11},{4,12},{5,13},{6,14},{7,15},{8,0},{9,1},... | collective-permute-start | bytes 49160 | tf_op jit(solution)/shard_map/ppermute | solution.py:472
  62.5 2.4 %collective-permute-start.31 = (f32[8,512]{1,0:T(8,128)S(1)}, f32[8,512]{1,0:T(8,128)S(1)}, u32[]{:S(2)}, u32[]{:S(2)}) collective-permute-start(f32[8,512]{1,0:T(8,128)S(1)} %get-tuple-element.32.refs_9_.refs_5_), channel_id=1, source_target_pairs={{0,16},{1,17},{2,18},{3,19},{4,20},{5,21},{6,22},{7,23},{8,24},{9,... | collective-permute-start | bytes 49160 | tf_op jit(solution)/shard_map/ppermute | solution.py:472
  65.8 8.9 %collective-permute-done.30.refs_6_ = f32[8,512]{1,0:T(8,128)S(1)} collective-permute-done((f32[8,512]{1,0:T(8,128)S(1)}, f32[8,512]{1,0:T(8,128)S(1)}, u32[]{:S(2)}, u32[]{:S(2)}) %collective-permute-start.30) | collective-permute-done | bytes 16416 | tf_op jit(solution)/shard_map/ppermute | solution.py:472
  74.7 7.8 %collective-permute-done.31.refs_7_ = f32[8,512]{1,0:T(8,128)S(1)} collective-permute-done((f32[8,512]{1,0:T(8,128)S(1)}, f32[8,512]{1,0:T(8,128)S(1)}, u32[]{:S(2)}, u32[]{:S(2)}) %collective-permute-start.31) | collective-permute-done | bytes 16416 | tf_op jit(solution)/shard_map/ppermute | solution.py:472
  82.6 1.7 %stage.1 = (bf16[1024,1024]{1,0:T(8,128)(2,1)S(1)}, f32[8,1024]{1,0:T(8,128)S(1)}, f32[96,8]{1,0:T(8,128)S(1)}, s32[96,1]{1,0:T(8,128)S(1)}, s32[1,192]{1,0:T(1,128)S(1)}) custom-call(s32[1]{0:T(128)S(6)} %copy.16.length_ref, f32[8,128]{1,0:T(8,128)S(1)} %get-tuple-element.49.after_ref, bf16[1024,1024]{1,0:T(8,128)(2,1)} %bitcast.20, ...), custom_call_target="tpu_custom_call" | custom-call | tf_op jit(solution)/shard_map/stage/pallas_call | solution.py:537
  84.3 4.4 %attend.1 = bf16[32,48,128]{2,1,0:T(8,128)(2,1)} custom-call(bf16[4,8,96,128]{3,2,1,0:T(8,128)(2,1)S(1)} %bitcast.14, bf16[1024,1024]{1,0:T(8,128)(2,1)S(1)} %get-tuple-element.50.keys_ref, bf16[1024,1024]{1,0:T(8,128)(2,1)} %bitcast.21, f32[8,1024]{1,0:T(8,128)S(1)} %get-tuple-element.51.cache_bias_ref, f32[96,8]{1,0:T(8,128)S(1)} %get-tuple-element.52.new_bias_ref, ...), custom_call_target="tpu_custom_call" | custom-call | tf_op jit(solution)/shard_map/attend/pallas_call | solution.py:566
  88.8 3.5 %all-to-all-start.3 = ((bf16[32,48,128]{2,1,0:T(8,128)(2,1)}), bf16[32,48,128]{2,1,0:T(8,128)(2,1)S(1)}, u32[]{:S(2)}, u32[]{:S(2)}) async-start(bf16[32,48,128]{2,1,0:T(8,128)(2,1)} %attend.1), calls=%async_computation.3 | async-start | bytes 786432 | tf_op jit(solution)/shard_map/all_to_all | solution.py:583
  92.8 0.7 collective-permute-done.14.refs_2_
  93.8 1.7 %collective-permute-start.16 = (bf16[128,128]{1,0:T(8,128)(2,1)S(1)}, bf16[128,128]{1,0:T(8,128)(2,1)S(1)}, u32[]{:S(2)}, u32[]{:S(2)}) collective-permute-start(bf16[128,128]{1,0:T(8,128)(2,1)S(1)} %get-tuple-element.39), channel_id=1, source_target_pairs={{0,4},{1,5},{2,6},{3,7},{4,0},{5,1},{6,2},{7,3},{8,12},{9,13},{10,... | collective-permute-start | bytes 98312 | tf_op jit(solution)/shard_map/ppermute | solution.py:435
  95.5 1.5 %collective-permute-start.17 = (bf16[128,128]{1,0:T(8,128)(2,1)S(1)}, bf16[128,128]{1,0:T(8,128)(2,1)S(1)}, u32[]{:S(2)}, u32[]{:S(2)}) collective-permute-start(bf16[128,128]{1,0:T(8,128)(2,1)S(1)} %get-tuple-element.38.refs_0_), channel_id=1, source_target_pairs={{0,8},{1,9},{2,10},{3,11},{4,12},{5,13},{6,14},{7,15},{8,0},{9,1},... | collective-permute-start | bytes 98312 | tf_op jit(solution)/shard_map/ppermute | solution.py:435
  97.3 2.6 %collective-permute-start.19 = (bf16[128,128]{1,0:T(8,128)(2,1)S(1)}, bf16[128,128]{1,0:T(8,128)(2,1)S(1)}, u32[]{:S(2)}, u32[]{:S(2)}) collective-permute-start(bf16[128,128]{1,0:T(8,128)(2,1)S(1)} %get-tuple-element.38.refs_0_), channel_id=1, source_target_pairs={{0,16},{1,17},{2,18},{3,19},{4,20},{5,21},{6,22},{7,23},{8,24},{9,... | collective-permute-start | bytes 98312 | tf_op jit(solution)/shard_map/ppermute | solution.py:435
  99.9 1.5 %collective-permute-start.20 = (bf16[128,128]{1,0:T(8,128)(2,1)S(1)}, bf16[128,128]{1,0:T(8,128)(2,1)S(1)}, u32[]{:S(2)}, u32[]{:S(2)}) collective-permute-start(bf16[128,128]{1,0:T(8,128)(2,1)S(1)} %get-tuple-element.39), channel_id=1, source_target_pairs={{0,20},{1,21},{2,22},{3,23},{4,16},{5,17},{6,18},{7,19},{8,28},{9,... | collective-permute-start | bytes 98312 | tf_op jit(solution)/shard_map/ppermute | solution.py:435
  101.4 3.3 %collective-permute-start.21 = (bf16[128,128]{1,0:T(8,128)(2,1)S(1)}, bf16[128,128]{1,0:T(8,128)(2,1)S(1)}, u32[]{:S(2)}, u32[]{:S(2)}) collective-permute-start(bf16[128,128]{1,0:T(8,128)(2,1)S(1)} %get-tuple-element.38.refs_0_), channel_id=1, source_target_pairs={{0,24},{1,25},{2,26},{3,27},{4,28},{5,29},{6,30},{7,31},{8,16},{9,... | collective-permute-start | bytes 98312 | tf_op jit(solution)/shard_map/ppermute | solution.py:435
  105.0 2.8 %collective-permute-done.19.refs_4_ = bf16[128,128]{1,0:T(8,128)(2,1)S(1)} collective-permute-done((bf16[128,128]{1,0:T(8,128)(2,1)S(1)}, bf16[128,128]{1,0:T(8,128)(2,1)S(1)}, u32[]{:S(2)}, u32[]{:S(2)}) %collective-permute-start.19) | collective-permute-done | bytes 32800 | tf_op jit(solution)/shard_map/ppermute | solution.py:435
  107.8 1.9 %collective-permute-done.20.refs_5_ = bf16[128,128]{1,0:T(8,128)(2,1)S(1)} collective-permute-done((bf16[128,128]{1,0:T(8,128)(2,1)S(1)}, bf16[128,128]{1,0:T(8,128)(2,1)S(1)}, u32[]{:S(2)}, u32[]{:S(2)}) %collective-permute-start.20) | collective-permute-done | bytes 32800 | tf_op jit(solution)/shard_map/ppermute | solution.py:435
  109.8 1.6 %collective-permute-done.22.refs_7_ = bf16[128,128]{1,0:T(8,128)(2,1)S(1)} collective-permute-done((bf16[128,128]{1,0:T(8,128)(2,1)S(1)}, bf16[128,128]{1,0:T(8,128)(2,1)S(1)}, u32[]{:S(2)}, u32[]{:S(2)}) %collective-permute-start.22) | collective-permute-done | bytes 32800 | tf_op jit(solution)/shard_map/ppermute | solution.py:435
  111.3 1.7 %gate.1 = (bf16[64,128]{1,0:T(8,128)(2,1)S(1)}, bf16[64,128]{1,0:T(8,128)(2,1)S(1)}, bf16[64,128]{1,0:T(8,128)(2,1)S(1)}, bf16[64,128]{1,0:T(8,128)(2,1)S(1)}, b...) custom-call(bf16[512,1024]{1,0:T(8,128)(2,1)} %get-tuple-element.33., ...), custom_call_target="tpu_custom_call" | custom-call | tf_op jit(solution)/shard_map/gate/pallas_call | solution.py:499
  113.0 1.6 %collective-permute-start.23 = (bf16[64,128]{1,0:T(8,128)(2,1)S(1)}, bf16[64,128]{1,0:T(8,128)(2,1)S(1)}, u32[]{:S(2)}, u32[]{:S(2)}) collective-permute-start(bf16[64,128]{1,0:T(8,128)(2,1)S(1)} %get-tuple-element.41), channel_id=1, source_target_pairs={{0,1},{1,0},{2,3},{3,2},{4,5},{5,4},{6,7},{7,6},{8,9},{9,8},{10,11... | collective-permute-start | bytes 49160 | tf_op jit(solution)/shard_map/ppermute | solution.py:371
  114.7 0.7 collective-permute-start.25
  115.5 0.5 collective-permute-start.26
  116.0 2.4 %collective-permute-start.27 = (bf16[64,128]{1,0:T(8,128)(2,1)S(1)}, bf16[64,128]{1,0:T(8,128)(2,1)S(1)}, u32[]{:S(2)}, u32[]{:S(2)}) collective-permute-start(bf16[64,128]{1,0:T(8,128)(2,1)S(1)} %get-tuple-element.45), channel_id=1, source_target_pairs={{0,5},{1,4},{2,7},{3,6},{4,1},{5,0},{6,3},{7,2},{8,13},{9,12},{10,... | collective-permute-start | bytes 49160 | tf_op jit(solution)/shard_map/ppermute | solution.py:371
  118.4 1.7 %collective-permute-start.29 = (bf16[64,128]{1,0:T(8,128)(2,1)S(1)}, bf16[64,128]{1,0:T(8,128)(2,1)S(1)}, u32[]{:S(2)}, u32[]{:S(2)}) collective-permute-start(bf16[64,128]{1,0:T(8,128)(2,1)S(1)} %get-tuple-element.47), channel_id=1, source_target_pairs={{0,7},{1,6},{2,5},{3,4},{4,3},{5,2},{6,1},{7,0},{8,15},{9,14},{10,... | collective-permute-start | bytes 49160 | tf_op jit(solution)/shard_map/ppermute | solution.py:371
  120.1 0.5 collective-permute-done.27.refs_5_
  120.6 0.9 collective-permute-done.28.refs_6_
  121.6 1.0 collective-permute-done.29.refs_7_
  122.6 1.5 %finish.1 = bf16[64,1024]{1,0:T(8,128)(2,1)} custom-call(s32[2,64]{1,0:T(2,128)S(1)} %multiply_add_fusion.place_ref, bf16[64,128]{1,0:T(8,128)(2,1)S(1)} %get-tuple-element.40.refs_0_, bf16[64,128]{1,0:T(8,128)(2,1)S(1)} %collective-permute-done.23.refs_1_, bf16[64,128]{1,0:T(8,128)(2,1)S(1)} %collective-permute-done.24.refs_2_, ...), custom_call_target="tpu_custom_call" | custom-call | tf_op jit(solution)/shard_map/finish/pallas_call | solution.py:586
  (59 shorter events, 3.0 us)
Async XLA Ops:
  0.0 40.8 %copy-start.4 = (f32[1024]{0:T(1024)S(1)}, f32[1024]{0:T(1024)}, u32[]{:S(2)}) copy-start(f32[1024]{0:T(1024)} %param.19) | copy-start | bytes 12292
  1.6 51.9 %copy-start.3 = (s32[1,512]{1,0:T(1,128)S(1)}, s32[1,512]{1,0:T(1,128)}, u32[]{:S(2)}) copy-start(s32[1,512]{1,0:T(1,128)} %constant.12.clone.refs_10_.refs_4_) | copy-start | bytes 6148
  1.6 17.5 %all-to-all-start = ((bf16[16,64,128]{2,1,0:T(8,128)(2,1)}), bf16[16,64,128]{2,1,0:T(8,128)(2,1)S(1)}, u32[]{:S(2)}, u32[]{:S(2)}) async-start(bf16[16,64,128]{2,1,0:T(8,128)(2,1)} %cross_columns.1), calls=%async_computation | async-start | bytes 524288 | tf_op jit(solution)/shard_map/all_to_all | solution.py:422
  9.2 1.0 copy-start.1
  19.2 34.4 %all-to-all-start.1 = ((bf16[16,64,384]{2,1,0:T(8,128)(2,1)}), bf16[16,64,384]{2,1,0:T(8,128)(2,1)S(1)}, u32[]{:S(2)}, u32[]{:S(2)}) async-start(bf16[16,64,384]{2,1,0:T(8,128)(2,1)} %get-tuple-element.31), calls=%async_computation.1 | async-start | bytes 1572864 | tf_op jit(solution)/shard_map/all_to_all | solution.py:423
  24.7 6.3 %collective-permute-start = (bf16[64,1152]{1,0:T(8,128)(2,1)}, bf16[64,1152]{1,0:T(8,128)(2,1)S(1)}, u32[]{:S(2)}, u32[]{:S(2)}) collective-permute-start(bf16[64,1152]{1,0:T(8,128)(2,1)} %prepare.1.refs_0_), channel_id=1, source_target_pairs={{0,1},{1,0},{2,3},{3,2},{4,5},{5,4},{6,7},{7,6},{8,9},{9,8},{10,11... | collective-permute-start | bytes 442376 | tf_op jit(solution)/shard_map/ppermute | solution.py:371
  26.2 9.6 %collective-permute-start.3 = (bf16[64,1152]{1,0:T(8,128)(2,1)}, bf16[64,1152]{1,0:T(8,128)(2,1)S(1)}, u32[]{:S(2)}, u32[]{:S(2)}) collective-permute-start(bf16[64,1152]{1,0:T(8,128)(2,1)} %prepare.1.refs_0_), channel_id=1, source_target_pairs={{0,4},{1,5},{2,6},{3,7},{4,0},{5,1},{6,2},{7,3},{8,12},{9,13},{10,... | collective-permute-start | bytes 442376 | tf_op jit(solution)/shard_map/ppermute | solution.py:371
  28.0 11.4 %collective-permute-start.4 = (bf16[64,1152]{1,0:T(8,128)(2,1)}, bf16[64,1152]{1,0:T(8,128)(2,1)S(1)}, u32[]{:S(2)}, u32[]{:S(2)}) collective-permute-start(bf16[64,1152]{1,0:T(8,128)(2,1)} %prepare.1.refs_0_), channel_id=1, source_target_pairs={{0,5},{1,4},{2,7},{3,6},{4,1},{5,0},{6,3},{7,2},{8,13},{9,12},{10,... | collective-permute-start | bytes 442376 | tf_op jit(solution)/shard_map/ppermute | solution.py:371
  28.1 11.3 %collective-permute-start.1 = (bf16[64,1152]{1,0:T(8,128)(2,1)}, bf16[64,1152]{1,0:T(8,128)(2,1)S(1)}, u32[]{:S(2)}, u32[]{:S(2)}) collective-permute-start(bf16[64,1152]{1,0:T(8,128)(2,1)} %prepare.1.refs_0_), channel_id=1, source_target_pairs={{0,2},{1,3},{2,0},{3,1},{4,6},{5,7},{6,4},{7,5},{8,10},{9,11},{10,... | collective-permute-start | bytes 442376 | tf_op jit(solution)/shard_map/ppermute | solution.py:371
  30.9 8.5 %collective-permute-start.2 = (bf16[64,1152]{1,0:T(8,128)(2,1)S(1)}, bf16[64,1152]{1,0:T(8,128)(2,1)S(1)}, u32[]{:S(2)}, u32[]{:S(2)}) collective-permute-start(bf16[64,1152]{1,0:T(8,128)(2,1)S(1)} %collective-permute-done.refs_1_), channel_id=1, source_target_pairs={{0,2},{1,3},{2,0},{3,1},{4,6},{5,7},{6,4},{7,5},{8,10},{9,11},{10,... | collective-permute-start | bytes 442376 | tf_op jit(solution)/shard_map/ppermute | solution.py:371
  35.8 3.6 %collective-permute-start.5 = (bf16[64,1152]{1,0:T(8,128)(2,1)S(1)}, bf16[64,1152]{1,0:T(8,128)(2,1)S(1)}, u32[]{:S(2)}, u32[]{:S(2)}) collective-permute-start(bf16[64,1152]{1,0:T(8,128)(2,1)S(1)} %collective-permute-done.3.refs_4_), channel_id=1, source_target_pairs={{0,2},{1,3},{2,0},{3,1},{4,6},{5,7},{6,4},{7,5},{8,10},{9,11},{10,... | collective-permute-start | bytes 442376 | tf_op jit(solution)/shard_map/ppermute | solution.py:371
  39.4 1.4 %collective-permute-start.6 = (bf16[64,1152]{1,0:T(8,128)(2,1)S(1)}, bf16[64,1152]{1,0:T(8,128)(2,1)S(1)}, u32[]{:S(2)}, u32[]{:S(2)}) collective-permute-start(bf16[64,1152]{1,0:T(8,128)(2,1)S(1)} %collective-permute-done.4.refs_5_), channel_id=1, source_target_pairs={{0,2},{1,3},{2,0},{3,1},{4,6},{5,7},{6,4},{7,5},{8,10},{9,11},{10,... | collective-permute-start | bytes 442376 | tf_op jit(solution)/shard_map/ppermute | solution.py:371
  40.8 0.9 copy-start
  41.7 40.8 %copy-start.2 = (s32[96,1]{1,0:T(8,128)S(1)}, s32[96,1]{1,0:T(8,128)}, u32[]{:S(2)}) copy-start(s32[96,1]{1,0:T(8,128)} %constant.19.refs_2_) | copy-start | bytes 1156
  41.7 40.8 %copy-start.5 = (s32[1,1024]{1,0:T(1,128)S(1)}, s32[1,1024]{1,0:T(1,128)}, u32[]{:S(2)}) copy-start(s32[1,1024]{1,0:T(1,128)} %refs_0_.1) | copy-start | bytes 12292
  41.7 40.9 %copy-start.6 = (f32[32,8]{0,1:T(8,128)S(1)}, f32[32,8]{0,1:T(8,128)}, u32[]{:S(2)}) copy-start(f32[32,8]{0,1:T(8,128)} %param.25) | copy-start | bytes 3076
  41.7 40.9 %copy-start.8 = (s32[1,192]{1,0:T(1,128)S(1)}, s32[1,192]{1,0:T(1,128)}, u32[]{:S(2)}) copy-start(s32[1,192]{1,0:T(1,128)} %constant.20.refs_3_) | copy-start | bytes 2308
  42.2 5.6 %collective-permute-start.7 = (bf16[512,128]{1,0:T(8,128)(2,1)S(1)}, bf16[512,128]{1,0:T(8,128)(2,1)S(1)}, u32[]{:S(2)}, u32[]{:S(2)}) collective-permute-start(bf16[512,128]{1,0:T(8,128)(2,1)S(1)} %get-tuple-element.30.refs_0_), channel_id=1, source_target_pairs={{0,1},{1,0},{2,3},{3,2},{4,5},{5,4},{6,7},{7,6},{8,9},{9,8},{10,11... | collective-permute-start | bytes 393224 | tf_op jit(solution)/shard_map/ppermute | solution.py:371
  42.7 7.2 %collective-permute-start.10 = (bf16[512,128]{1,0:T(8,128)(2,1)S(1)}, bf16[512,128]{1,0:T(8,128)(2,1)S(1)}, u32[]{:S(2)}, u32[]{:S(2)}) collective-permute-start(bf16[512,128]{1,0:T(8,128)(2,1)S(1)} %get-tuple-element.30.refs_0_), channel_id=1, source_target_pairs={{0,4},{1,5},{2,6},{3,7},{4,0},{5,1},{6,2},{7,3},{8,12},{9,13},{10,... | collective-permute-start | bytes 393224 | tf_op jit(solution)/shard_map/ppermute | solution.py:371
  45.6 6.7 %collective-permute-start.11 = (bf16[512,128]{1,0:T(8,128)(2,1)S(1)}, bf16[512,128]{1,0:T(8,128)(2,1)S(1)}, u32[]{:S(2)}, u32[]{:S(2)}) collective-permute-start(bf16[512,128]{1,0:T(8,128)(2,1)S(1)} %get-tuple-element.30.refs_0_), channel_id=1, source_target_pairs={{0,5},{1,4},{2,7},{3,6},{4,1},{5,0},{6,3},{7,2},{8,13},{9,12},{10,... | collective-permute-start | bytes 393224 | tf_op jit(solution)/shard_map/ppermute | solution.py:371
  45.9 6.3 %collective-permute-start.8 = (bf16[512,128]{1,0:T(8,128)(2,1)S(1)}, bf16[512,128]{1,0:T(8,128)(2,1)S(1)}, u32[]{:S(2)}, u32[]{:S(2)}) collective-permute-start(bf16[512,128]{1,0:T(8,128)(2,1)S(1)} %get-tuple-element.30.refs_0_), channel_id=1, source_target_pairs={{0,2},{1,3},{2,0},{3,1},{4,6},{5,7},{6,4},{7,5},{8,10},{9,11},{10,... | collective-permute-start | bytes 393224 | tf_op jit(solution)/shard_map/ppermute | solution.py:371
  47.8 4.5 %collective-permute-start.9 = (bf16[512,128]{1,0:T(8,128)(2,1)S(1)}, bf16[512,128]{1,0:T(8,128)(2,1)S(1)}, u32[]{:S(2)}, u32[]{:S(2)}) collective-permute-start(bf16[512,128]{1,0:T(8,128)(2,1)S(1)} %collective-permute-done.7.refs_1_), channel_id=1, source_target_pairs={{0,2},{1,3},{2,0},{3,1},{4,6},{5,7},{6,4},{7,5},{8,10},{9,11},{10,... | collective-permute-start | bytes 393224 | tf_op jit(solution)/shard_map/ppermute | solution.py:371
  49.9 2.4 %collective-permute-start.12 = (bf16[512,128]{1,0:T(8,128)(2,1)S(1)}, bf16[512,128]{1,0:T(8,128)(2,1)S(1)}, u32[]{:S(2)}, u32[]{:S(2)}) collective-permute-start(bf16[512,128]{1,0:T(8,128)(2,1)S(1)} %collective-permute-done.10.refs_4_), channel_id=1, source_target_pairs={{0,2},{1,3},{2,0},{3,1},{4,6},{5,7},{6,4},{7,5},{8,10},{9,11},{10,... | collective-permute-start | bytes 393224 | tf_op jit(solution)/shard_map/ppermute | solution.py:371
  52.2 1.3 %collective-permute-start.13 = (bf16[512,128]{1,0:T(8,128)(2,1)S(1)}, bf16[512,128]{1,0:T(8,128)(2,1)S(1)}, u32[]{:S(2)}, u32[]{:S(2)}) collective-permute-start(bf16[512,128]{1,0:T(8,128)(2,1)S(1)} %collective-permute-done.11.refs_5_), channel_id=1, source_target_pairs={{0,2},{1,3},{2,0},{3,1},{4,6},{5,7},{6,4},{7,5},{8,10},{9,11},{10,... | collective-permute-start | bytes 393224 | tf_op jit(solution)/shard_map/ppermute | solution.py:371
  55.9 28.4 %all-to-all-start.2 = ((bf16[32,96,128]{2,1,0:T(8,128)(2,1)}), bf16[32,96,128]{2,1,0:T(8,128)(2,1)S(1)}, u32[]{:S(2)}, u32[]{:S(2)}) async-start(bf16[32,96,128]{2,1,0:T(8,128)(2,1)} %get-tuple-element.48), calls=%async_computation.2 | async-start | bytes 1572864 | tf_op jit(solution)/shard_map/all_to_all | solution.py:517
  60.7 14.0 %collective-permute-start.30 = (f32[8,512]{1,0:T(8,128)S(1)}, f32[8,512]{1,0:T(8,128)S(1)}, u32[]{:S(2)}, u32[]{:S(2)}) collective-permute-start(f32[8,512]{1,0:T(8,128)S(1)} %get-tuple-element.32.refs_9_.refs_5_), channel_id=1, source_target_pairs={{0,8},{1,9},{2,10},{3,11},{4,12},{5,13},{6,14},{7,15},{8,0},{9,1},... | collective-permute-start | bytes 49160 | tf_op jit(solution)/shard_map/ppermute | solution.py:472
  62.5 20.0 %collective-permute-start.31 = (f32[8,512]{1,0:T(8,128)S(1)}, f32[8,512]{1,0:T(8,128)S(1)}, u32[]{:S(2)}, u32[]{:S(2)}) collective-permute-start(f32[8,512]{1,0:T(8,128)S(1)} %get-tuple-element.32.refs_9_.refs_5_), channel_id=1, source_target_pairs={{0,16},{1,17},{2,18},{3,19},{4,20},{5,21},{6,22},{7,23},{8,24},{9,... | collective-permute-start | bytes 49160 | tf_op jit(solution)/shard_map/ppermute | solution.py:472
  65.0 17.6 %collective-permute-start.32 = (f32[8,512]{1,0:T(8,128)S(1)}, f32[8,512]{1,0:T(8,128)S(1)}, u32[]{:S(2)}, u32[]{:S(2)}) collective-permute-start(f32[8,512]{1,0:T(8,128)S(1)} %get-tuple-element.32.refs_9_.refs_5_), channel_id=1, source_target_pairs={{0,24},{1,25},{2,26},{3,27},{4,28},{5,29},{6,30},{7,31},{8,16},{9,... | collective-permute-start | bytes 49160 | tf_op jit(solution)/shard_map/ppermute | solution.py:472
  84.3 20.7 %copy-start.9 = (s32[64,1]{0,1:T(1,128)S(1)}, s32[64,1]{0,1:T(1,128)}, u32[]{:S(2)}) copy-start(s32[64,1]{0,1:T(1,128)} %param.16) | copy-start | bytes 772
  88.7 33.8 %copy-start.7 = (f32[1024]{0:T(1024)S(1)}, f32[1024]{0:T(1024)}, u32[]{:S(2)}) copy-start(f32[1024]{0:T(1024)} %param.26) | copy-start | bytes 12292
  88.8 33.8 %all-to-all-start.3 = ((bf16[32,48,128]{2,1,0:T(8,128)(2,1)}), bf16[32,48,128]{2,1,0:T(8,128)(2,1)S(1)}, u32[]{:S(2)}, u32[]{:S(2)}) async-start(bf16[32,48,128]{2,1,0:T(8,128)(2,1)} %attend.1), calls=%async_computation.3 | async-start | bytes 786432 | tf_op jit(solution)/shard_map/all_to_all | solution.py:583
  92.3 1.2 %collective-permute-start.14 = (bf16[64,128]{1,0:T(8,128)(2,1)S(1)}, bf16[64,128]{1,0:T(8,128)(2,1)S(1)}, u32[]{:S(2)}, u32[]{:S(2)}) collective-permute-start(bf16[64,128]{1,0:T(8,128)(2,1)S(1)} %get-tuple-element.36), channel_id=1, source_target_pairs={{0,2},{1,3},{2,0},{3,1},{4,6},{5,7},{6,4},{7,5},{8,10},{9,11},{10,... | collective-permute-start | bytes 49160 | tf_op jit(solution)/shard_map/ppermute | solution.py:435
  92.6 1.2 collective-permute-start.15
  93.8 7.6 %collective-permute-start.16 = (bf16[128,128]{1,0:T(8,128)(2,1)S(1)}, bf16[128,128]{1,0:T(8,128)(2,1)S(1)}, u32[]{:S(2)}, u32[]{:S(2)}) collective-permute-start(bf16[128,128]{1,0:T(8,128)(2,1)S(1)} %get-tuple-element.39), channel_id=1, source_target_pairs={{0,4},{1,5},{2,6},{3,7},{4,0},{5,1},{6,2},{7,3},{8,12},{9,13},{10,... | collective-permute-start | bytes 98312 | tf_op jit(solution)/shard_map/ppermute | solution.py:435
  95.5 9.2 %collective-permute-start.17 = (bf16[128,128]{1,0:T(8,128)(2,1)S(1)}, bf16[128,128]{1,0:T(8,128)(2,1)S(1)}, u32[]{:S(2)}, u32[]{:S(2)}) collective-permute-start(bf16[128,128]{1,0:T(8,128)(2,1)S(1)} %get-tuple-element.38.refs_0_), channel_id=1, source_target_pairs={{0,8},{1,9},{2,10},{3,11},{4,12},{5,13},{6,14},{7,15},{8,0},{9,1},... | collective-permute-start | bytes 98312 | tf_op jit(solution)/shard_map/ppermute | solution.py:435
  97.0 8.0 %collective-permute-start.18 = (bf16[128,128]{1,0:T(8,128)(2,1)S(1)}, bf16[128,128]{1,0:T(8,128)(2,1)S(1)}, u32[]{:S(2)}, u32[]{:S(2)}) collective-permute-start(bf16[128,128]{1,0:T(8,128)(2,1)S(1)} %get-tuple-element.39), channel_id=1, source_target_pairs={{0,12},{1,13},{2,14},{3,15},{4,8},{5,9},{6,10},{7,11},{8,4},{9,5},... | collective-permute-start | bytes 98312 | tf_op jit(solution)/shard_map/ppermute | solution.py:435
  97.3 10.5 %collective-permute-start.19 = (bf16[128,128]{1,0:T(8,128)(2,1)S(1)}, bf16[128,128]{1,0:T(8,128)(2,1)S(1)}, u32[]{:S(2)}, u32[]{:S(2)}) collective-permute-start(bf16[128,128]{1,0:T(8,128)(2,1)S(1)} %get-tuple-element.38.refs_0_), channel_id=1, source_target_pairs={{0,16},{1,17},{2,18},{3,19},{4,20},{5,21},{6,22},{7,23},{8,24},{9,... | collective-permute-start | bytes 98312 | tf_op jit(solution)/shard_map/ppermute | solution.py:435
  99.9 9.8 %collective-permute-start.20 = (bf16[128,128]{1,0:T(8,128)(2,1)S(1)}, bf16[128,128]{1,0:T(8,128)(2,1)S(1)}, u32[]{:S(2)}, u32[]{:S(2)}) collective-permute-start(bf16[128,128]{1,0:T(8,128)(2,1)S(1)} %get-tuple-element.39), channel_id=1, source_target_pairs={{0,20},{1,21},{2,22},{3,23},{4,16},{5,17},{6,18},{7,19},{8,28},{9,... | collective-permute-start | bytes 98312 | tf_op jit(solution)/shard_map/ppermute | solution.py:435
  101.4 8.4 %collective-permute-start.21 = (bf16[128,128]{1,0:T(8,128)(2,1)S(1)}, bf16[128,128]{1,0:T(8,128)(2,1)S(1)}, u32[]{:S(2)}, u32[]{:S(2)}) collective-permute-start(bf16[128,128]{1,0:T(8,128)(2,1)S(1)} %get-tuple-element.38.refs_0_), channel_id=1, source_target_pairs={{0,24},{1,25},{2,26},{3,27},{4,28},{5,29},{6,30},{7,31},{8,16},{9,... | collective-permute-start | bytes 98312 | tf_op jit(solution)/shard_map/ppermute | solution.py:435
  104.7 6.6 %collective-permute-start.22 = (bf16[128,128]{1,0:T(8,128)(2,1)S(1)}, bf16[128,128]{1,0:T(8,128)(2,1)S(1)}, u32[]{:S(2)}, u32[]{:S(2)}) collective-permute-start(bf16[128,128]{1,0:T(8,128)(2,1)S(1)} %get-tuple-element.39), channel_id=1, source_target_pairs={{0,28},{1,29},{2,30},{3,31},{4,24},{5,25},{6,26},{7,27},{8,20},{9,... | collective-permute-start | bytes 98312 | tf_op jit(solution)/shard_map/ppermute | solution.py:435
  113.0 5.4 %collective-permute-start.23 = (bf16[64,128]{1,0:T(8,128)(2,1)S(1)}, bf16[64,128]{1,0:T(8,128)(2,1)S(1)}, u32[]{:S(2)}, u32[]{:S(2)}) collective-permute-start(bf16[64,128]{1,0:T(8,128)(2,1)S(1)} %get-tuple-element.41), channel_id=1, source_target_pairs={{0,1},{1,0},{2,3},{3,2},{4,5},{5,4},{6,7},{7,6},{8,9},{9,8},{10,11... | collective-permute-start | bytes 49160 | tf_op jit(solution)/shard_map/ppermute | solution.py:371
  114.6 3.9 %collective-permute-start.24 = (bf16[64,128]{1,0:T(8,128)(2,1)S(1)}, bf16[64,128]{1,0:T(8,128)(2,1)S(1)}, u32[]{:S(2)}, u32[]{:S(2)}) collective-permute-start(bf16[64,128]{1,0:T(8,128)(2,1)S(1)} %get-tuple-element.42), channel_id=1, source_target_pairs={{0,2},{1,3},{2,0},{3,1},{4,6},{5,7},{6,4},{7,5},{8,10},{9,11},{10,... | collective-permute-start | bytes 49160 | tf_op jit(solution)/shard_map/ppermute | solution.py:371
  114.7 5.4 %collective-permute-start.25 = (bf16[64,128]{1,0:T(8,128)(2,1)S(1)}, bf16[64,128]{1,0:T(8,128)(2,1)S(1)}, u32[]{:S(2)}, u32[]{:S(2)}) collective-permute-start(bf16[64,128]{1,0:T(8,128)(2,1)S(1)} %get-tuple-element.43), channel_id=1, source_target_pairs={{0,3},{1,2},{2,1},{3,0},{4,7},{5,6},{6,5},{7,4},{8,11},{9,10},{10,... | collective-permute-start | bytes 49160 | tf_op jit(solution)/shard_map/ppermute | solution.py:371
  115.5 4.7 %collective-permute-start.26 = (bf16[64,128]{1,0:T(8,128)(2,1)S(1)}, bf16[64,128]{1,0:T(8,128)(2,1)S(1)}, u32[]{:S(2)}, u32[]{:S(2)}) collective-permute-start(bf16[64,128]{1,0:T(8,128)(2,1)S(1)} %get-tuple-element.44), channel_id=1, source_target_pairs={{0,4},{1,5},{2,6},{3,7},{4,0},{5,1},{6,2},{7,3},{8,12},{9,13},{10,... | collective-permute-start | bytes 49160 | tf_op jit(solution)/shard_map/ppermute | solution.py:371
  116.0 4.6 %collective-permute-start.27 = (bf16[64,128]{1,0:T(8,128)(2,1)S(1)}, bf16[64,128]{1,0:T(8,128)(2,1)S(1)}, u32[]{:S(2)}, u32[]{:S(2)}) collective-permute-start(bf16[64,128]{1,0:T(8,128)(2,1)S(1)} %get-tuple-element.45), channel_id=1, source_target_pairs={{0,5},{1,4},{2,7},{3,6},{4,1},{5,0},{6,3},{7,2},{8,13},{9,12},{10,... | collective-permute-start | bytes 49160 | tf_op jit(solution)/shard_map/ppermute | solution.py:371
  118.4 3.2 %collective-permute-start.28 = (bf16[64,128]{1,0:T(8,128)(2,1)S(1)}, bf16[64,128]{1,0:T(8,128)(2,1)S(1)}, u32[]{:S(2)}, u32[]{:S(2)}) collective-permute-start(bf16[64,128]{1,0:T(8,128)(2,1)S(1)} %get-tuple-element.46), channel_id=1, source_target_pairs={{0,6},{1,7},{2,4},{3,5},{4,2},{5,3},{6,0},{7,1},{8,14},{9,15},{10,... | collective-permute-start | bytes 49160 | tf_op jit(solution)/shard_map/ppermute | solution.py:371
  118.4 4.1 %collective-permute-start.29 = (bf16[64,128]{1,0:T(8,128)(2,1)S(1)}, bf16[64,128]{1,0:T(8,128)(2,1)S(1)}, u32[]{:S(2)}, u32[]{:S(2)}) collective-permute-start(bf16[64,128]{1,0:T(8,128)(2,1)S(1)} %get-tuple-element.47), channel_id=1, source_target_pairs={{0,7},{1,6},{2,5},{3,4},{4,3},{5,2},{6,1},{7,0},{8,15},{9,14},{10,... | collective-permute-start | bytes 49160 | tf_op jit(solution)/shard_map/ppermute | solution.py:371

commit v4 on v3

--- a/solution.py
+++ b/solution.py
@@ -12,6 +12,7 @@
 AXES = ("users", "ctx")
 NORM_EPSILON = 1e-05
 DEAD = -1e30
+LAG = 6
 VMEM = pltpu.MemorySpace.VMEM
 SMEM = pltpu.MemorySpace.SMEM
 
@@ -235,10 +236,16 @@
     summed_ref,
     values_ref,
     weights_ref,
-    sem,
+    sems,
 ):
-    copy = pltpu.make_async_copy(far_values_ref, values_ref, sem)
-    copy.start()
+    half_width = values_ref.shape[1] // 2
+    copies = []
+    for side in range(2):
+        part = slice(side * half_width, (side + 1) * half_width)
+        copies.append(
+            pltpu.make_async_copy(far_values_ref.at[:, part], values_ref.at[:, part], sems.at[side])
+        )
+        copies[-1].start()
     group_count, head_count, _, head_width = recv_ref.shape
     context_count = slot_stride // kv_slots
     inner = head_count // context_count
@@ -252,11 +259,14 @@
         columns = slice(head * head_width, (head + 1) * head_width)
         queries = recv_ref[pl.ds(first, block_groups), head, 0:slot_stride, :]
         queries = queries.reshape(block_rows, head_width)
-        scores = lax.dot_general(
-            queries, keys_ref[:, columns], nt, preferred_element_type=jnp.float32
-        )
-        half = scores * half_scale + cache_bias_ref[head : head + 1, :]
-        weights_ref[head] = (half * (1.0 + jnp.tanh(half))).astype(jnp.bfloat16)
+        step = min(256, keys_ref.shape[0])
+        for start in range(0, keys_ref.shape[0], step):
+            part = slice(start, start + step)
+            scores = lax.dot_general(
+                queries, keys_ref[part, columns], nt, preferred_element_type=jnp.float32
+            )
+            half = scores * half_scale + cache_bias_ref[head : head + 1, part]
+            weights_ref[head, :, part] = (half * (1.0 + jnp.tanh(half))).astype(jnp.bfloat16)
 
     def gather(block, first, head):
         columns = slice(head * head_width, (head + 1) * head_width)
@@ -283,12 +293,14 @@
 
     def one_block(block, waits):
         first = block * block_groups
-        lag = head_count // 2
+        lag = LAG
         for head in range(head_count + lag):
             if head < head_count:
                 weigh(first, head)
             if waits and head == lag:
-                copy.wait()
+                copies[0].wait()
+            if waits and head == lag + head_count // 2:
+                copies[1].wait()
             if head >= lag:
                 gather(block, first, head - lag)
         for group in range(block_groups):
@@ -303,7 +315,8 @@
     if block_count == 1:
         one_block(0, True)
     else:
-        copy.wait()
+        for copy in copies:
+            copy.wait()
 
         def step(block, carry):
             one_block(block, False)
@@ -574,7 +587,7 @@
             pltpu.VMEM((block_rows * H, head_width), jnp.float32),
             pltpu.VMEM(cache_values.shape[1:], cache_values.dtype),
             pltpu.VMEM((H, block_rows, cache_rows), jnp.bfloat16),
-            pltpu.SemaphoreType.DMA(()),
+            pltpu.SemaphoreType.DMA((2,)),
         ],
         compiler_params=grant(arrived, cache_keys, cache_values, query_order),
         name="attend",

time: 125 us -> 125 us (level)
  no operation moved by 1% of the time
where the time goes in v4:
time: 125 us; the launch traced here: 124 us
  waiting for transfers between devices  54.6 us (44%)
  starting transfers between devices  49.9 us (40%)
  Pallas kernels  16.4 us (13%)
  local copies, waits for them, and re-layouts  1.98 us (2%)
    ppermute x21, waiting for transfers between devices, swap(): return lax.ppermute(block, AXES, pairs)  22.6 us
    ppermute x3, waiting for transfers between devices, shards(): metas.append(lax.ppermute(group_meta, AXES, pairs))  16.7 us
    ppermute x21, starting transfers between devices, swap(): return lax.ppermute(block, AXES, pairs)  14.2 us
    ppermute x9, starting transfers between devices, trade(): return lax.ppermute(block, AXES, pairs)  11.8 us
    all_to_all x1, waiting for transfers between devices, shards(): lax.all_to_all(cross_columns, 'users', split_axis=0, concat_axis=0, tiled...  7.98 us
    all_to_all x1, starting transfers between devices, shards(): lax.all_to_all(cross_columns, 'users', split_axis=0, concat_axis=0, tiled...  7.52 us
    ppermute x9, waiting for transfers between devices, trade(): return lax.ppermute(block, AXES, pairs)  7.24 us
    all_to_all x1, starting transfers between devices, shards(): lax.all_to_all(outgoing, AXES, split_axis=0, concat_axis=0, tiled=True)  4.81 us
  transfers between devices with their start and end apart: 37, of which 19 were waited for; matrix products, arithmetic and copies ran while one was open for 0% of the time, Pallas kernels for 5%

profile of v4, /device:TPU:0, one launch (start us, length us, event | category | flops | bytes accessed | tf_op | source)
XLA Modules:
  0.0 123.9 jit_solution(10518525426771742725)
XLA Ops:
  0.0 1.6 %cross_columns.1 = bf16[16,64,128]{2,1,0:T(8,128)(2,1)} custom-call(bf16[64,1024]{1,0:T(8,128)(2,1)} %matrix_ref.2), custom_call_target="tpu_custom_call" | custom-call | tf_op jit(solution)/shard_map/cross_columns/pallas_call | solution.py:406
  1.6 7.5 %all-to-all-start = ((bf16[16,64,128]{2,1,0:T(8,128)(2,1)}), bf16[16,64,128]{2,1,0:T(8,128)(2,1)S(1)}, u32[]{:S(2)}, u32[]{:S(2)}) async-start(bf16[16,64,128]{2,1,0:T(8,128)(2,1)} %cross_columns.1), calls=%async_computation | async-start | bytes 524288 | tf_op jit(solution)/shard_map/all_to_all | solution.py:435
  9.2 1.0 copy-done.1
  10.2 1.0 columns.1
  11.2 8.0 %all-to-all-done = bf16[16,64,128]{2,1,0:T(8,128)(2,1)S(1)} async-done(((bf16[16,64,128]{2,1,0:T(8,128)(2,1)}), bf16[16,64,128]{2,1,0:T(8,128)(2,1)S(1)}, u32[]{:S(2)}, u32[]{:S(2)}) %all-to-all-start) | async-done | bytes 262176 | tf_op jit(solution)/shard_map/all_to_all | solution.py:435
  19.2 3.6 %all-to-all-start.1 = ((bf16[16,64,384]{2,1,0:T(8,128)(2,1)}), bf16[16,64,384]{2,1,0:T(8,128)(2,1)S(1)}, u32[]{:S(2)}, u32[]{:S(2)}) async-start(bf16[16,64,384]{2,1,0:T(8,128)(2,1)} %get-tuple-element.31), calls=%async_computation.1 | async-start | bytes 1572864 | tf_op jit(solution)/shard_map/all_to_all | solution.py:436
  22.8 1.8 %prepare.1.refs_0_ = bf16[64,1152]{1,0:T(8,128)(2,1)} custom-call(bf16[64,1024]{1,0:T(8,128)(2,1)} %events_ref.1, s32[1,64]{1,0:T(1,128)} %bitcast.23, s32[1,64]{1,0:T(1,128)} %bitcast.22), custom_call_target="tpu_custom_call" | custom-call | tf_op jit(solution)/shard_map/prepare/pallas_call | solution.py:413
  24.7 1.5 %collective-permute-start = (bf16[64,1152]{1,0:T(8,128)(2,1)}, bf16[64,1152]{1,0:T(8,128)(2,1)S(1)}, u32[]{:S(2)}, u32[]{:S(2)}) collective-permute-start(bf16[64,1152]{1,0:T(8,128)(2,1)} %prepare.1.refs_0_), channel_id=1, source_target_pairs={{0,1},{1,0},{2,3},{3,2},{4,5},{5,4},{6,7},{7,6},{8,9},{9,8},{10,11... | collective-permute-start | bytes 442376 | tf_op jit(solution)/shard_map/ppermute | solution.py:384
  26.2 1.8 %collective-permute-start.3 = (bf16[64,1152]{1,0:T(8,128)(2,1)}, bf16[64,1152]{1,0:T(8,128)(2,1)S(1)}, u32[]{:S(2)}, u32[]{:S(2)}) collective-permute-start(bf16[64,1152]{1,0:T(8,128)(2,1)} %prepare.1.refs_0_), channel_id=1, source_target_pairs={{0,4},{1,5},{2,6},{3,7},{4,0},{5,1},{6,2},{7,3},{8,12},{9,13},{10,... | collective-permute-start | bytes 442376 | tf_op jit(solution)/shard_map/ppermute | solution.py:384
  28.1 2.8 %collective-permute-done.refs_1_ = bf16[64,1152]{1,0:T(8,128)(2,1)S(1)} collective-permute-done((bf16[64,1152]{1,0:T(8,128)(2,1)}, bf16[64,1152]{1,0:T(8,128)(2,1)S(1)}, u32[]{:S(2)}, u32[]{:S(2)}) %collective-permute-start) | collective-permute-done | bytes 147488 | tf_op jit(solution)/shard_map/ppermute | solution.py:384
  30.9 4.9 %collective-permute-done.3.refs_4_ = bf16[64,1152]{1,0:T(8,128)(2,1)S(1)} collective-permute-done((bf16[64,1152]{1,0:T(8,128)(2,1)}, bf16[64,1152]{1,0:T(8,128)(2,1)S(1)}, u32[]{:S(2)}, u32[]{:S(2)}) %collective-permute-start.3) | collective-permute-done | bytes 147488 | tf_op jit(solution)/shard_map/ppermute | solution.py:384
  35.8 3.6 %collective-permute-done.4.refs_5_ = bf16[64,1152]{1,0:T(8,128)(2,1)S(1)} collective-permute-done((bf16[64,1152]{1,0:T(8,128)(2,1)}, bf16[64,1152]{1,0:T(8,128)(2,1)S(1)}, u32[]{:S(2)}, u32[]{:S(2)}) %collective-permute-start.4) | collective-permute-done | bytes 147488 | tf_op jit(solution)/shard_map/ppermute | solution.py:384
  39.4 1.3 %collective-permute-done.6.refs_7_ = bf16[64,1152]{1,0:T(8,128)(2,1)S(1)} collective-permute-done((bf16[64,1152]{1,0:T(8,128)(2,1)S(1)}, bf16[64,1152]{1,0:T(8,128)(2,1)S(1)}, u32[]{:S(2)}, u32[]{:S(2)}) %collective-permute-start.6) | collective-permute-done | bytes 147488 | tf_op jit(solution)/shard_map/ppermute | solution.py:384
  40.8 0.9 copy-done
  42.2 0.6 collective-permute-start.7
  42.7 2.8 %collective-permute-start.10 = (bf16[512,128]{1,0:T(8,128)(2,1)S(1)}, bf16[512,128]{1,0:T(8,128)(2,1)S(1)}, u32[]{:S(2)}, u32[]{:S(2)}) collective-permute-start(bf16[512,128]{1,0:T(8,128)(2,1)S(1)} %get-tuple-element.30.refs_0_), channel_id=1, source_target_pairs={{0,4},{1,5},{2,6},{3,7},{4,0},{5,1},{6,2},{7,3},{8,12},{9,13},{10,... | collective-permute-start | bytes 393224 | tf_op jit(solution)/shard_map/ppermute | solution.py:384
  45.9 1.8 %collective-permute-done.7.refs_1_ = bf16[512,128]{1,0:T(8,128)(2,1)S(1)} collective-permute-done((bf16[512,128]{1,0:T(8,128)(2,1)S(1)}, bf16[512,128]{1,0:T(8,128)(2,1)S(1)}, u32[]{:S(2)}, u32[]{:S(2)}) %collective-permute-start.7) | collective-permute-done | bytes 131104 | tf_op jit(solution)/shard_map/ppermute | solution.py:384
  47.8 2.1 %collective-permute-done.10.refs_4_ = bf16[512,128]{1,0:T(8,128)(2,1)S(1)} collective-permute-done((bf16[512,128]{1,0:T(8,128)(2,1)S(1)}, bf16[512,128]{1,0:T(8,128)(2,1)S(1)}, u32[]{:S(2)}, u32[]{:S(2)}) %collective-permute-start.10) | collective-permute-done | bytes 131104 | tf_op jit(solution)/shard_map/ppermute | solution.py:384
  49.9 2.3 %collective-permute-done.11.refs_5_ = bf16[512,128]{1,0:T(8,128)(2,1)S(1)} collective-permute-done((bf16[512,128]{1,0:T(8,128)(2,1)S(1)}, bf16[512,128]{1,0:T(8,128)(2,1)S(1)}, u32[]{:S(2)}, u32[]{:S(2)}) %collective-permute-start.11) | collective-permute-done | bytes 131104 | tf_op jit(solution)/shard_map/ppermute | solution.py:384
  52.3 1.3 %collective-permute-done.13.refs_7_ = bf16[512,128]{1,0:T(8,128)(2,1)S(1)} collective-permute-done((bf16[512,128]{1,0:T(8,128)(2,1)S(1)}, bf16[512,128]{1,0:T(8,128)(2,1)S(1)}, u32[]{:S(2)}, u32[]{:S(2)}) %collective-permute-start.13) | collective-permute-done | bytes 131104 | tf_op jit(solution)/shard_map/ppermute | solution.py:384
  53.6 2.3 %project.1 = (f32[8,128]{1,0:T(8,128)S(1)}, bf16[512,1024]{1,0:T(8,128)(2,1)}, bf16[32,96,128]{2,1,0:T(8,128)(2,1)}) custom-call(bf16[512,128]{1,0:T(8,128)(2,1)S(1)} %get-tuple-element.30.refs_0_, bf16[512,128]{1,0:T(8,128)(2,1)S(1)} %collective-permute-done.7.refs_1_, bf16[512,128]{1,0:T(8,128)(2,1)S(1)} %collective-permute-done.8.refs_2_, ...), custom_call_target="tpu_custom_call" | custom-call | tf_op jit(solution)/shard_map/project/pallas_call | solution.py:495
  55.9 4.8 %all-to-all-start.2 = ((bf16[32,96,128]{2,1,0:T(8,128)(2,1)}), bf16[32,96,128]{2,1,0:T(8,128)(2,1)S(1)}, u32[]{:S(2)}, u32[]{:S(2)}) async-start(bf16[32,96,128]{2,1,0:T(8,128)(2,1)} %get-tuple-element.48), calls=%async_computation.2 | async-start | bytes 1572864 | tf_op jit(solution)/shard_map/all_to_all | solution.py:530
  60.7 1.8 %collective-permute-start.30 = (f32[8,512]{1,0:T(8,128)S(1)}, f32[8,512]{1,0:T(8,128)S(1)}, u32[]{:S(2)}, u32[]{:S(2)}) collective-permute-start(f32[8,512]{1,0:T(8,128)S(1)} %get-tuple-element.32.refs_9_.refs_5_), channel_id=1, source_target_pairs={{0,8},{1,9},{2,10},{3,11},{4,12},{5,13},{6,14},{7,15},{8,0},{9,1},... | collective-permute-start | bytes 49160 | tf_op jit(solution)/shard_map/ppermute | solution.py:485
  62.5 2.4 %collective-permute-start.31 = (f32[8,512]{1,0:T(8,128)S(1)}, f32[8,512]{1,0:T(8,128)S(1)}, u32[]{:S(2)}, u32[]{:S(2)}) collective-permute-start(f32[8,512]{1,0:T(8,128)S(1)} %get-tuple-element.32.refs_9_.refs_5_), channel_id=1, source_target_pairs={{0,16},{1,17},{2,18},{3,19},{4,20},{5,21},{6,22},{7,23},{8,24},{9,... | collective-permute-start | bytes 49160 | tf_op jit(solution)/shard_map/ppermute | solution.py:485
  65.8 8.9 %collective-permute-done.30.refs_6_ = f32[8,512]{1,0:T(8,128)S(1)} collective-permute-done((f32[8,512]{1,0:T(8,128)S(1)}, f32[8,512]{1,0:T(8,128)S(1)}, u32[]{:S(2)}, u32[]{:S(2)}) %collective-permute-start.30) | collective-permute-done | bytes 16416 | tf_op jit(solution)/shard_map/ppermute | solution.py:485
  74.7 7.8 %collective-permute-done.31.refs_7_ = f32[8,512]{1,0:T(8,128)S(1)} collective-permute-done((f32[8,512]{1,0:T(8,128)S(1)}, f32[8,512]{1,0:T(8,128)S(1)}, u32[]{:S(2)}, u32[]{:S(2)}) %collective-permute-start.31) | collective-permute-done | bytes 16416 | tf_op jit(solution)/shard_map/ppermute | solution.py:485
  82.6 1.7 %stage.1 = (bf16[1024,1024]{1,0:T(8,128)(2,1)S(1)}, f32[8,1024]{1,0:T(8,128)S(1)}, f32[96,8]{1,0:T(8,128)S(1)}, s32[96,1]{1,0:T(8,128)S(1)}, s32[1,192]{1,0:T(1,128)S(1)}) custom-call(s32[1]{0:T(128)S(6)} %copy.16.length_ref, f32[8,128]{1,0:T(8,128)S(1)} %get-tuple-element.49.after_ref, bf16[1024,1024]{1,0:T(8,128)(2,1)} %bitcast.20, ...), custom_call_target="tpu_custom_call" | custom-call | tf_op jit(solution)/shard_map/stage/pallas_call | solution.py:550
  84.3 4.2 %attend.1 = bf16[32,48,128]{2,1,0:T(8,128)(2,1)} custom-call(bf16[4,8,96,128]{3,2,1,0:T(8,128)(2,1)S(1)} %bitcast.14, bf16[1024,1024]{1,0:T(8,128)(2,1)S(1)} %get-tuple-element.50.keys_ref, bf16[1024,1024]{1,0:T(8,128)(2,1)} %bitcast.21, f32[8,1024]{1,0:T(8,128)S(1)} %get-tuple-element.51.cache_bias_ref, f32[96,8]{1,0:T(8,128)S(1)} %get-tuple-element.52.new_bias_ref, ...), custom_call_target="tpu_custom_call" | custom-call | tf_op jit(solution)/shard_map/attend/pallas_call | solution.py:579
  88.5 3.5 %all-to-all-start.3 = ((bf16[32,48,128]{2,1,0:T(8,128)(2,1)}), bf16[32,48,128]{2,1,0:T(8,128)(2,1)S(1)}, u32[]{:S(2)}, u32[]{:S(2)}) async-start(bf16[32,48,128]{2,1,0:T(8,128)(2,1)} %attend.1), calls=%async_computation.3 | async-start | bytes 786432 | tf_op jit(solution)/shard_map/all_to_all | solution.py:596
  92.6 0.7 collective-permute-done.14.refs_2_
  93.6 1.7 %collective-permute-start.16 = (bf16[128,128]{1,0:T(8,128)(2,1)S(1)}, bf16[128,128]{1,0:T(8,128)(2,1)S(1)}, u32[]{:S(2)}, u32[]{:S(2)}) collective-permute-start(bf16[128,128]{1,0:T(8,128)(2,1)S(1)} %get-tuple-element.39), channel_id=1, source_target_pairs={{0,4},{1,5},{2,6},{3,7},{4,0},{5,1},{6,2},{7,3},{8,12},{9,13},{10,... | collective-permute-start | bytes 98312 | tf_op jit(solution)/shard_map/ppermute | solution.py:448
  95.3 1.5 %collective-permute-start.17 = (bf16[128,128]{1,0:T(8,128)(2,1)S(1)}, bf16[128,128]{1,0:T(8,128)(2,1)S(1)}, u32[]{:S(2)}, u32[]{:S(2)}) collective-permute-start(bf16[128,128]{1,0:T(8,128)(2,1)S(1)} %get-tuple-element.38.refs_0_), channel_id=1, source_target_pairs={{0,8},{1,9},{2,10},{3,11},{4,12},{5,13},{6,14},{7,15},{8,0},{9,1},... | collective-permute-start | bytes 98312 | tf_op jit(solution)/shard_map/ppermute | solution.py:448
  97.1 2.6 %collective-permute-start.19 = (bf16[128,128]{1,0:T(8,128)(2,1)S(1)}, bf16[128,128]{1,0:T(8,128)(2,1)S(1)}, u32[]{:S(2)}, u32[]{:S(2)}) collective-permute-start(bf16[128,128]{1,0:T(8,128)(2,1)S(1)} %get-tuple-element.38.refs_0_), channel_id=1, source_target_pairs={{0,16},{1,17},{2,18},{3,19},{4,20},{5,21},{6,22},{7,23},{8,24},{9,... | collective-permute-start | bytes 98312 | tf_op jit(solution)/shard_map/ppermute | solution.py:448
  99.7 1.5 %collective-permute-start.20 = (bf16[128,128]{1,0:T(8,128)(2,1)S(1)}, bf16[128,128]{1,0:T(8,128)(2,1)S(1)}, u32[]{:S(2)}, u32[]{:S(2)}) collective-permute-start(bf16[128,128]{1,0:T(8,128)(2,1)S(1)} %get-tuple-element.39), channel_id=1, source_target_pairs={{0,20},{1,21},{2,22},{3,23},{4,16},{5,17},{6,18},{7,19},{8,28},{9,... | collective-permute-start | bytes 98312 | tf_op jit(solution)/shard_map/ppermute | solution.py:448
  101.2 3.3 %collective-permute-start.21 = (bf16[128,128]{1,0:T(8,128)(2,1)S(1)}, bf16[128,128]{1,0:T(8,128)(2,1)S(1)}, u32[]{:S(2)}, u32[]{:S(2)}) collective-permute-start(bf16[128,128]{1,0:T(8,128)(2,1)S(1)} %get-tuple-element.38.refs_0_), channel_id=1, source_target_pairs={{0,24},{1,25},{2,26},{3,27},{4,28},{5,29},{6,30},{7,31},{8,16},{9,... | collective-permute-start | bytes 98312 | tf_op jit(solution)/shard_map/ppermute | solution.py:448
  104.8 2.8 %collective-permute-done.19.refs_4_ = bf16[128,128]{1,0:T(8,128)(2,1)S(1)} collective-permute-done((bf16[128,128]{1,0:T(8,128)(2,1)S(1)}, bf16[128,128]{1,0:T(8,128)(2,1)S(1)}, u32[]{:S(2)}, u32[]{:S(2)}) %collective-permute-start.19) | collective-permute-done | bytes 32800 | tf_op jit(solution)/shard_map/ppermute | solution.py:448
  107.6 1.9 %collective-permute-done.20.refs_5_ = bf16[128,128]{1,0:T(8,128)(2,1)S(1)} collective-permute-done((bf16[128,128]{1,0:T(8,128)(2,1)S(1)}, bf16[128,128]{1,0:T(8,128)(2,1)S(1)}, u32[]{:S(2)}, u32[]{:S(2)}) %collective-permute-start.20) | collective-permute-done | bytes 32800 | tf_op jit(solution)/shard_map/ppermute | solution.py:448
  109.6 1.6 %collective-permute-done.22.refs_7_ = bf16[128,128]{1,0:T(8,128)(2,1)S(1)} collective-permute-done((bf16[128,128]{1,0:T(8,128)(2,1)S(1)}, bf16[128,128]{1,0:T(8,128)(2,1)S(1)}, u32[]{:S(2)}, u32[]{:S(2)}) %collective-permute-start.22) | collective-permute-done | bytes 32800 | tf_op jit(solution)/shard_map/ppermute | solution.py:448
  111.1 1.7 %gate.1 = (bf16[64,128]{1,0:T(8,128)(2,1)S(1)}, bf16[64,128]{1,0:T(8,128)(2,1)S(1)}, bf16[64,128]{1,0:T(8,128)(2,1)S(1)}, bf16[64,128]{1,0:T(8,128)(2,1)S(1)}, b...) custom-call(bf16[512,1024]{1,0:T(8,128)(2,1)} %get-tuple-element.33., ...), custom_call_target="tpu_custom_call" | custom-call | tf_op jit(solution)/shard_map/gate/pallas_call | solution.py:512
  112.8 1.6 %collective-permute-start.23 = (bf16[64,128]{1,0:T(8,128)(2,1)S(1)}, bf16[64,128]{1,0:T(8,128)(2,1)S(1)}, u32[]{:S(2)}, u32[]{:S(2)}) collective-permute-start(bf16[64,128]{1,0:T(8,128)(2,1)S(1)} %get-tuple-element.41), channel_id=1, source_target_pairs={{0,1},{1,0},{2,3},{3,2},{4,5},{5,4},{6,7},{7,6},{8,9},{9,8},{10,11... | collective-permute-start | bytes 49160 | tf_op jit(solution)/shard_map/ppermute | solution.py:384
  114.5 0.7 collective-permute-start.25
  115.2 0.5 collective-permute-start.26
  115.8 2.4 %collective-permute-start.27 = (bf16[64,128]{1,0:T(8,128)(2,1)S(1)}, bf16[64,128]{1,0:T(8,128)(2,1)S(1)}, u32[]{:S(2)}, u32[]{:S(2)}) collective-permute-start(bf16[64,128]{1,0:T(8,128)(2,1)S(1)} %get-tuple-element.45), channel_id=1, source_target_pairs={{0,5},{1,4},{2,7},{3,6},{4,1},{5,0},{6,3},{7,2},{8,13},{9,12},{10,... | collective-permute-start | bytes 49160 | tf_op jit(solution)/shard_map/ppermute | solution.py:384
  118.2 1.7 %collective-permute-start.29 = (bf16[64,128]{1,0:T(8,128)(2,1)S(1)}, bf16[64,128]{1,0:T(8,128)(2,1)S(1)}, u32[]{:S(2)}, u32[]{:S(2)}) collective-permute-start(bf16[64,128]{1,0:T(8,128)(2,1)S(1)} %get-tuple-element.47), channel_id=1, source_target_pairs={{0,7},{1,6},{2,5},{3,4},{4,3},{5,2},{6,1},{7,0},{8,15},{9,14},{10,... | collective-permute-start | bytes 49160 | tf_op jit(solution)/shard_map/ppermute | solution.py:384
  119.9 0.5 collective-permute-done.27.refs_5_
  120.4 0.9 collective-permute-done.28.refs_6_
  121.4 1.0 collective-permute-done.29.refs_7_
  122.3 1.5 %finish.1 = bf16[64,1024]{1,0:T(8,128)(2,1)} custom-call(s32[2,64]{1,0:T(2,128)S(1)} %multiply_add_fusion.place_ref, bf16[64,128]{1,0:T(8,128)(2,1)S(1)} %get-tuple-element.40.refs_0_, bf16[64,128]{1,0:T(8,128)(2,1)S(1)} %collective-permute-done.23.refs_1_, bf16[64,128]{1,0:T(8,128)(2,1)S(1)} %collective-permute-done.24.refs_2_, ...), custom_call_target="tpu_custom_call" | custom-call | tf_op jit(solution)/shard_map/finish/pallas_call | solution.py:599
  (59 shorter events, 3.0 us)
Async XLA Ops:
  0.0 40.8 %copy-start.4 = (f32[1024]{0:T(1024)S(1)}, f32[1024]{0:T(1024)}, u32[]{:S(2)}) copy-start(f32[1024]{0:T(1024)} %param.19) | copy-start | bytes 12292
  1.6 51.9 %copy-start.3 = (s32[1,512]{1,0:T(1,128)S(1)}, s32[1,512]{1,0:T(1,128)}, u32[]{:S(2)}) copy-start(s32[1,512]{1,0:T(1,128)} %constant.12.clone.refs_10_.refs_4_) | copy-start | bytes 6148
  1.6 17.5 %all-to-all-start = ((bf16[16,64,128]{2,1,0:T(8,128)(2,1)}), bf16[16,64,128]{2,1,0:T(8,128)(2,1)S(1)}, u32[]{:S(2)}, u32[]{:S(2)}) async-start(bf16[16,64,128]{2,1,0:T(8,128)(2,1)} %cross_columns.1), calls=%async_computation | async-start | bytes 524288 | tf_op jit(solution)/shard_map/all_to_all | solution.py:435
  9.2 1.0 copy-start.1
  19.2 34.4 %all-to-all-start.1 = ((bf16[16,64,384]{2,1,0:T(8,128)(2,1)}), bf16[16,64,384]{2,1,0:T(8,128)(2,1)S(1)}, u32[]{:S(2)}, u32[]{:S(2)}) async-start(bf16[16,64,384]{2,1,0:T(8,128)(2,1)} %get-tuple-element.31), calls=%async_computation.1 | async-start | bytes 1572864 | tf_op jit(solution)/shard_map/all_to_all | solution.py:436
  24.7 6.3 %collective-permute-start = (bf16[64,1152]{1,0:T(8,128)(2,1)}, bf16[64,1152]{1,0:T(8,128)(2,1)S(1)}, u32[]{:S(2)}, u32[]{:S(2)}) collective-permute-start(bf16[64,1152]{1,0:T(8,128)(2,1)} %prepare.1.refs_0_), channel_id=1, source_target_pairs={{0,1},{1,0},{2,3},{3,2},{4,5},{5,4},{6,7},{7,6},{8,9},{9,8},{10,11... | collective-permute-start | bytes 442376 | tf_op jit(solution)/shard_map/ppermute | solution.py:384
  26.2 9.6 %collective-permute-start.3 = (bf16[64,1152]{1,0:T(8,128)(2,1)}, bf16[64,1152]{1,0:T(8,128)(2,1)S(1)}, u32[]{:S(2)}, u32[]{:S(2)}) collective-permute-start(bf16[64,1152]{1,0:T(8,128)(2,1)} %prepare.1.refs_0_), channel_id=1, source_target_pairs={{0,4},{1,5},{2,6},{3,7},{4,0},{5,1},{6,2},{7,3},{8,12},{9,13},{10,... | collective-permute-start | bytes 442376 | tf_op jit(solution)/shard_map/ppermute | solution.py:384
  28.0 11.4 %collective-permute-start.4 = (bf16[64,1152]{1,0:T(8,128)(2,1)}, bf16[64,1152]{1,0:T(8,128)(2,1)S(1)}, u32[]{:S(2)}, u32[]{:S(2)}) collective-permute-start(bf16[64,1152]{1,0:T(8,128)(2,1)} %prepare.1.refs_0_), channel_id=1, source_target_pairs={{0,5},{1,4},{2,7},{3,6},{4,1},{5,0},{6,3},{7,2},{8,13},{9,12},{10,... | collective-permute-start | bytes 442376 | tf_op jit(solution)/shard_map/ppermute | solution.py:384
  28.1 11.3 %collective-permute-start.1 = (bf16[64,1152]{1,0:T(8,128)(2,1)}, bf16[64,1152]{1,0:T(8,128)(2,1)S(1)}, u32[]{:S(2)}, u32[]{:S(2)}) collective-permute-start(bf16[64,1152]{1,0:T(8,128)(2,1)} %prepare.1.refs_0_), channel_id=1, source_target_pairs={{0,2},{1,3},{2,0},{3,1},{4,6},{5,7},{6,4},{7,5},{8,10},{9,11},{10,... | collective-permute-start | bytes 442376 | tf_op jit(solution)/shard_map/ppermute | solution.py:384
  30.9 8.5 %collective-permute-start.2 = (bf16[64,1152]{1,0:T(8,128)(2,1)S(1)}, bf16[64,1152]{1,0:T(8,128)(2,1)S(1)}, u32[]{:S(2)}, u32[]{:S(2)}) collective-permute-start(bf16[64,1152]{1,0:T(8,128)(2,1)S(1)} %collective-permute-done.refs_1_), channel_id=1, source_target_pairs={{0,2},{1,3},{2,0},{3,1},{4,6},{5,7},{6,4},{7,5},{8,10},{9,11},{10,... | collective-permute-start | bytes 442376 | tf_op jit(solution)/shard_map/ppermute | solution.py:384
  35.8 3.6 %collective-permute-start.5 = (bf16[64,1152]{1,0:T(8,128)(2,1)S(1)}, bf16[64,1152]{1,0:T(8,128)(2,1)S(1)}, u32[]{:S(2)}, u32[]{:S(2)}) collective-permute-start(bf16[64,1152]{1,0:T(8,128)(2,1)S(1)} %collective-permute-done.3.refs_4_), channel_id=1, source_target_pairs={{0,2},{1,3},{2,0},{3,1},{4,6},{5,7},{6,4},{7,5},{8,10},{9,11},{10,... | collective-permute-start | bytes 442376 | tf_op jit(solution)/shard_map/ppermute | solution.py:384
  39.4 1.4 %collective-permute-start.6 = (bf16[64,1152]{1,0:T(8,128)(2,1)S(1)}, bf16[64,1152]{1,0:T(8,128)(2,1)S(1)}, u32[]{:S(2)}, u32[]{:S(2)}) collective-permute-start(bf16[64,1152]{1,0:T(8,128)(2,1)S(1)} %collective-permute-done.4.refs_5_), channel_id=1, source_target_pairs={{0,2},{1,3},{2,0},{3,1},{4,6},{5,7},{6,4},{7,5},{8,10},{9,11},{10,... | collective-permute-start | bytes 442376 | tf_op jit(solution)/shard_map/ppermute | solution.py:384
  40.8 0.9 copy-start
  41.7 40.8 %copy-start.2 = (s32[96,1]{1,0:T(8,128)S(1)}, s32[96,1]{1,0:T(8,128)}, u32[]{:S(2)}) copy-start(s32[96,1]{1,0:T(8,128)} %constant.19.refs_2_) | copy-start | bytes 1156
  41.7 40.8 %copy-start.5 = (s32[1,1024]{1,0:T(1,128)S(1)}, s32[1,1024]{1,0:T(1,128)}, u32[]{:S(2)}) copy-start(s32[1,1024]{1,0:T(1,128)} %refs_0_.1) | copy-start | bytes 12292
  41.7 40.9 %copy-start.6 = (f32[32,8]{0,1:T(8,128)S(1)}, f32[32,8]{0,1:T(8,128)}, u32[]{:S(2)}) copy-start(f32[32,8]{0,1:T(8,128)} %param.25) | copy-start | bytes 3076
  41.7 40.9 %copy-start.8 = (s32[1,192]{1,0:T(1,128)S(1)}, s32[1,192]{1,0:T(1,128)}, u32[]{:S(2)}) copy-start(s32[1,192]{1,0:T(1,128)} %constant.20.refs_3_) | copy-start | bytes 2308
  42.2 5.6 %collective-permute-start.7 = (bf16[512,128]{1,0:T(8,128)(2,1)S(1)}, bf16[512,128]{1,0:T(8,128)(2,1)S(1)}, u32[]{:S(2)}, u32[]{:S(2)}) collective-permute-start(bf16[512,128]{1,0:T(8,128)(2,1)S(1)} %get-tuple-element.30.refs_0_), channel_id=1, source_target_pairs={{0,1},{1,0},{2,3},{3,2},{4,5},{5,4},{6,7},{7,6},{8,9},{9,8},{10,11... | collective-permute-start | bytes 393224 | tf_op jit(solution)/shard_map/ppermute | solution.py:384
  42.7 7.2 %collective-permute-start.10 = (bf16[512,128]{1,0:T(8,128)(2,1)S(1)}, bf16[512,128]{1,0:T(8,128)(2,1)S(1)}, u32[]{:S(2)}, u32[]{:S(2)}) collective-permute-start(bf16[512,128]{1,0:T(8,128)(2,1)S(1)} %get-tuple-element.30.refs_0_), channel_id=1, source_target_pairs={{0,4},{1,5},{2,6},{3,7},{4,0},{5,1},{6,2},{7,3},{8,12},{9,13},{10,... | collective-permute-start | bytes 393224 | tf_op jit(solution)/shard_map/ppermute | solution.py:384
  45.6 6.7 %collective-permute-start.11 = (bf16[512,128]{1,0:T(8,128)(2,1)S(1)}, bf16[512,128]{1,0:T(8,128)(2,1)S(1)}, u32[]{:S(2)}, u32[]{:S(2)}) collective-permute-start(bf16[512,128]{1,0:T(8,128)(2,1)S(1)} %get-tuple-element.30.refs_0_), channel_id=1, source_target_pairs={{0,5},{1,4},{2,7},{3,6},{4,1},{5,0},{6,3},{7,2},{8,13},{9,12},{10,... | collective-permute-start | bytes 393224 | tf_op jit(solution)/shard_map/ppermute | solution.py:384
  45.9 6.3 %collective-permute-start.8 = (bf16[512,128]{1,0:T(8,128)(2,1)S(1)}, bf16[512,128]{1,0:T(8,128)(2,1)S(1)}, u32[]{:S(2)}, u32[]{:S(2)}) collective-permute-start(bf16[512,128]{1,0:T(8,128)(2,1)S(1)} %get-tuple-element.30.refs_0_), channel_id=1, source_target_pairs={{0,2},{1,3},{2,0},{3,1},{4,6},{5,7},{6,4},{7,5},{8,10},{9,11},{10,... | collective-permute-start | bytes 393224 | tf_op jit(solution)/shard_map/ppermute | solution.py:384
  47.8 4.5 %collective-permute-start.9 = (bf16[512,128]{1,0:T(8,128)(2,1)S(1)}, bf16[512,128]{1,0:T(8,128)(2,1)S(1)}, u32[]{:S(2)}, u32[]{:S(2)}) collective-permute-start(bf16[512,128]{1,0:T(8,128)(2,1)S(1)} %collective-permute-done.7.refs_1_), channel_id=1, source_target_pairs={{0,2},{1,3},{2,0},{3,1},{4,6},{5,7},{6,4},{7,5},{8,10},{9,11},{10,... | collective-permute-start | bytes 393224 | tf_op jit(solution)/shard_map/ppermute | solution.py:384
  49.9 2.4 %collective-permute-start.12 = (bf16[512,128]{1,0:T(8,128)(2,1)S(1)}, bf16[512,128]{1,0:T(8,128)(2,1)S(1)}, u32[]{:S(2)}, u32[]{:S(2)}) collective-permute-start(bf16[512,128]{1,0:T(8,128)(2,1)S(1)} %collective-permute-done.10.refs_4_), channel_id=1, source_target_pairs={{0,2},{1,3},{2,0},{3,1},{4,6},{5,7},{6,4},{7,5},{8,10},{9,11},{10,... | collective-permute-start | bytes 393224 | tf_op jit(solution)/shard_map/ppermute | solution.py:384
  52.2 1.3 %collective-permute-start.13 = (bf16[512,128]{1,0:T(8,128)(2,1)S(1)}, bf16[512,128]{1,0:T(8,128)(2,1)S(1)}, u32[]{:S(2)}, u32[]{:S(2)}) collective-permute-start(bf16[512,128]{1,0:T(8,128)(2,1)S(1)} %collective-permute-done.11.refs_5_), channel_id=1, source_target_pairs={{0,2},{1,3},{2,0},{3,1},{4,6},{5,7},{6,4},{7,5},{8,10},{9,11},{10,... | collective-permute-start | bytes 393224 | tf_op jit(solution)/shard_map/ppermute | solution.py:384
  55.9 28.4 %all-to-all-start.2 = ((bf16[32,96,128]{2,1,0:T(8,128)(2,1)}), bf16[32,96,128]{2,1,0:T(8,128)(2,1)S(1)}, u32[]{:S(2)}, u32[]{:S(2)}) async-start(bf16[32,96,128]{2,1,0:T(8,128)(2,1)} %get-tuple-element.48), calls=%async_computation.2 | async-start | bytes 1572864 | tf_op jit(solution)/shard_map/all_to_all | solution.py:530
  60.7 14.0 %collective-permute-start.30 = (f32[8,512]{1,0:T(8,128)S(1)}, f32[8,512]{1,0:T(8,128)S(1)}, u32[]{:S(2)}, u32[]{:S(2)}) collective-permute-start(f32[8,512]{1,0:T(8,128)S(1)} %get-tuple-element.32.refs_9_.refs_5_), channel_id=1, source_target_pairs={{0,8},{1,9},{2,10},{3,11},{4,12},{5,13},{6,14},{7,15},{8,0},{9,1},... | collective-permute-start | bytes 49160 | tf_op jit(solution)/shard_map/ppermute | solution.py:485
  62.5 20.0 %collective-permute-start.31 = (f32[8,512]{1,0:T(8,128)S(1)}, f32[8,512]{1,0:T(8,128)S(1)}, u32[]{:S(2)}, u32[]{:S(2)}) collective-permute-start(f32[8,512]{1,0:T(8,128)S(1)} %get-tuple-element.32.refs_9_.refs_5_), channel_id=1, source_target_pairs={{0,16},{1,17},{2,18},{3,19},{4,20},{5,21},{6,22},{7,23},{8,24},{9,... | collective-permute-start | bytes 49160 | tf_op jit(solution)/shard_map/ppermute | solution.py:485
  65.0 17.6 %collective-permute-start.32 = (f32[8,512]{1,0:T(8,128)S(1)}, f32[8,512]{1,0:T(8,128)S(1)}, u32[]{:S(2)}, u32[]{:S(2)}) collective-permute-start(f32[8,512]{1,0:T(8,128)S(1)} %get-tuple-element.32.refs_9_.refs_5_), channel_id=1, source_target_pairs={{0,24},{1,25},{2,26},{3,27},{4,28},{5,29},{6,30},{7,31},{8,16},{9,... | collective-permute-start | bytes 49160 | tf_op jit(solution)/shard_map/ppermute | solution.py:485
  84.3 20.5 %copy-start.9 = (s32[64,1]{0,1:T(1,128)S(1)}, s32[64,1]{0,1:T(1,128)}, u32[]{:S(2)}) copy-start(s32[64,1]{0,1:T(1,128)} %param.16) | copy-start | bytes 772
  88.5 33.8 %copy-start.7 = (f32[1024]{0:T(1024)S(1)}, f32[1024]{0:T(1024)}, u32[]{:S(2)}) copy-start(f32[1024]{0:T(1024)} %param.26) | copy-start | bytes 12292
  88.5 33.8 %all-to-all-start.3 = ((bf16[32,48,128]{2,1,0:T(8,128)(2,1)}), bf16[32,48,128]{2,1,0:T(8,128)(2,1)S(1)}, u32[]{:S(2)}, u32[]{:S(2)}) async-start(bf16[32,48,128]{2,1,0:T(8,128)(2,1)} %attend.1), calls=%async_computation.3 | async-start | bytes 786432 | tf_op jit(solution)/shard_map/all_to_all | solution.py:596
  92.1 1.2 %collective-permute-start.14 = (bf16[64,128]{1,0:T(8,128)(2,1)S(1)}, bf16[64,128]{1,0:T(8,128)(2,1)S(1)}, u32[]{:S(2)}, u32[]{:S(2)}) collective-permute-start(bf16[64,128]{1,0:T(8,128)(2,1)S(1)} %get-tuple-element.36), channel_id=1, source_target_pairs={{0,2},{1,3},{2,0},{3,1},{4,6},{5,7},{6,4},{7,5},{8,10},{9,11},{10,... | collective-permute-start | bytes 49160 | tf_op jit(solution)/shard_map/ppermute | solution.py:448
  92.4 1.2 collective-permute-start.15
  93.6 7.6 %collective-permute-start.16 = (bf16[128,128]{1,0:T(8,128)(2,1)S(1)}, bf16[128,128]{1,0:T(8,128)(2,1)S(1)}, u32[]{:S(2)}, u32[]{:S(2)}) collective-permute-start(bf16[128,128]{1,0:T(8,128)(2,1)S(1)} %get-tuple-element.39), channel_id=1, source_target_pairs={{0,4},{1,5},{2,6},{3,7},{4,0},{5,1},{6,2},{7,3},{8,12},{9,13},{10,... | collective-permute-start | bytes 98312 | tf_op jit(solution)/shard_map/ppermute | solution.py:448
  95.3 9.2 %collective-permute-start.17 = (bf16[128,128]{1,0:T(8,128)(2,1)S(1)}, bf16[128,128]{1,0:T(8,128)(2,1)S(1)}, u32[]{:S(2)}, u32[]{:S(2)}) collective-permute-start(bf16[128,128]{1,0:T(8,128)(2,1)S(1)} %get-tuple-element.38.refs_0_), channel_id=1, source_target_pairs={{0,8},{1,9},{2,10},{3,11},{4,12},{5,13},{6,14},{7,15},{8,0},{9,1},... | collective-permute-start | bytes 98312 | tf_op jit(solution)/shard_map/ppermute | solution.py:448
  96.8 8.0 %collective-permute-start.18 = (bf16[128,128]{1,0:T(8,128)(2,1)S(1)}, bf16[128,128]{1,0:T(8,128)(2,1)S(1)}, u32[]{:S(2)}, u32[]{:S(2)}) collective-permute-start(bf16[128,128]{1,0:T(8,128)(2,1)S(1)} %get-tuple-element.39), channel_id=1, source_target_pairs={{0,12},{1,13},{2,14},{3,15},{4,8},{5,9},{6,10},{7,11},{8,4},{9,5},... | collective-permute-start | bytes 98312 | tf_op jit(solution)/shard_map/ppermute | solution.py:448
  97.1 10.5 %collective-permute-start.19 = (bf16[128,128]{1,0:T(8,128)(2,1)S(1)}, bf16[128,128]{1,0:T(8,128)(2,1)S(1)}, u32[]{:S(2)}, u32[]{:S(2)}) collective-permute-start(bf16[128,128]{1,0:T(8,128)(2,1)S(1)} %get-tuple-element.38.refs_0_), channel_id=1, source_target_pairs={{0,16},{1,17},{2,18},{3,19},{4,20},{5,21},{6,22},{7,23},{8,24},{9,... | collective-permute-start | bytes 98312 | tf_op jit(solution)/shard_map/ppermute | solution.py:448
  99.7 9.8 %collective-permute-start.20 = (bf16[128,128]{1,0:T(8,128)(2,1)S(1)}, bf16[128,128]{1,0:T(8,128)(2,1)S(1)}, u32[]{:S(2)}, u32[]{:S(2)}) collective-permute-start(bf16[128,128]{1,0:T(8,128)(2,1)S(1)} %get-tuple-element.39), channel_id=1, source_target_pairs={{0,20},{1,21},{2,22},{3,23},{4,16},{5,17},{6,18},{7,19},{8,28},{9,... | collective-permute-start | bytes 98312 | tf_op jit(solution)/shard_map/ppermute | solution.py:448
  101.2 8.4 %collective-permute-start.21 = (bf16[128,128]{1,0:T(8,128)(2,1)S(1)}, bf16[128,128]{1,0:T(8,128)(2,1)S(1)}, u32[]{:S(2)}, u32[]{:S(2)}) collective-permute-start(bf16[128,128]{1,0:T(8,128)(2,1)S(1)} %get-tuple-element.38.refs_0_), channel_id=1, source_target_pairs={{0,24},{1,25},{2,26},{3,27},{4,28},{5,29},{6,30},{7,31},{8,16},{9,... | collective-permute-start | bytes 98312 | tf_op jit(solution)/shard_map/ppermute | solution.py:448
  104.5 6.6 %collective-permute-start.22 = (bf16[128,128]{1,0:T(8,128)(2,1)S(1)}, bf16[128,128]{1,0:T(8,128)(2,1)S(1)}, u32[]{:S(2)}, u32[]{:S(2)}) collective-permute-start(bf16[128,128]{1,0:T(8,128)(2,1)S(1)} %get-tuple-element.39), channel_id=1, source_target_pairs={{0,28},{1,29},{2,30},{3,31},{4,24},{5,25},{6,26},{7,27},{8,20},{9,... | collective-permute-start | bytes 98312 | tf_op jit(solution)/shard_map/ppermute | solution.py:448
  112.8 5.4 %collective-permute-start.23 = (bf16[64,128]{1,0:T(8,128)(2,1)S(1)}, bf16[64,128]{1,0:T(8,128)(2,1)S(1)}, u32[]{:S(2)}, u32[]{:S(2)}) collective-permute-start(bf16[64,128]{1,0:T(8,128)(2,1)S(1)} %get-tuple-element.41), channel_id=1, source_target_pairs={{0,1},{1,0},{2,3},{3,2},{4,5},{5,4},{6,7},{7,6},{8,9},{9,8},{10,11... | collective-permute-start | bytes 49160 | tf_op jit(solution)/shard_map/ppermute | solution.py:384
  114.4 3.9 %collective-permute-start.24 = (bf16[64,128]{1,0:T(8,128)(2,1)S(1)}, bf16[64,128]{1,0:T(8,128)(2,1)S(1)}, u32[]{:S(2)}, u32[]{:S(2)}) collective-permute-start(bf16[64,128]{1,0:T(8,128)(2,1)S(1)} %get-tuple-element.42), channel_id=1, source_target_pairs={{0,2},{1,3},{2,0},{3,1},{4,6},{5,7},{6,4},{7,5},{8,10},{9,11},{10,... | collective-permute-start | bytes 49160 | tf_op jit(solution)/shard_map/ppermute | solution.py:384
  114.5 5.4 %collective-permute-start.25 = (bf16[64,128]{1,0:T(8,128)(2,1)S(1)}, bf16[64,128]{1,0:T(8,128)(2,1)S(1)}, u32[]{:S(2)}, u32[]{:S(2)}) collective-permute-start(bf16[64,128]{1,0:T(8,128)(2,1)S(1)} %get-tuple-element.43), channel_id=1, source_target_pairs={{0,3},{1,2},{2,1},{3,0},{4,7},{5,6},{6,5},{7,4},{8,11},{9,10},{10,... | collective-permute-start | bytes 49160 | tf_op jit(solution)/shard_map/ppermute | solution.py:384
  115.2 4.7 %collective-permute-start.26 = (bf16[64,128]{1,0:T(8,128)(2,1)S(1)}, bf16[64,128]{1,0:T(8,128)(2,1)S(1)}, u32[]{:S(2)}, u32[]{:S(2)}) collective-permute-start(bf16[64,128]{1,0:T(8,128)(2,1)S(1)} %get-tuple-element.44), channel_id=1, source_target_pairs={{0,4},{1,5},{2,6},{3,7},{4,0},{5,1},{6,2},{7,3},{8,12},{9,13},{10,... | collective-permute-start | bytes 49160 | tf_op jit(solution)/shard_map/ppermute | solution.py:384
  115.8 4.6 %collective-permute-start.27 = (bf16[64,128]{1,0:T(8,128)(2,1)S(1)}, bf16[64,128]{1,0:T(8,128)(2,1)S(1)}, u32[]{:S(2)}, u32[]{:S(2)}) collective-permute-start(bf16[64,128]{1,0:T(8,128)(2,1)S(1)} %get-tuple-element.45), channel_id=1, source_target_pairs={{0,5},{1,4},{2,7},{3,6},{4,1},{5,0},{6,3},{7,2},{8,13},{9,12},{10,... | collective-permute-start | bytes 49160 | tf_op jit(solution)/shard_map/ppermute | solution.py:384
  118.2 3.2 %collective-permute-start.28 = (bf16[64,128]{1,0:T(8,128)(2,1)S(1)}, bf16[64,128]{1,0:T(8,128)(2,1)S(1)}, u32[]{:S(2)}, u32[]{:S(2)}) collective-permute-start(bf16[64,128]{1,0:T(8,128)(2,1)S(1)} %get-tuple-element.46), channel_id=1, source_target_pairs={{0,6},{1,7},{2,4},{3,5},{4,2},{5,3},{6,0},{7,1},{8,14},{9,15},{10,... | collective-permute-start | bytes 49160 | tf_op jit(solution)/shard_map/ppermute | solution.py:384
  118.2 4.1 %collective-permute-start.29 = (bf16[64,128]{1,0:T(8,128)(2,1)S(1)}, bf16[64,128]{1,0:T(8,128)(2,1)S(1)}, u32[]{:S(2)}, u32[]{:S(2)}) collective-permute-start(bf16[64,128]{1,0:T(8,128)(2,1)S(1)} %get-tuple-element.47), channel_id=1, source_target_pairs={{0,7},{1,6},{2,5},{3,4},{4,3},{5,2},{6,1},{7,0},{8,15},{9,14},{10,... | collective-permute-start | bytes 49160 | tf_op jit(solution)/shard_map/ppermute | solution.py:384
